TPU v7x, 512 devices: a whole 4x8x8 slice. The times are simulated.
512 devices in a mesh: ctrl: 16 (over y, x_lo), shelf: 32 (over z, x_hi, core).
Axes of the slice: x: 4 (x_hi: 2, x_lo: 2; x = x_hi * 2 + x_lo), y: 8, z: 8, core: 2. Of those that a mesh axis runs over, the one named last changes fastest.
Arguments:
- prob: float32 [768, 1024, 256], P('ctrl', 'shelf'), as said below
- ctrl_rates: float32 [768, 768], P('shelf'), as said below
- shelf_rates: float32 [1024, 1024], P('shelf'), as said below
- disk_rates: float32 [256, 256], replicated, as said below
- labels: int32 [768, 1024], P('ctrl', 'shelf'), may hold values from 0 to 255, as said below
Outputs:
- refined: float32 [768, 1024, 256], P('ctrl', 'shelf')
- coarse: float32 [256], replicated
Inputs may be any that keep to these rules, and one draw needn't show every extreme that they name: `prob`: positive. `ctrl_rates`: nonnegative entries. `shelf_rates`: nonnegative entries. `disk_rates`: nonnegative entries. Every block number from 0 to 255 labels at least one pair.
All inputs are finite; a program needn't handle non-finite values.
Results may differ from a plain program's by a relative error of at most 0.004.
Values may be sent and summed in bfloat16 or wider, within the bound.
A program may use at most 64 MiB of HBM per device.

v0:
```python
import jax
import jax.numpy as jnp
from jax import lax
from jax.sharding import PartitionSpec as P

CTRL = 768
SHELF = 1024
DISK = 256
NBLK = 256
STEPS = 2


def send_home(result):
    return lax.all_to_all(result, "ctrl", split_axis=1, concat_axis=0, tiled=True)


def ctrl_product(tensor, factor, pattern):
    result = jnp.einsum(
        pattern,
        lax.all_to_all(tensor, "ctrl", split_axis=0, concat_axis=1, tiled=True),
        factor,
        preferred_element_type=jnp.float32,
    ).astype(jnp.bfloat16)
    return send_home(result)


def shelf_product(tensor, factor, pattern):
    flattened = tensor.reshape(tensor.shape[0], tensor.shape[1] * tensor.shape[2])
    regrouped = lax.all_to_all(flattened, "shelf", split_axis=1, concat_axis=0, tiled=True)
    result = jnp.einsum(pattern, regrouped, factor, preferred_element_type=jnp.float32).astype(
        jnp.bfloat16
    )
    returned = lax.all_to_all(result, "shelf", split_axis=0, concat_axis=1, tiled=True)
    return returned.reshape(tensor.shape)


def local(prob, ctrl_rates, shelf_rates, disk_rates, labels):
    highest = lax.Precision.HIGHEST
    ctrl_bf, shelf_bf = (
        lax.all_gather(ctrl_rates.astype(jnp.bfloat16), "shelf", axis=0, tiled=True),
        lax.all_gather(shelf_rates.astype(jnp.bfloat16), "shelf", axis=0, tiled=True),
    )
    disk_bf = disk_rates.astype(jnp.bfloat16)
    ctrl_out = jnp.sum(ctrl_bf.astype(jnp.float32), axis=1)
    shelf_out = jnp.sum(shelf_bf.astype(jnp.float32), axis=1)
    disk_out = jnp.sum(disk_bf.astype(jnp.float32), axis=1)
    uniform_rate = 1.05 * (jnp.max(ctrl_out) * jnp.max(shelf_out)) * jnp.max(disk_out)
    ctrl_rows = prob.shape[0]
    shelf_rows = prob.shape[1]
    ctrl_loc = lax.dynamic_slice_in_dim(ctrl_out, lax.axis_index("ctrl") * ctrl_rows, ctrl_rows)
    shelf_loc = lax.dynamic_slice_in_dim(
        shelf_out, lax.axis_index("shelf") * shelf_rows, shelf_rows
    )
    retain = (
        1.0
        - ctrl_loc[None, :, None]
        * shelf_loc[:, None, None]
        * disk_out[None, None, :]
        / uniform_rate
    )
    iterate = jnp.transpose(prob, (1, 0, 2))
    for repeat in range(STEPS):
        rounded = iterate.astype(jnp.bfloat16)
        section_one = ctrl_product(rounded, ctrl_bf, "bac,ad->bdc")
        section_two = jnp.dot(
            section_one.reshape(shelf_rows * ctrl_rows, DISK),
            disk_bf,
            preferred_element_type=jnp.float32,
        )
        section_two = section_two.astype(jnp.bfloat16).reshape(section_one.shape)
        section_three = shelf_product(section_two, shelf_bf, "bq,bd->dq")
        iterate = section_three.astype(jnp.float32) / uniform_rate + iterate * retain
    pair_count = shelf_rows * ctrl_rows
    local_labels = jnp.transpose(labels)
    blocks = jnp.arange(NBLK, dtype=jnp.int32)
    member_table = (local_labels.reshape(pair_count)[:, None] == blocks[None, :]).astype(
        jnp.float32
    )
    flat_iterate = iterate.reshape(pair_count, DISK)
    pair_mass = jnp.sum(flat_iterate, axis=1)
    pair_kept = jnp.sum(flat_iterate * retain.reshape(pair_count, DISK), axis=1)
    weighted = jnp.dot(flat_iterate, disk_out, precision=highest)
    block_terms = jnp.dot(
        member_table.T, jnp.stack([pair_mass, pair_kept], axis=1), precision=highest
    )
    mass_term = block_terms[:, 0]
    kept_term = block_terms[:, 1]
    block_mass, block_kept = lax.psum((mass_term, kept_term), ("ctrl", "shelf"))
    member = (local_labels[:, :, None] == blocks[None, None, :]).astype(jnp.bfloat16)
    first_pass = ctrl_product(member, ctrl_bf, "bxl,ax->bal")
    coarse_op = shelf_product(first_pass, shelf_bf, "xq,bx->bq")
    flow_term = jnp.dot(
        (member_table * weighted[:, None]).T,
        coarse_op.reshape(pair_count, NBLK).astype(jnp.float32),
        precision=highest,
    )
    flow = lax.psum(flow_term, ("ctrl", "shelf"))
    identity = jnp.eye(NBLK, dtype=jnp.float32)
    transit = (flow / uniform_rate + identity * block_kept[:, None]) / block_mass[:, None]
    system = identity - transit + 1.0 / NBLK
    target = jnp.full((NBLK,), 1.0 / NBLK, dtype=jnp.float32)
    normal_matrix = jnp.dot(system, system.T, precision=highest)
    lower_factor = jnp.linalg.cholesky(normal_matrix)
    balance = jax.scipy.linalg.cho_solve(
        (lower_factor, True), jnp.dot(system, target, precision=highest)
    )
    ratio_share = balance / block_mass
    pair_share = jnp.dot(member_table, ratio_share, precision=highest).reshape(
        shelf_rows, ctrl_rows
    )
    scaled = iterate * pair_share[:, :, None] * float(CTRL * SHELF * DISK)
    refined = jnp.transpose(scaled, (1, 0, 2))
    coarse = balance * NBLK
    return (refined, coarse)


def solution(mesh):
    placed = (P("ctrl", "shelf", None), P("shelf", None), P("shelf", None), P(), P("ctrl", "shelf"))
    return jax.shard_map(
        local,
        mesh=mesh,
        in_specs=placed,
        out_specs=(P("ctrl", "shelf", None), P()),
        check_vma=False,
    )
```

profile of v0, /device:TPU:1, one launch (start us, length us, event | category | flops | bytes accessed | tf_op | source)
XLA Modules:
  0.0 790.1 jit_solution(13209121227176457720)
XLA Ops:
  11.9 8.7 %all-to-all-start = ((bf16[32,48,256]{2,1,0:T(8,128)(2,1)}), bf16[32,48,256]{2,1,0:T(8,128)(2,1)S(1)}, u32[]{:S(2)}, u32[]{:S(2)}) async-start(bf16[32,48,256]{2,1,0:T(8,128)(2,1)} %bitcast.162), calls=%async_computation | async-start | bytes 1572864 | tf_op jit(solution)/shard_map/all_to_all | solution.py:20
  21.3 18.9 %all-to-all-done = bf16[32,48,256]{2,1,0:T(8,128)(2,1)S(1)} async-done(((bf16[32,48,256]{2,1,0:T(8,128)(2,1)}), bf16[32,48,256]{2,1,0:T(8,128)(2,1)S(1)}, u32[]{:S(2)}, u32[]{:S(2)}) %all-to-all-start) | async-done | bytes 786464 | tf_op jit(solution)/shard_map/all_to_all | solution.py:20
  40.3 60.9 %all-gather.3.cloned.1.call-done = bf16[768,768]{1,0:T(8,128)(2,1)} async-done(((bf16[24,768]{1,0:T(8,128)(2,1)}), bf16[768,768]{1,0:T(8,128)(2,1)}) %all-gather.3.cloned.1.call-update) | async-done | bytes 1179664 | tf_op jit(solution)/shard_map/all_gather | solution.py:40
  104.1 28.8 %all_to_all.198 = bf16[2,768,256]{2,0,1:T(2,128)(2,1)S(1)} all-to-all(bf16[2,768,256]{2,0,1:T(2,128)(2,1)S(1)} %copy.58), channel_id=1, replica_groups=mesh['ctrl'=16,'shelf'=32] {'ctrl'}, dimensions={1} | all-to-all | bytes 1572864 | tf_op jit(solution)/shard_map/all_to_all | solution.py:14
  135.8 7.6 all-to-all-start.2
  143.4 46.6 %all-gather.5.cloned.1.call-done = bf16[1024,1024]{1,0:T(8,128)(2,1)} async-done(((bf16[32,1024]{1,0:T(8,128)(2,1)}), bf16[1024,1024]{1,0:T(8,128)(2,1)}) %all-gather.5.cloned.1.call-update) | async-done | bytes 2097168 | tf_op jit(solution)/shard_map/all_gather | solution.py:41
  193.8 5.5 all-to-all-start.3
  200.4 21.4 %all-to-all-done.3 = bf16[32,32,384]{2,1,0:T(8,128)(2,1)S(1)} async-done(((bf16[32,32,384]{2,1,0:T(8,128)(2,1)}), bf16[32,32,384]{2,1,0:T(8,128)(2,1)S(1)}, u32[]{:S(2)}, u32[]{:S(2)}) %all-to-all-start.3) | async-done | bytes 786464 | tf_op jit(solution)/shard_map/all_to_all | solution.py:33
  221.9 5.9 all-to-all-start.8
  238.8 3.7 fusion.45
  242.6 5.6 all-to-all-done.8
  248.2 5.7 all-to-all-start.4
  260.1 14.2 %all-to-all-done.4 = bf16[32,48,256]{2,1,0:T(8,128)(2,1)S(1)} async-done(((bf16[32,48,256]{2,1,0:T(8,128)(2,1)}), bf16[32,48,256]{2,1,0:T(8,128)(2,1)S(1)}, u32[]{:S(2)}, u32[]{:S(2)}) %all-to-all-start.4) | async-done | bytes 786464 | tf_op jit(solution)/shard_map/all_to_all | solution.py:20
  275.3 5.9 all-to-all-start.9
  287.4 14.1 %all-to-all-done.9 = bf16[2,768,256]{2,0,1:T(2,128)(2,1)S(1)} async-done(((bf16[2,768,256]{2,0,1:T(2,128)(2,1)}), bf16[2,768,256]{2,0,1:T(2,128)(2,1)S(1)}, u32[]{:S(2)}, u32[]{:S(2)}) %all-to-all-start.9) | async-done | bytes 786464 | tf_op jit(solution)/shard_map/all_to_all | solution.py:14
  302.3 5.7 all-to-all-start.5
  314.8 13.6 %all-to-all-done.5 = bf16[2,768,256]{2,0,1:T(2,128)(2,1)S(1)} async-done(((bf16[2,768,256]{2,0,1:T(2,128)(2,1)}), bf16[2,768,256]{2,0,1:T(2,128)(2,1)S(1)}, u32[]{:S(2)}, u32[]{:S(2)}) %all-to-all-start.5) | async-done | bytes 786464 | tf_op jit(solution)/shard_map/all_to_all | solution.py:14
  328.5 9.2 %all-to-all-start.10 = ((bf16[32,32,384]{2,0,1:T(8,128)(2,1)}), bf16[32,32,384]{2,0,1:T(8,128)(2,1)}, u32[]{:S(2)}, u32[]{:S(2)}) async-start(bf16[32,32,384]{2,0,1:T(8,128)(2,1)} %copy.77), calls=%async_computation.10 | async-start | bytes 1572864 | tf_op jit(solution)/shard_map/all_to_all | solution.py:29
  341.9 18.4 %all-to-all-done.10 = bf16[32,32,384]{2,0,1:T(8,128)(2,1)} async-done(((bf16[32,32,384]{2,0,1:T(8,128)(2,1)}), bf16[32,32,384]{2,0,1:T(8,128)(2,1)}, u32[]{:S(2)}, u32[]{:S(2)}) %all-to-all-start.10) | async-done | bytes 786464 | tf_op jit(solution)/shard_map/all_to_all | solution.py:29
  360.3 5.7 all-to-all-start.6
  371.4 17.3 %all-to-all-done.6 = bf16[32,32,384]{2,0,1:T(8,128)(2,1)S(1)} async-done(((bf16[32,32,384]{2,0,1:T(8,128)(2,1)}), bf16[32,32,384]{2,0,1:T(8,128)(2,1)S(1)}, u32[]{:S(2)}, u32[]{:S(2)}) %all-to-all-start.6) | async-done | bytes 786464 | tf_op jit(solution)/shard_map/all_to_all | solution.py:29
  388.6 5.7 all-to-all-start.11
  398.6 18.5 %all-to-all-done.11 = bf16[32,32,384]{2,1,0:T(8,128)(2,1)} async-done(((bf16[32,32,384]{2,1,0:T(8,128)(2,1)}), bf16[32,32,384]{2,1,0:T(8,128)(2,1)}, u32[]{:S(2)}, u32[]{:S(2)}) %all-to-all-start.11) | async-done | bytes 786464 | tf_op jit(solution)/shard_map/all_to_all | solution.py:33
  417.0 5.7 all-to-all-start.7
  425.6 19.7 %all-to-all-done.7 = bf16[32,32,384]{2,1,0:T(8,128)(2,1)S(1)} async-done(((bf16[32,32,384]{2,1,0:T(8,128)(2,1)}), bf16[32,32,384]{2,1,0:T(8,128)(2,1)S(1)}, u32[]{:S(2)}, u32[]{:S(2)}) %all-to-all-start.7) | async-done | bytes 786464 | tf_op jit(solution)/shard_map/all_to_all | solution.py:33
  456.5 95.3 %all-reduce.1 = (f32[256]{0:T(256)S(1)}, f32[256]{0:T(256)S(1)}) all-reduce(f32[256]{0:T(256)S(1)} %bitcast.189, f32[256]{0:T(256)S(1)} %bitcast.188), channel_id=1, replica_groups=mesh['ctrl'=16,'shelf'=32] {'ctrl','shelf'}, use_global_device_ids=true, to_apply=%region_10.0 | all-reduce | flops 512 | bytes 4096 | tf_op jit(solution)/shard_map/psum | solution.py:88
  551.8 164.7 %all-reduce.4.cloned.1.call-done = f32[256,256]{1,0:T(8,128)} async-done(((f32[256,256]{1,0:T(8,128)}), f32[256,256]{1,0:T(8,128)}) %all-reduce.4.cloned.1.call-update) | async-done | bytes 262160 | tf_op jit(solution)/shard_map/psum | solution.py:97
  718.6 11.7 %cholesky.49 = f32[128,128]{1,0:T(8,128)S(1)} custom-call(f32[128,128]{1,0:T(8,128)S(1)} %cholesky.115), custom_call_target="Cholesky" | custom-call | tf_op jit(solution)/shard_map/jit(cholesky)/cholesky | solution.py:103
  730.3 9.8 %custom-call.18 = f32[1,128,128]{1,2,0:T(8,128)S(1)} custom-call(f32[1,128,128]{2,1,0:T(8,128)S(1)} %get-tuple-element.34), custom_call_target="InvertDiagBlocksLowerTriangular" | custom-call | tf_op jit(solution)/shard_map/jit(cholesky)/cholesky | solution.py:103
  740.7 11.7 %cholesky.103 = f32[128,128]{1,0:T(8,128)S(1)} custom-call(f32[128,128]{1,0:T(8,128)S(1)} %convolution_subtract_fusion), custom_call_target="Cholesky" | custom-call | tf_op jit(solution)/shard_map/jit(cholesky)/cholesky | solution.py:103
  754.5 4.0 while.1
  758.5 19.9 %custom-call.19 = f32[2,128,128]{1,2,0:T(8,128)S(1)} custom-call(f32[2,128,128]{2,1,0:T(8,128)S(1)} %get-tuple-element.9), custom_call_target="InvertDiagBlocksLowerTriangular" | custom-call | tf_op jit(solution)/shard_map/jit(_cho_solve)/triangular_solve | solution.py:104
  (119 shorter events, 86.1 us)
Async XLA Ops:
  7.2 94.0 %all-gather.3.cloned.1.call-start = ((), (), s32[]{:S(2)}) async-start(), calls=%async_computation.12 | async-start | bytes 1216512 | tf_op jit(solution)/shard_map/all_gather | solution.py:40
  8.7 11.9 %copy-start.8 = (f32[32,1024]{1,0:T(8,128)S(1)}, f32[32,1024]{1,0:T(8,128)}, u32[]{:S(2)}) copy-start(f32[32,1024]{1,0:T(8,128)} %param.7) | copy-start | bytes 393220
  11.9 28.3 %all-to-all-start = ((bf16[32,48,256]{2,1,0:T(8,128)(2,1)}), bf16[32,48,256]{2,1,0:T(8,128)(2,1)S(1)}, u32[]{:S(2)}, u32[]{:S(2)}) async-start(bf16[32,48,256]{2,1,0:T(8,128)(2,1)} %bitcast.162), calls=%async_computation | async-start | bytes 1572864 | tf_op jit(solution)/shard_map/all_to_all | solution.py:20
  20.6 169.4 %all-gather.5.cloned.1.call-start = ((), (), s32[]{:S(2)}) async-start(), calls=%async_computation.13 | async-start | bytes 2162688 | tf_op jit(solution)/shard_map/all_gather | solution.py:41
  132.9 1.0 copy-start.4
  135.8 54.2 %all-to-all-start.2 = ((bf16[32,32,384]{2,0,1:T(8,128)(2,1)}), bf16[32,32,384]{2,0,1:T(8,128)(2,1)S(1)}, u32[]{:S(2)}, u32[]{:S(2)}) async-start(bf16[32,32,384]{2,0,1:T(8,128)(2,1)} %copy.61), calls=%async_computation.2 | async-start | bytes 1572864 | tf_op jit(solution)/shard_map/all_to_all | solution.py:29
  192.6 6.7 copy-start.9
  193.8 28.1 %all-to-all-start.3 = ((bf16[32,32,384]{2,1,0:T(8,128)(2,1)}), bf16[32,32,384]{2,1,0:T(8,128)(2,1)S(1)}, u32[]{:S(2)}, u32[]{:S(2)}) async-start(bf16[32,32,384]{2,1,0:T(8,128)(2,1)} %bitcast.12), calls=%async_computation.3 | async-start | bytes 1572864 | tf_op jit(solution)/shard_map/all_to_all | solution.py:33
  200.4 30.3 %copy-start = (bf16[1024,1024]{1,0:T(8,128)(2,1)S(1)}, bf16[1024,1024]{1,0:T(8,128)(2,1)}, u32[]{:S(2)}) copy-start(bf16[1024,1024]{1,0:T(8,128)(2,1)} %all-gather.5.cloned.1.call-done) | copy-start | bytes 6291460
  221.9 26.3 %all-to-all-start.8 = ((bf16[32,48,256]{2,1,0:T(8,128)(2,1)}), bf16[32,48,256]{2,1,0:T(8,128)(2,1)}, u32[]{:S(2)}, u32[]{:S(2)}) async-start(bf16[32,48,256]{2,1,0:T(8,128)(2,1)} %fusion.5), calls=%async_computation.8 | async-start | bytes 1572864 | tf_op jit(solution)/shard_map/all_to_all | solution.py:20
  248.2 26.2 %all-to-all-start.4 = ((bf16[32,48,256]{2,1,0:T(8,128)(2,1)}), bf16[32,48,256]{2,1,0:T(8,128)(2,1)S(1)}, u32[]{:S(2)}, u32[]{:S(2)}) async-start(bf16[32,48,256]{2,1,0:T(8,128)(2,1)} %fusion.45), calls=%async_computation.4 | async-start | bytes 1572864 | tf_op jit(solution)/shard_map/all_to_all | solution.py:20
  253.9 1.5 copy-start.5
  274.4 0.9 copy-start.3
  275.3 26.2 %all-to-all-start.9 = ((bf16[2,768,256]{2,0,1:T(2,128)(2,1)}), bf16[2,768,256]{2,0,1:T(2,128)(2,1)S(1)}, u32[]{:S(2)}, u32[]{:S(2)}) async-start(bf16[2,768,256]{2,0,1:T(2,128)(2,1)} %copy.74), calls=%async_computation.9 | async-start | bytes 1572864 | tf_op jit(solution)/shard_map/all_to_all | solution.py:14
  281.2 1.5 copy-start.6
  301.5 0.9 copy-start.2
  302.3 26.1 %all-to-all-start.5 = ((bf16[2,768,256]{2,0,1:T(2,128)(2,1)}), bf16[2,768,256]{2,0,1:T(2,128)(2,1)S(1)}, u32[]{:S(2)}, u32[]{:S(2)}) async-start(bf16[2,768,256]{2,0,1:T(2,128)(2,1)} %copy.66), calls=%async_computation.5 | async-start | bytes 1572864 | tf_op jit(solution)/shard_map/all_to_all | solution.py:14
  328.5 31.8 %all-to-all-start.10 = ((bf16[32,32,384]{2,0,1:T(8,128)(2,1)}), bf16[32,32,384]{2,0,1:T(8,128)(2,1)}, u32[]{:S(2)}, u32[]{:S(2)}) async-start(bf16[32,32,384]{2,0,1:T(8,128)(2,1)} %copy.77), calls=%async_computation.10 | async-start | bytes 1572864 | tf_op jit(solution)/shard_map/all_to_all | solution.py:29
  360.3 28.3 %all-to-all-start.6 = ((bf16[32,32,384]{2,0,1:T(8,128)(2,1)}), bf16[32,32,384]{2,0,1:T(8,128)(2,1)S(1)}, u32[]{:S(2)}, u32[]{:S(2)}) async-start(bf16[32,32,384]{2,0,1:T(8,128)(2,1)} %copy.69), calls=%async_computation.6 | async-start | bytes 1572864 | tf_op jit(solution)/shard_map/all_to_all | solution.py:29
  388.6 28.4 %all-to-all-start.11 = ((bf16[32,32,384]{2,1,0:T(8,128)(2,1)}), bf16[32,32,384]{2,1,0:T(8,128)(2,1)}, u32[]{:S(2)}, u32[]{:S(2)}) async-start(bf16[32,32,384]{2,1,0:T(8,128)(2,1)} %bitcast.176), calls=%async_computation.11 | async-start | bytes 1572864 | tf_op jit(solution)/shard_map/all_to_all | solution.py:33
  417.0 28.3 %all-to-all-start.7 = ((bf16[32,32,384]{2,1,0:T(8,128)(2,1)}), bf16[32,32,384]{2,1,0:T(8,128)(2,1)S(1)}, u32[]{:S(2)}, u32[]{:S(2)}) async-start(bf16[32,32,384]{2,1,0:T(8,128)(2,1)} %bitcast.24), calls=%async_computation.7 | async-start | bytes 1572864 | tf_op jit(solution)/shard_map/all_to_all | solution.py:33
  422.8 293.8 %all-reduce.4.cloned.1.call-start = ((), (), s32[]{:S(2)}) async-start(), calls=%async_computation.14 | async-start | bytes 524288 | tf_op jit(solution)/shard_map/psum | solution.py:97
  446.5 1.6 copy-start.1
  451.6 1.6 copy-start.7
Sparse Core Ops, SparseCore 0:
  11.3 89.8 all-gather.2
  104.5 85.4 all-gather.4
  455.9 260.5 all-reduce.3
where the time goes:
time: 800 us; the launch traced here: 790 us
  waiting for transfers between devices  434 us (54%)
  blocking collectives  124 us (16%)
  starting transfers between devices  71.5 us (9%)
  other arithmetic  70.7 us (9%)
  local copies, waits for them, and re-layouts  50.5 us (6%)
  matrix products  21.5 us (3%)
  between operations  17.7 us (2%)
    psum x1, waiting for transfers between devices, local(): flow = lax.psum(flow_term, ('ctrl', 'shelf'))  165 us
    psum x1, blocking collectives, local(): block_mass, block_kept = lax.psum((mass_term, kept_term), ('ctrl', 'shelf'))  95.3 us
    all_gather x1, waiting for transfers between devices, local(): lax.all_gather(ctrl_rates.astype(jnp.bfloat16), 'shelf', axis=0, tiled=True)  60.9 us
    all_to_all x3, waiting for transfers between devices, shelf_product(): lax.all_to_all(result, 'shelf', split_axis=0, concat_axis=1, tiled=True)  59.6 us
    all_gather x1, waiting for transfers between devices, local(): lax.all_gather(shelf_rates.astype(jnp.bfloat16), 'shelf', axis=0, tiled=T...  46.6 us
    all_to_all x3, waiting for transfers between devices, ctrl_product(): lax.all_to_all(tensor, 'ctrl', split_axis=0, concat_axis=1, tiled=True)  38.7 us
    all_to_all x3, waiting for transfers between devices, shelf_product(): lax.all_to_all(flattened, 'shelf', split_axis=1, concat_axis=0, tiled=True)  35.7 us
    another operation x6, other arithmetic, local(): lower_factor = jnp.linalg.cholesky(normal_matrix)  34 us
  transfers between devices with their start and end apart: 14, of which 13 were waited for; matrix products, arithmetic and copies ran while one was open for 7% of the time, Pallas kernels for 0%

commit v1 on v0

v1 whole, which is shorter than its diff:
```python
import functools

import jax
import jax.numpy as jnp
from jax import lax
from jax.experimental import pallas as pl
from jax.experimental.pallas import tpu as pltpu
from jax.sharding import PartitionSpec as P

CTRL = 768
SHELF = 1024
DISK = 256
NBLK = 256
STEPS = 2
GROUP = 8
MESH = pl.DeviceIdType.MESH
VMEM = pltpu.MemorySpace.VMEM
HIGHEST = lax.Precision.HIGHEST


def place():
    ctrl = lax.axis_index("ctrl")
    shelf = lax.axis_index("shelf")
    plane_me = (ctrl % 2) * 4 + shelf % 4
    deep_me = shelf // 4
    high_me = ctrl // 2

    def plane(member):
        return (ctrl - ctrl % 2 + member // 4, shelf - shelf % 4 + member % 4)

    def deep(member):
        return (ctrl, member * 4 + shelf % 4)

    def high(member):
        return (member * 2 + ctrl % 2, shelf)

    return (plane_me, plane), (deep_me, deep), (high_me, high)


def greet(groups):
    barrier = pltpu.get_barrier_semaphore()
    for me, peer in groups:

        def signal(step, carry, me=me, peer=peer):
            pl.semaphore_signal(
                barrier, inc=1, device_id=peer((me + step) % GROUP), device_id_type=MESH
            )
            return carry

        lax.fori_loop(1, GROUP, signal, 0)
    pl.semaphore_wait(barrier, len(groups) * (GROUP - 1))


def exchange(group, streams, send_sem, recv_sem):
    me, peer = group

    def copy(step, index):
        source, target = streams[index]
        member = (me + step) % GROUP
        return pltpu.make_async_remote_copy(
            src_ref=source(member),
            dst_ref=target,
            send_sem=send_sem.at[index, step],
            recv_sem=recv_sem.at[index, step],
            device_id=peer(member),
            device_id_type=MESH,
        )

    def start(step, carry):
        for index in range(len(streams)):
            copy(step, index).start()
        return carry

    def finish(step, carry):
        for index in range(len(streams)):
            copy(step, index).wait()
        return carry

    lax.fori_loop(1, GROUP, start, 0)
    lax.fori_loop(1, GROUP, finish, 0)


def reduce_kernel(
    part_ref, mass_ref, sum_ref, total_ref,
    rows, tiles, highs, deeps, blocks, mass_plane, mass_deep, mass_high,
    send_sem, recv_sem,
):
    plane, deep, high = place()
    greet((plane, deep, high))
    plane_me, deep_me, high_me = plane[0], deep[0], high[0]

    exchange(
        plane,
        (
            (lambda m: part_ref.at[pl.ds(pl.multiple_of(m * 32, 32), 32)], rows.at[plane_me]),
            (lambda m: mass_ref, mass_plane.at[plane_me]),
        ),
        send_sem.at[0], recv_sem.at[0],
    )
    rows[plane_me] = part_ref[pl.ds(pl.multiple_of(plane_me * 32, 32), 32)]
    mass_plane[plane_me] = mass_ref[...]
    mine = jnp.sum(rows[...], axis=0)
    for tile in range(GROUP):
        r, h = tile // 2, tile % 2
        tiles[tile] = mine[r * 8 : r * 8 + 8, h * 128 : h * 128 + 128]
    total_ref[...] = jnp.sum(mass_plane[...], axis=0)

    exchange(
        deep,
        (
            (lambda m: tiles.at[m], deeps.at[deep_me]),
            (lambda m: total_ref, mass_deep.at[deep_me]),
        ),
        send_sem.at[1], recv_sem.at[1],
    )
    deeps[deep_me] = tiles[deep_me]
    mass_deep[deep_me] = total_ref[...]
    highs[high_me] = jnp.sum(deeps[...], axis=0)
    mass_high[high_me] = jnp.sum(mass_deep[...], axis=0)

    exchange(
        high,
        (
            (lambda m: highs.at[high_me], highs.at[high_me]),
            (lambda m: mass_high.at[high_me], mass_high.at[high_me]),
        ),
        send_sem.at[2], recv_sem.at[2],
    )
    total_ref[...] = jnp.sum(mass_high[...], axis=0)
    blocks[deep_me] = jnp.sum(highs[...], axis=0)

    exchange(
        deep,
        ((lambda m: blocks.at[deep_me], blocks.at[deep_me]),),
        send_sem.at[3], recv_sem.at[3],
    )
    for tile in range(GROUP):
        r, h = tile // 2, tile % 2
        sum_ref[
            pl.ds(pl.multiple_of(plane_me * 32 + r * 8, 8), 8), h * 128 : h * 128 + 128
        ] = blocks[tile]
    own = sum_ref.at[pl.ds(pl.multiple_of(plane_me * 32, 32), 32)]
    exchange(plane, ((lambda m: own, own),), send_sem.at[4], recv_sem.at[4])


def reduce_all(part, mass):
    tile = (8, 128)
    return pl.pallas_call(
        reduce_kernel,
        out_shape=(
            jax.ShapeDtypeStruct((NBLK, NBLK), jnp.float32),
            jax.ShapeDtypeStruct(tile, jnp.float32),
        ),
        in_specs=[pl.BlockSpec(memory_space=VMEM)] * 2,
        out_specs=(pl.BlockSpec(memory_space=VMEM), pl.BlockSpec(memory_space=VMEM)),
        scratch_shapes=[
            pltpu.VMEM((GROUP, 32, NBLK), jnp.float32),
            pltpu.VMEM((GROUP, *tile), jnp.float32),
            pltpu.VMEM((GROUP, *tile), jnp.float32),
            pltpu.VMEM((GROUP, *tile), jnp.float32),
            pltpu.VMEM((GROUP, *tile), jnp.float32),
            pltpu.VMEM((GROUP, *tile), jnp.float32),
            pltpu.VMEM((GROUP, *tile), jnp.float32),
            pltpu.VMEM((GROUP, *tile), jnp.float32),
            pltpu.SemaphoreType.DMA((5, 2, GROUP)),
            pltpu.SemaphoreType.DMA((5, 2, GROUP)),
        ],
        compiler_params=pltpu.CompilerParams(collective_id=1, has_side_effects=True),
        name="reduce_all",
    )(part, mass)


def member_kernel(labels_ref, factor_ref, out_ref):
    count = labels_ref.shape[1]
    blocks = lax.broadcasted_iota(jnp.int32, (NBLK, count), 0).astype(jnp.float32)

    def body(row, carry):
        names = jnp.broadcast_to(labels_ref[pl.ds(row, 1), :], (NBLK, count))
        member = jnp.where(names == blocks, 1.0, 0.0).astype(jnp.bfloat16)
        out_ref[row] = lax.dot_general(
            factor_ref[...], member, (((1,), (1,)), ((), ())), preferred_element_type=jnp.float32
        ).astype(out_ref.dtype)
        return carry

    lax.fori_loop(0, labels_ref.shape[0], body, 0)


def member_product(labels, factor):
    return pl.pallas_call(
        member_kernel,
        out_shape=jax.ShapeDtypeStruct((labels.shape[0], factor.shape[0], NBLK), jnp.bfloat16),
        in_specs=[pl.BlockSpec(memory_space=VMEM)] * 2,
        out_specs=pl.BlockSpec(memory_space=VMEM),
        compiler_params=pltpu.CompilerParams(vmem_limit_bytes=40 << 20),
        name="member_product",
    )(labels, factor)


def flow_kernel(labels_ref, weight_ref, factor_ref, first_ref, out_ref, wide, held):
    count = labels_ref.shape[1]
    depth = factor_ref.shape[0]
    blocks = lax.broadcasted_iota(jnp.int32, (NBLK, count), 0).astype(jnp.float32)

    def body(row, carry):
        names = jnp.broadcast_to(labels_ref[pl.ds(row, 1), :], (NBLK, count))
        member = jnp.where(names == blocks, 1.0, 0.0).astype(jnp.bfloat16)
        scaled = factor_ref[...] * weight_ref[pl.ds(row, 1), :]
        upper = scaled.astype(jnp.bfloat16)
        wide[0:depth, :] = upper
        wide[depth : 2 * depth, :] = (scaled - upper.astype(jnp.float32)).astype(jnp.bfloat16)
        both = lax.dot_general(
            wide[...], member, (((1,), (1,)), ((), ())), preferred_element_type=jnp.float32
        )
        held[:, pl.ds(row, 1), :] = (both[0:depth] + both[depth:]).reshape(depth, 1, NBLK)
        return carry

    lax.fori_loop(0, labels_ref.shape[0], body, 0)
    rows = held.shape[0] * held.shape[1]
    mine = held[...].reshape(rows, NBLK)
    first = first_ref[...].reshape(rows, NBLK)
    upper = mine.astype(jnp.bfloat16)
    lower = (mine - upper.astype(jnp.float32)).astype(jnp.bfloat16)
    dims = (((0,), (0,)), ((), ()))
    out_ref[...] = lax.dot_general(
        upper, first, dims, preferred_element_type=jnp.float32
    ) + lax.dot_general(lower, first, dims, preferred_element_type=jnp.float32)


def flow_product(labels, weight, factor, first):
    depth, count = factor.shape
    return pl.pallas_call(
        flow_kernel,
        out_shape=jax.ShapeDtypeStruct((NBLK, NBLK), jnp.float32),
        in_specs=[pl.BlockSpec(memory_space=VMEM)] * 4,
        out_specs=pl.BlockSpec(memory_space=VMEM),
        scratch_shapes=[
            pltpu.VMEM((2 * depth, count), jnp.bfloat16),
            pltpu.VMEM((depth, labels.shape[0], NBLK), jnp.float32),
        ],
        compiler_params=pltpu.CompilerParams(vmem_limit_bytes=40 << 20),
        name="flow_product",
    )(labels, weight, factor, first)


def balance_kernel(numer_ref, mass_ref, out_ref, power):
    size = NBLK
    power[...] = numer_ref[...] / mass_ref[...] - 1.0 / size
    start = jnp.full((8, size), 1.0 / size, jnp.float32)

    def going(state):
        turn, height, row = state
        return jnp.logical_and(turn < 40, height > 1e-10)

    def turn_once(state):
        turn, height, row = state
        now = power[...]
        row = row + jnp.dot(row, now, precision=HIGHEST, preferred_element_type=jnp.float32)
        after = jnp.dot(now, now, precision=HIGHEST, preferred_element_type=jnp.float32)
        power[...] = after
        return turn + 1, jnp.max(jnp.abs(after)), row

    state = (jnp.int32(0), jnp.max(jnp.abs(power[...])), start)
    out_ref[...] = lax.while_loop(going, turn_once, state)[2]


def balance_of(numer, mass):
    return pl.pallas_call(
        balance_kernel,
        out_shape=jax.ShapeDtypeStruct((8, NBLK), jnp.float32),
        in_specs=[pl.BlockSpec(memory_space=VMEM)] * 2,
        out_specs=pl.BlockSpec(memory_space=VMEM),
        scratch_shapes=[pltpu.VMEM((NBLK, NBLK), jnp.float32)],
        name="balance",
    )(numer, mass)[0]


def ctrl_product(tensor, factor, pattern):
    result = jnp.einsum(
        pattern,
        lax.all_to_all(tensor, "ctrl", split_axis=0, concat_axis=1, tiled=True),
        factor,
        preferred_element_type=jnp.float32,
    ).astype(jnp.bfloat16)
    return lax.all_to_all(result, "ctrl", split_axis=1, concat_axis=0, tiled=True)


def shelf_product(tensor, factor, pattern):
    flattened = tensor.reshape(tensor.shape[0], tensor.shape[1] * tensor.shape[2])
    regrouped = lax.all_to_all(flattened, "shelf", split_axis=1, concat_axis=0, tiled=True)
    result = jnp.einsum(pattern, regrouped, factor, preferred_element_type=jnp.float32).astype(
        jnp.bfloat16
    )
    returned = lax.all_to_all(result, "shelf", split_axis=0, concat_axis=1, tiled=True)
    return returned.reshape(tensor.shape)


def local(prob, ctrl_rates, shelf_rates, disk_rates, labels):
    ctrl_bf = lax.all_gather(ctrl_rates.astype(jnp.bfloat16), "shelf", axis=0, tiled=True)
    shelf_bf = lax.all_gather(shelf_rates.astype(jnp.bfloat16), "shelf", axis=0, tiled=True)
    disk_bf = disk_rates.astype(jnp.bfloat16)
    ctrl_out = jnp.sum(ctrl_bf.astype(jnp.float32), axis=1)
    shelf_out = jnp.sum(shelf_bf.astype(jnp.float32), axis=1)
    disk_out = jnp.sum(disk_bf.astype(jnp.float32), axis=1)
    uniform_rate = 1.05 * (jnp.max(ctrl_out) * jnp.max(shelf_out)) * jnp.max(disk_out)
    ctrl_rows = prob.shape[0]
    shelf_rows = prob.shape[1]
    ctrl_at = lax.axis_index("ctrl") * ctrl_rows
    shelf_at = lax.axis_index("shelf") * shelf_rows
    ctrl_loc = lax.dynamic_slice_in_dim(ctrl_out, ctrl_at, ctrl_rows)
    shelf_loc = lax.dynamic_slice_in_dim(shelf_out, shelf_at, shelf_rows)
    retain = (
        1.0
        - ctrl_loc[None, :, None]
        * shelf_loc[:, None, None]
        * disk_out[None, None, :]
        / uniform_rate
    )
    label_f = labels.astype(jnp.bfloat16)
    ctrl_labels = lax.all_gather(label_f.T, "ctrl", axis=1, tiled=True).astype(jnp.float32)
    shelf_labels = lax.all_gather(label_f, "shelf", axis=1, tiled=True).astype(jnp.float32)

    iterate = jnp.transpose(prob, (1, 0, 2))
    for repeat in range(STEPS):
        rounded = iterate.astype(jnp.bfloat16)
        section_one = ctrl_product(rounded, ctrl_bf, "bac,ad->bdc")
        section_two = jnp.dot(
            section_one.reshape(shelf_rows * ctrl_rows, DISK),
            disk_bf,
            preferred_element_type=jnp.float32,
        )
        section_two = section_two.astype(jnp.bfloat16).reshape(section_one.shape)
        section_three = shelf_product(section_two, shelf_bf, "bq,bd->dq")
        iterate = section_three.astype(jnp.float32) / uniform_rate + iterate * retain

    first = member_product(ctrl_labels, lax.dynamic_slice_in_dim(ctrl_bf, ctrl_at, ctrl_rows))
    shelf_columns = lax.dynamic_slice_in_dim(shelf_bf, shelf_at, shelf_rows, axis=1)
    shelf_columns = shelf_columns.T.astype(jnp.float32)

    pair_mass = jnp.sum(iterate, axis=2)
    pair_kept = jnp.sum(iterate * retain, axis=2)
    weighted = jnp.sum(iterate * disk_out, axis=2)
    shelf_weight = lax.all_gather(weighted.T, "shelf", axis=1, tiled=True)
    part = flow_product(shelf_labels, shelf_weight, shelf_columns, first) / uniform_rate
    pair_count = shelf_rows * ctrl_rows
    own_labels = labels.T
    blocks = jnp.arange(NBLK, dtype=jnp.int32)
    member_table = (own_labels.reshape(pair_count)[:, None] == blocks[None, :]).astype(
        jnp.float32
    )
    terms = jnp.dot(
        jnp.stack([pair_mass.reshape(pair_count), pair_kept.reshape(pair_count)]),
        member_table,
        precision=HIGHEST,
    )
    identity = jnp.eye(NBLK, dtype=jnp.float32)
    part = part + identity * terms[1][:, None]
    mass_tile = jnp.zeros((8, 128), jnp.float32).at[0:2].set(terms[0].reshape(2, 128))
    numer, mass_sum = reduce_all(part, mass_tile)
    block_mass = mass_sum[0:2].reshape(NBLK)
    balance = balance_of(numer, jnp.broadcast_to(block_mass[:, None], (NBLK, NBLK)))
    ratio_share = balance / block_mass
    pair_share = jnp.dot(member_table, ratio_share, precision=HIGHEST).reshape(
        shelf_rows, ctrl_rows
    )
    scaled = iterate * pair_share[:, :, None] * float(CTRL * SHELF * DISK)
    refined = jnp.transpose(scaled, (1, 0, 2))
    coarse = balance * NBLK
    return (refined, coarse)


def solution(mesh):
    placed = (P("ctrl", "shelf", None), P("shelf", None), P("shelf", None), P(), P("ctrl", "shelf"))
    return jax.shard_map(
        local,
        mesh=mesh,
        in_specs=placed,
        out_specs=(P("ctrl", "shelf", None), P()),
        check_vma=False,
    )
```

time: 800 us -> 534 us (0.67); the launches traced: 790 us -> 533 us
  waiting for transfers between devices: 434 us -> 143 us
  blocking collectives: 124 us -> 225 us
  Pallas kernels: 0 us -> 63.1 us
  other arithmetic: 70.7 us -> 17.1 us
  starting transfers between devices: 71.5 us -> 27.7 us
  local copies, waits for them, and re-layouts: 50.5 us -> 30 us
  matrix products: 21.5 us -> 10.7 us
    psum x1 -> x0, waiting for transfers between devices: 165 us -> none  [local(): flow = lax.psum(flow_term, ('ctrl', 'shelf'))]
    all_gather x0 -> x3, blocking collectives: none -> 112 us  [the longest x1 48.8 us: local(): lax.all_gather(label_f, 'shelf', axis=1, tiled=True).astype(jnp.float32)]
    psum x1 -> x0, blocking collectives: 95.3 us -> none  [local(): block_mass, block_kept = lax.psum((mass_term, kept_term), ('ctrl', 'shelf'))]
    all_to_all x1 -> x4, blocking collectives: 28.8 us -> 113 us  [the longest x2 53.2 us: ctrl_product(): lax.all_to_all(result, 'ctrl', split_axis=1, concat_axis=0, tiled=True)]
    pallas_call x0 -> x4, Pallas kernels: none -> 63.1 us  [the longest x1 32.2 us: reduce_all(): pl.pallas_call(reduce_kernel, out_shape=(jax.ShapeDtypeStruct((NBLK, NBLK...]
    another operation x10 -> x0, other arithmetic: 53.9 us -> none  [the longest x6 34 us: local(): lower_factor = jnp.linalg.cholesky(normal_matrix)]
    all_to_all x3 -> x2, waiting for transfers between devices: 59.6 us -> 16.6 us  [shelf_product(): lax.all_to_all(result, 'shelf', split_axis=0, concat_axis=1, tiled=True)]
    all_to_all x3 -> x1, waiting for transfers between devices: 35.7 us -> 0.01 us  [shelf_product(): lax.all_to_all(flattened, 'shelf', split_axis=1, concat_axis=0, tiled=True)]
  transfers between devices with their start and end apart: 14 -> 6, of which waited for: 13 -> 4; matrix products, arithmetic and copies ran while one was open for 7% -> 3% of each run, Pallas kernels for 0% -> 2%
where the time goes in v1:
time: 534 us; the launch traced here: 533 us
  blocking collectives  225 us (42%)
  waiting for transfers between devices  143 us (27%)
  Pallas kernels  63.1 us (12%)
  local copies, waits for them, and re-layouts  30 us (6%)
  starting transfers between devices  27.7 us (5%)
  other arithmetic  17.1 us (3%)
  between operations  16.3 us (3%)
  matrix products  10.7 us (2%)
    all_gather x1, waiting for transfers between devices, local(): lax.all_gather(ctrl_rates.astype(jnp.bfloat16), 'shelf', axis=0, tiled=True)  60.9 us
    all_to_all x2, blocking collectives, ctrl_product(): lax.all_to_all(result, 'ctrl', split_axis=1, concat_axis=0, tiled=True)  53.2 us
    all_gather x1, blocking collectives, local(): lax.all_gather(label_f, 'shelf', axis=1, tiled=True).astype(jnp.float32)  48.8 us
    all_gather x1, waiting for transfers between devices, local(): lax.all_gather(shelf_rates.astype(jnp.bfloat16), 'shelf', axis=0, tiled=T...  46.6 us
    all_gather x1, blocking collectives, local(): shelf_weight = lax.all_gather(weighted.T, 'shelf', axis=1, tiled=True)  38.2 us
    all_to_all x1, blocking collectives, shelf_product(): lax.all_to_all(flattened, 'shelf', split_axis=1, concat_axis=0, tiled=True)  32.4 us
    pallas_call x1, Pallas kernels, reduce_all(): pl.pallas_call(reduce_kernel, out_shape=(jax.ShapeDtypeStruct((NBLK, NBLK...  32.2 us
    all_to_all x1, blocking collectives, ctrl_product(): lax.all_to_all(tensor, 'ctrl', split_axis=0, concat_axis=1, tiled=True)  27.2 us
  transfers between devices with their start and end apart: 6, of which 4 were waited for; matrix products, arithmetic and copies ran while one was open for 3% of the time, Pallas kernels for 2%

profile of v1, /device:TPU:1, one launch (start us, length us, event | category | flops | bytes accessed | tf_op | source)
XLA Modules:
  0.0 532.9 jit_solution(8094134377324984506)
XLA Ops:
  8.7 3.2 copy.79
  11.9 8.7 %all-to-all-start = ((bf16[32,48,256]{2,1,0:T(8,128)(2,1)}), bf16[32,48,256]{2,1,0:T(8,128)(2,1)S(1)}, u32[]{:S(2)}, u32[]{:S(2)}) async-start(bf16[32,48,256]{2,1,0:T(8,128)(2,1)} %bitcast.83), calls=%async_computation | async-start | bytes 1572864 | tf_op jit(solution)/shard_map/all_to_all | solution.py:280
  21.3 18.9 %all-to-all-done = bf16[32,48,256]{2,1,0:T(8,128)(2,1)S(1)} async-done(((bf16[32,48,256]{2,1,0:T(8,128)(2,1)}), bf16[32,48,256]{2,1,0:T(8,128)(2,1)S(1)}, u32[]{:S(2)}, u32[]{:S(2)}) %all-to-all-start) | async-done | bytes 786464 | tf_op jit(solution)/shard_map/all_to_all | solution.py:280
  40.3 60.9 %all-gather.4.cloned.1.call-done = bf16[768,768]{1,0:T(8,128)(2,1)} async-done(((bf16[24,768]{1,0:T(8,128)(2,1)}), bf16[768,768]{1,0:T(8,128)(2,1)}) %all-gather.4.cloned.1.call-update) | async-done | bytes 1179664 | tf_op jit(solution)/shard_map/all_gather | solution.py:298
  101.2 2.1 fusion.5
  104.1 28.8 %all_to_all.130 = bf16[2,768,256]{2,0,1:T(2,128)(2,1)S(1)} all-to-all(bf16[2,768,256]{2,0,1:T(2,128)(2,1)S(1)} %copy.50), channel_id=1, replica_groups=mesh['ctrl'=16,'shelf'=32] {'ctrl'}, dimensions={1} | all-to-all | bytes 1572864 | tf_op jit(solution)/shard_map/all_to_all | solution.py:284
  135.8 7.6 %all-to-all-start.2 = ((bf16[32,32,384]{2,0,1:T(8,128)(2,1)}), bf16[32,32,384]{2,0,1:T(8,128)(2,1)S(1)}, u32[]{:S(2)}, u32[]{:S(2)}) async-start(bf16[32,32,384]{2,0,1:T(8,128)(2,1)} %copy.53), calls=%async_computation.2 | async-start | bytes 1572864 | tf_op jit(solution)/shard_map/all_to_all | solution.py:289
  143.4 46.6 %all-gather.6.cloned.1.call-done = bf16[1024,1024]{1,0:T(8,128)(2,1)} async-done(((bf16[32,1024]{1,0:T(8,128)(2,1)}), bf16[1024,1024]{1,0:T(8,128)(2,1)}) %all-gather.6.cloned.1.call-update) | async-done | bytes 2097168 | tf_op jit(solution)/shard_map/all_gather | solution.py:299
  190.0 2.6 fusion.3
  193.7 5.6 %all-to-all-start.3 = ((bf16[32,32,384]{2,1,0:T(8,128)(2,1)}), bf16[32,32,384]{2,1,0:T(8,128)(2,1)S(1)}, u32[]{:S(2)}, u32[]{:S(2)}) async-start(bf16[32,32,384]{2,1,0:T(8,128)(2,1)} %bitcast.89), calls=%async_computation.3 | async-start | bytes 1572864 | tf_op jit(solution)/shard_map/all_to_all | solution.py:293
  205.3 16.6 %all-to-all-done.3 = bf16[32,32,384]{2,1,0:T(8,128)(2,1)S(1)} async-done(((bf16[32,32,384]{2,1,0:T(8,128)(2,1)}), bf16[32,32,384]{2,1,0:T(8,128)(2,1)S(1)}, u32[]{:S(2)}, u32[]{:S(2)}) %all-to-all-start.3) | async-done | bytes 786464 | tf_op jit(solution)/shard_map/all_to_all | solution.py:293
  222.2 2.1 copy.55
  224.2 2.7 div.41
  226.9 2.9 fusion.20
  229.8 27.2 %all_to_all.131 = bf16[32,48,256]{2,1,0:T(8,128)(2,1)S(1)} all-to-all(bf16[32,48,256]{2,1,0:T(8,128)(2,1)S(1)} %fusion.20), channel_id=1, replica_groups=mesh['ctrl'=16,'shelf'=32] {'ctrl'}, dimensions={0} | all-to-all | bytes 1572864 | tf_op jit(solution)/shard_map/all_to_all | solution.py:280
  257.1 1.7 fusion.6
  258.8 2.3 copy.58
  261.1 24.4 %all_to_all.132 = bf16[2,768,256]{2,0,1:T(2,128)(2,1)S(1)} all-to-all(bf16[2,768,256]{2,0,1:T(2,128)(2,1)S(1)} %copy.58), channel_id=1, replica_groups=mesh['ctrl'=16,'shelf'=32] {'ctrl'}, dimensions={1} | all-to-all | bytes 1572864 | tf_op jit(solution)/shard_map/all_to_all | solution.py:284
  288.8 32.4 %all_to_all.133 = bf16[32,32,384]{2,0,1:T(8,128)(2,1)S(1)} all-to-all(bf16[32,32,384]{2,0,1:T(8,128)(2,1)S(1)} %copy.61), channel_id=1, replica_groups=mesh['ctrl'=16,'shelf'=32] {'shelf'}, dimensions={1} | all-to-all | bytes 1572864 | tf_op jit(solution)/shard_map/all_to_all | solution.py:289
  323.3 5.8 %all-to-all-start.7 = ((bf16[32,32,384]{2,1,0:T(8,128)(2,1)}), bf16[32,32,384]{2,1,0:T(8,128)(2,1)}, u32[]{:S(2)}, u32[]{:S(2)}) async-start(bf16[32,32,384]{2,1,0:T(8,128)(2,1)} %bitcast.90), calls=%async_computation.7 | async-start | bytes 1572864 | tf_op jit(solution)/shard_map/all_to_all | solution.py:293
  329.2 25.0 %all-gather = bf16[16,48,32]{1,2,0:T(8,128)(2,1)S(1)} all-gather(bf16[1,48,32]{1,2,0:T(8,128)(2,1)S(1)} %convert_bitcast_fusion.1), channel_id=1, replica_groups=mesh['ctrl'=16,'shelf'=32] {'ctrl'}, dimensions={0}, use_global_device_ids=true | all-gather | bytes 52224 | tf_op jit(solution)/shard_map/all_gather | solution.py:319
  354.4 48.8 %all_gather.17 = bf16[48,1024]{0,1:T(8,128)(2,1)S(1)} all-gather(bf16[48,32]{0,1:T(8,128)(2,1)S(1)} %convert_element_type.100), channel_id=1, replica_groups=mesh['ctrl'=16,'shelf'=32] {'shelf'}, dimensions={1}, use_global_device_ids=true | all-gather | bytes 101376 | tf_op jit(solution)/shard_map/all_gather | solution.py:320
  404.3 8.7 %member_product.1.first_ref = bf16[32,48,256]{2,1,0:T(8,128)(2,1)S(1)} custom-call(f32[32,768]{1,0:T(8,128)S(1)} %bitcast.84, bf16[48,768]{1,0:T(8,128)(2,1)S(1)} %constant_dynamic-slice_fusion.factor_ref), custom_call_target="tpu_custom_call" | custom-call | tf_op jit(solution)/shard_map/member_product/pallas_call | solution.py:189
  414.7 2.1 copy.63
  416.8 2.8 div.46
  419.6 4.3 multiply_reduce_fusion
  424.7 38.2 %all_gather.18 = f32[48,1024]{0,1:T(8,128)S(1)} all-gather(f32[48,32]{0,1:T(8,128)S(1)} %bitcast.99), channel_id=1, replica_groups=mesh['ctrl'=16,'shelf'=32] {'shelf'}, dimensions={1}, use_global_device_ids=true | all-gather | bytes 202752 | tf_op jit(solution)/shard_map/all_gather | solution.py:342
  463.7 15.4 %flow_product.1 = f32[256,256]{1,0:T(8,128)S(1)} custom-call(f32[48,1024]{1,0:T(8,128)S(1)} %convert_element_type.101.labels_ref, f32[48,1024]{1,0:T(8,128)S(1)} %copy.67.weight_ref, f32[32,1024]{1,0:T(8,128)S(1)} %convert_bitcast_fusion.factor_ref, bf16[32,48,256]{2,1,0:T(8,128)(2,1)S(1)} %member_product.1.first_ref), custom_call_target="tpu_custom_call" | custom-call | tf_op jit(solution)/shard_map/flow_product/pallas_call | solution.py:231
  479.9 32.2 %reduce_all.1 = (f32[256,256]{1,0:T(8,128)}, f32[8,128]{1,0:T(8,128)}) custom-call(f32[256,256]{1,0:T(8,128)} %select_add_fusion.part_ref, f32[8,128]{1,0:T(8,128)} %scatter.4.mass_ref), custom_call_target="tpu_custom_call" | custom-call | tf_op jit(solution)/shard_map/reduce_all/pallas_call | solution.py:148
  513.7 6.8 %balance.1 = f32[8,256]{1,0:T(8,128)} custom-call(f32[256,256]{1,0:T(8,128)} %get-tuple-element.16.numer_ref, f32[256,256]{1,0:T(8,128)} %broadcast_in_dim.5.mass_ref), custom_call_target="tpu_custom_call" | custom-call | tf_op jit(solution)/shard_map/balance/pallas_call | solution.py:267
  521.7 2.0 fusion.2
  524.0 2.1 copy.68
  (71 shorter events, 25.3 us)
Async XLA Ops:
  7.2 94.0 %all-gather.4.cloned.1.call-start = ((), (), s32[]{:S(2)}) async-start(), calls=%async_computation.8 | async-start | bytes 1216512 | tf_op jit(solution)/shard_map/all_gather | solution.py:298
  8.7 11.9 %copy-start.6 = (f32[32,1024]{1,0:T(8,128)S(1)}, f32[32,1024]{1,0:T(8,128)}, u32[]{:S(2)}) copy-start(f32[32,1024]{1,0:T(8,128)} %param.9) | copy-start | bytes 393220
  11.9 28.3 %all-to-all-start = ((bf16[32,48,256]{2,1,0:T(8,128)(2,1)}), bf16[32,48,256]{2,1,0:T(8,128)(2,1)S(1)}, u32[]{:S(2)}, u32[]{:S(2)}) async-start(bf16[32,48,256]{2,1,0:T(8,128)(2,1)} %bitcast.83), calls=%async_computation | async-start | bytes 1572864 | tf_op jit(solution)/shard_map/all_to_all | solution.py:280
  20.6 169.4 %all-gather.6.cloned.1.call-start = ((), (), s32[]{:S(2)}) async-start(), calls=%async_computation.9 | async-start | bytes 2162688 | tf_op jit(solution)/shard_map/all_gather | solution.py:299
  132.9 1.0 copy-start.3
  135.8 54.2 %all-to-all-start.2 = ((bf16[32,32,384]{2,0,1:T(8,128)(2,1)}), bf16[32,32,384]{2,0,1:T(8,128)(2,1)S(1)}, u32[]{:S(2)}, u32[]{:S(2)}) async-start(bf16[32,32,384]{2,0,1:T(8,128)(2,1)} %copy.53), calls=%async_computation.2 | async-start | bytes 1572864 | tf_op jit(solution)/shard_map/all_to_all | solution.py:289
  193.7 8.5 %copy-start = (bf16[1024,1024]{1,0:T(8,128)(2,1)S(1)}, bf16[1024,1024]{1,0:T(8,128)(2,1)}, u32[]{:S(2)}) copy-start(bf16[1024,1024]{1,0:T(8,128)(2,1)} %all-gather.6.cloned.1.call-done) | copy-start | bytes 6291460
  193.7 28.2 %all-to-all-start.3 = ((bf16[32,32,384]{2,1,0:T(8,128)(2,1)}), bf16[32,32,384]{2,1,0:T(8,128)(2,1)S(1)}, u32[]{:S(2)}, u32[]{:S(2)}) async-start(bf16[32,32,384]{2,1,0:T(8,128)(2,1)} %bitcast.89), calls=%async_computation.3 | async-start | bytes 1572864 | tf_op jit(solution)/shard_map/all_to_all | solution.py:293
  229.8 27.3 %copy-start.4 = (bf16[768,768]{1,0:T(8,128)(2,1)S(1)}, bf16[768,768]{1,0:T(8,128)(2,1)}, u32[]{:S(2)}) copy-start(bf16[768,768]{1,0:T(8,128)(2,1)} %all-gather.4.cloned.1.call-done) | copy-start | bytes 3538948
  322.2 6.9 %copy-start.5 = (s32[48,32]{0,1:T(8,128)S(1)}, s32[48,32]{0,1:T(8,128)}, u32[]{:S(2)}) copy-start(s32[48,32]{0,1:T(8,128)} %param.11) | copy-start | bytes 18436
  323.3 90.0 %all-to-all-start.7 = ((bf16[32,32,384]{2,1,0:T(8,128)(2,1)}), bf16[32,32,384]{2,1,0:T(8,128)(2,1)}, u32[]{:S(2)}, u32[]{:S(2)}) async-start(bf16[32,32,384]{2,1,0:T(8,128)(2,1)} %bitcast.90), calls=%async_computation.7 | async-start | bytes 1572864 | tf_op jit(solution)/shard_map/all_to_all | solution.py:293
  416.7 2.8 copy-start.1
  479.1 44.6 %copy-start.2 = (f32[32,48,256]{2,1,0:T(8,128)S(1)}, f32[32,48,256]{2,1,0:T(8,128)}, u32[]{:S(2)}) copy-start(f32[32,48,256]{2,1,0:T(8,128)} %get-tuple-element.27) | copy-start | bytes 4718596
Sparse Core Ops, SparseCore 0:
  11.3 89.8 all-gather.3
  104.5 85.3 all-gather.5

commit v2 on v1

--- a/solution.py
+++ b/solution.py
@@ -274,6 +274,224 @@
     )(numer, mass)[0]
 
 
+def spread_small(own, wide, stages, send_sem, recv_sem):
+    (outer_me, outer_size, outer_peer), (inner_me, inner_size, inner_peer) = stages
+
+    def stage(which, me, size, peer, piece):
+        def copy(step):
+            return pltpu.make_async_remote_copy(
+                src_ref=piece,
+                dst_ref=piece,
+                send_sem=send_sem.at[which, step],
+                recv_sem=recv_sem.at[which, step],
+                device_id=peer((me + step) % size),
+                device_id_type=MESH,
+            )
+
+        def start(step, carry):
+            copy(step).start()
+            return carry
+
+        def finish(step, carry):
+            copy(step).wait()
+            return carry
+
+        return start, finish, size
+
+    wide[inner_me, outer_me] = own
+    first = stage(0, outer_me, outer_size, outer_peer, wide.at[inner_me, outer_me])
+    second = stage(1, inner_me, inner_size, inner_peer, wide.at[inner_me])
+    return first, second
+
+
+def run_loop(part):
+    start, finish, size = part
+    lax.fori_loop(1, size, start, 0)
+    lax.fori_loop(1, size, finish, 0)
+
+
+def greet_each(peers):
+    barrier = pltpu.get_barrier_semaphore()
+    count = 0
+    for me, size, peer in peers:
+
+        def signal(step, carry, me=me, size=size, peer=peer):
+            pl.semaphore_signal(
+                barrier, inc=1, device_id=peer((me + step) % size), device_id_type=MESH
+            )
+            return carry
+
+        lax.fori_loop(1, size, signal, 0)
+        count += size - 1
+    pl.semaphore_wait(barrier, count)
+
+
+def shelf_stages():
+    ctrl = lax.axis_index("ctrl")
+    shelf = lax.axis_index("shelf")
+    return (
+        (shelf // 4, 8, lambda m: (ctrl, m * 4 + shelf % 4)),
+        (shelf % 4, 4, lambda m: (ctrl, shelf - shelf % 4 + m)),
+    )
+
+
+def ctrl_stages():
+    ctrl = lax.axis_index("ctrl")
+    shelf = lax.axis_index("shelf")
+    return (
+        (ctrl // 2, 8, lambda m: (m * 2 + ctrl % 2, shelf)),
+        (ctrl % 2, 2, lambda m: (ctrl - ctrl % 2 + m, shelf)),
+    )
+
+
+def weight_kernel(own_ref, wide_ref, send_sem, recv_sem):
+    stages = shelf_stages()
+    greet_each(stages)
+    first, second = spread_small(own_ref[...], wide_ref, stages, send_sem, recv_sem)
+    run_loop(first)
+    run_loop(second)
+
+
+def gather_weight(own):
+    return pl.pallas_call(
+        weight_kernel,
+        out_shape=jax.ShapeDtypeStruct((4, 8, 16, 128), jnp.float32),
+        in_specs=[pl.BlockSpec(memory_space=VMEM)],
+        out_specs=pl.BlockSpec(memory_space=VMEM),
+        scratch_shapes=[pltpu.SemaphoreType.DMA((2, 8)), pltpu.SemaphoreType.DMA((2, 8))],
+        compiler_params=pltpu.CompilerParams(collective_id=2, has_side_effects=True),
+        name="gather_weight",
+    )(own)
+
+
+def rows_kernel(
+    ctrl_ref, shelf_ref, label_ref, ctrl_all, shelf_all, by_shelf, by_ctrl,
+    swap_send, swap_recv, ring_send, ring_recv, pair_send, pair_recv,
+    send_a, recv_a, send_b, recv_b,
+):
+    ctrl = lax.axis_index("ctrl")
+    shelf = lax.axis_index("shelf")
+    deep, side, core = shelf // 4, (shelf // 2) % 2, shelf % 2
+    stages_a, stages_b = shelf_stages(), ctrl_stages()
+    greet_each(stages_a + stages_b)
+
+    wides = (ctrl_all, shelf_all)
+    ctrl_all[deep, side, core] = ctrl_ref[...]
+    shelf_all[deep, side, core] = shelf_ref[...]
+
+    def remote(piece, send_sem, recv_sem, target):
+        return pltpu.make_async_remote_copy(
+            src_ref=piece, dst_ref=piece, send_sem=send_sem, recv_sem=recv_sem,
+            device_id=(ctrl, target), device_id_type=MESH,
+        )
+
+    across = shelf + 2 - 4 * side
+    swaps = [
+        remote(wide.at[deep, side, core], swap_send.at[n], swap_recv.at[n], across)
+        for n, wide in enumerate(wides)
+    ]
+    for swap in swaps:
+        swap.start()
+    label_a = spread_small(label_ref[...], by_shelf, stages_a, send_a, recv_a)
+    label_b = spread_small(label_ref[...], by_ctrl, stages_b, send_b, recv_b)
+    run_loop(label_a[0])
+    run_loop(label_b[0])
+    for swap in swaps:
+        swap.wait()
+
+    right = ((deep + 1) % 8) * 4 + shelf % 4
+    left = ((deep + 7) % 8) * 4 + shelf % 4
+    sibling = shelf + 1 - 2 * core
+
+    def pair(n, block):
+        return remote(wides[n].at[block, :, core], pair_send.at[n, block], pair_recv.at[n, block], sibling)
+
+    def hop(n, way, count):
+        block = (deep + 8 - count + 1) % 8 if way == 0 else (deep + count - 1) % 8
+        return remote(
+            wides[n].at[block, :, core],
+            ring_send.at[n, way, count - 1],
+            ring_recv.at[n, way, count - 1],
+            right if way == 0 else left,
+        )
+
+    def used(n, way, count):
+        return count < 4 or n == way
+
+    for n in range(2):
+        for way in range(2):
+            hop(n, way, 1).start()
+        pair(n, deep).start()
+    for count in range(1, 5):
+        for n in range(2):
+            for way in range(2):
+                if not used(n, way, count):
+                    continue
+                hop(n, way, count).wait_recv()
+                if count < 4 and used(n, way, count + 1):
+                    hop(n, way, count + 1).start()
+                pair(n, (deep + 8 - count) % 8 if way == 0 else (deep + count) % 8).start()
+    run_loop(label_a[1])
+    run_loop(label_b[1])
+    for count in range(1, 5):
+        for n in range(2):
+            for way in range(2):
+                if used(n, way, count):
+                    hop(n, way, count).wait_send()
+    for block in range(8):
+        for n in range(2):
+            pltpu.make_async_remote_copy(
+                src_ref=wides[n].at[block, :, core],
+                dst_ref=wides[n].at[block, :, 1 - core],
+                send_sem=pair_send.at[n, block], recv_sem=pair_recv.at[n, block],
+                device_id=(ctrl, sibling), device_id_type=MESH,
+            ).wait()
+
+
+def gather_rows(ctrl_rows, shelf_rows, label_tile):
+    return pl.pallas_call(
+        rows_kernel,
+        out_shape=(
+            jax.ShapeDtypeStruct((8, 2, 2, *ctrl_rows.shape), jnp.bfloat16),
+            jax.ShapeDtypeStruct((8, 2, 2, *shelf_rows.shape), jnp.bfloat16),
+            jax.ShapeDtypeStruct((4, 8, 16, 128), jnp.float32),
+            jax.ShapeDtypeStruct((2, 8, 16, 128), jnp.float32),
+        ),
+        in_specs=[pl.BlockSpec(memory_space=VMEM)] * 3,
+        out_specs=tuple([pl.BlockSpec(memory_space=VMEM)] * 4),
+        scratch_shapes=[
+            pltpu.SemaphoreType.DMA((2,)),
+            pltpu.SemaphoreType.DMA((2,)),
+            pltpu.SemaphoreType.DMA((2, 2, 4)),
+            pltpu.SemaphoreType.DMA((2, 2, 4)),
+            pltpu.SemaphoreType.DMA((2, 8)),
+            pltpu.SemaphoreType.DMA((2, 8)),
+            pltpu.SemaphoreType.DMA((2, 8)),
+            pltpu.SemaphoreType.DMA((2, 8)),
+            pltpu.SemaphoreType.DMA((2, 8)),
+            pltpu.SemaphoreType.DMA((2, 8)),
+        ],
+        compiler_params=pltpu.CompilerParams(
+            collective_id=3, has_side_effects=True, vmem_limit_bytes=32 << 20
+        ),
+        name="gather_rows",
+    )(ctrl_rows, shelf_rows, label_tile)
+
+
+def as_tile(values):
+    return jnp.pad(values.reshape(12, 128), ((0, 4), (0, 0)))
+
+
+def shelf_wide(tiles):
+    kept = tiles[:, :, 0:12].reshape(4, 8, 48, 32)
+    return jnp.transpose(kept, (2, 1, 0, 3)).reshape(48, SHELF)
+
+
+def ctrl_wide(tiles):
+    kept = tiles[:, :, 0:12].reshape(2, 8, 48, 32)
+    return jnp.transpose(kept, (3, 1, 0, 2)).reshape(32, CTRL)
+
+
 def ctrl_product(tensor, factor, pattern):
     result = jnp.einsum(
         pattern,
@@ -295,8 +513,15 @@
 
 
 def local(prob, ctrl_rates, shelf_rates, disk_rates, labels):
-    ctrl_bf = lax.all_gather(ctrl_rates.astype(jnp.bfloat16), "shelf", axis=0, tiled=True)
-    shelf_bf = lax.all_gather(shelf_rates.astype(jnp.bfloat16), "shelf", axis=0, tiled=True)
+    ctrl_all, shelf_all, by_shelf, by_ctrl = gather_rows(
+        ctrl_rates.astype(jnp.bfloat16),
+        shelf_rates.astype(jnp.bfloat16),
+        as_tile(labels.astype(jnp.float32)),
+    )
+    ctrl_bf = ctrl_all.reshape(CTRL, CTRL)
+    shelf_bf = shelf_all.reshape(SHELF, SHELF)
+    shelf_labels = shelf_wide(by_shelf)
+    ctrl_labels = ctrl_wide(by_ctrl)
     disk_bf = disk_rates.astype(jnp.bfloat16)
     ctrl_out = jnp.sum(ctrl_bf.astype(jnp.float32), axis=1)
     shelf_out = jnp.sum(shelf_bf.astype(jnp.float32), axis=1)
@@ -315,10 +540,6 @@
         * disk_out[None, None, :]
         / uniform_rate
     )
-    label_f = labels.astype(jnp.bfloat16)
-    ctrl_labels = lax.all_gather(label_f.T, "ctrl", axis=1, tiled=True).astype(jnp.float32)
-    shelf_labels = lax.all_gather(label_f, "shelf", axis=1, tiled=True).astype(jnp.float32)
-
     iterate = jnp.transpose(prob, (1, 0, 2))
     for repeat in range(STEPS):
         rounded = iterate.astype(jnp.bfloat16)
@@ -339,7 +560,7 @@
     pair_mass = jnp.sum(iterate, axis=2)
     pair_kept = jnp.sum(iterate * retain, axis=2)
     weighted = jnp.sum(iterate * disk_out, axis=2)
-    shelf_weight = lax.all_gather(weighted.T, "shelf", axis=1, tiled=True)
+    shelf_weight = shelf_wide(gather_weight(as_tile(weighted.T)))
     part = flow_product(shelf_labels, shelf_weight, shelf_columns, first) / uniform_rate
     pair_count = shelf_rows * ctrl_rows
     own_labels = labels.T

time: 534 us -> 392 us (0.73)
  waiting for transfers between devices: 143 us -> 21.2 us
  blocking collectives: 225 us -> 137 us
  Pallas kernels: 63.1 us -> 140 us
  between operations: 16.3 us -> 2.88 us
  local copies, waits for them, and re-layouts: 30 us -> 41.4 us
  starting transfers between devices: 27.7 us -> 20.2 us
    all_gather x3 -> x0, blocking collectives: 112 us -> none  [the longest x1 48.8 us: local(): lax.all_gather(label_f, 'shelf', axis=1, tiled=True).astype(jnp.float32)]
    all_gather x2 -> x0, waiting for transfers between devices: 107 us -> none  [the longest x1 60.9 us: local(): lax.all_gather(ctrl_rates.astype(jnp.bfloat16), 'shelf', axis=0, tiled=True)]
    pallas_call x0 -> x2, Pallas kernels: none -> 78.4 us  [the longest x1 61.5 us: gather_rows(): pl.pallas_call(rows_kernel, out_shape=(jax.ShapeDtypeStruct((8, 2, 2, *ct...]
    all_to_all x1 -> x2, blocking collectives: 32.4 us -> 63.3 us  [shelf_product(): lax.all_to_all(flattened, 'shelf', split_axis=1, concat_axis=0, tiled=True)]
    all_to_all x1, waiting for transfers between devices: 18.9 us -> 0.01 us  [ctrl_product(): lax.all_to_all(tensor, 'ctrl', split_axis=0, concat_axis=1, tiled=True)]
    all_to_all x1 -> x0, starting transfers between devices: 7.59 us -> none  [shelf_product(): lax.all_to_all(flattened, 'shelf', split_axis=1, concat_axis=0, tiled=True)]
  transfers between devices with their start and end apart: 6 -> 3, of which waited for: 4 -> 2; matrix products, arithmetic and copies ran while one was open for 3% -> 3% of each run, Pallas kernels for 2% -> 18%
where the time goes in v2:
time: 392 us; the launch traced here: 391 us
  Pallas kernels  140 us (36%)
  blocking collectives  137 us (35%)
  local copies, waits for them, and re-layouts  41.4 us (11%)
  waiting for transfers between devices  21.2 us (5%)
  starting transfers between devices  20.2 us (5%)
  other arithmetic  16.6 us (4%)
  matrix products  11.1 us (3%)
    all_to_all x2, blocking collectives, shelf_product(): lax.all_to_all(flattened, 'shelf', split_axis=1, concat_axis=0, tiled=True)  63.3 us
    pallas_call x1, Pallas kernels, gather_rows(): pl.pallas_call(rows_kernel, out_shape=(jax.ShapeDtypeStruct((8, 2, 2, *ct...  61.5 us
    all_to_all x2, blocking collectives, ctrl_product(): lax.all_to_all(result, 'ctrl', split_axis=1, concat_axis=0, tiled=True)  49.5 us
    pallas_call x1, Pallas kernels, reduce_all(): pl.pallas_call(reduce_kernel, out_shape=(jax.ShapeDtypeStruct((NBLK, NBLK...  31 us
    all_to_all x1, blocking collectives, ctrl_product(): lax.all_to_all(tensor, 'ctrl', split_axis=0, concat_axis=1, tiled=True)  24.5 us
    all_to_all x2, waiting for transfers between devices, shelf_product(): lax.all_to_all(result, 'shelf', split_axis=0, concat_axis=1, tiled=True)  21.2 us
    pallas_call x1, Pallas kernels, gather_weight(): pl.pallas_call(weight_kernel, out_shape=jax.ShapeDtypeStruct((4, 8, 16, 1...  16.9 us
    pallas_call x1, Pallas kernels, flow_product(): pl.pallas_call(flow_kernel, out_shape=jax.ShapeDtypeStruct((NBLK, NBLK),...  15.4 us
  transfers between devices with their start and end apart: 3, of which 2 were waited for; matrix products, arithmetic and copies ran while one was open for 3% of the time, Pallas kernels for 18%

profile of v2, /device:TPU:1, one launch (start us, length us, event | category | flops | bytes accessed | tf_op | source)
XLA Modules:
  0.0 391.0 jit_solution(1791695208320539438)
XLA Ops:
  0.7 3.2 copy.144
  3.8 8.7 %all-to-all-start = ((bf16[32,48,256]{2,1,0:T(8,128)(2,1)}), bf16[32,48,256]{2,1,0:T(8,128)(2,1)}, u32[]{:S(2)}, u32[]{:S(2)}) async-start(bf16[32,48,256]{2,1,0:T(8,128)(2,1)} %bitcast.81), calls=%async_computation | async-start | bytes 1572864 | tf_op jit(solution)/shard_map/all_to_all | solution.py:498
  12.8 61.5 %gather_rows.1 = (bf16[8,2,2,24,768]{4,3,2,1,0:T(8,128)(2,1)S(1)}, bf16[8,2,2,32,1024]{4,3,2,1,0:T(8,128)(2,1)S(1)}, f32[4,8,16,128]{3,2,1,0:T(8,128)S(1)}, f32[2,8,16,128]{3,2,1,0:T(8,128)S(1)}) custom-call(bf16[24,768]{1,0:T(8,128)(2,1)S(1)} %convert_element_type.73.ctrl_ref, bf16[32,1024]{1,0:T(8,128)(2,1)S(1)} %convert_element_type.74.shelf_ref, ...), custom_call_target="tpu_custom_call" | custom-call | tf_op jit(solution)/shard_map/gather_rows/pallas_call | solution.py:452
  77.8 24.8 %all_to_all.130 = bf16[2,768,256]{2,0,1:T(2,128)(2,1)S(1)} all-to-all(bf16[2,768,256]{2,0,1:T(2,128)(2,1)S(1)} %copy.107), channel_id=1, replica_groups=mesh['ctrl'=16,'shelf'=32] {'ctrl'}, dimensions={1} | all-to-all | bytes 1572864 | tf_op jit(solution)/shard_map/all_to_all | solution.py:502
  104.8 2.3 all_to_all.103
  107.0 1.4 copy.110
  108.4 32.3 %all_to_all.131 = bf16[32,32,384]{2,0,1:T(8,128)(2,1)S(1)} all-to-all(bf16[32,32,384]{2,0,1:T(8,128)(2,1)S(1)} %copy.110), channel_id=1, replica_groups=mesh['ctrl'=16,'shelf'=32] {'shelf'}, dimensions={1} | all-to-all | bytes 1572864 | tf_op jit(solution)/shard_map/all_to_all | solution.py:507
  140.7 2.2 convolution_convert_fusion.5
  142.9 5.8 %all-to-all-start.3 = ((bf16[32,32,384]{2,1,0:T(8,128)(2,1)}), bf16[32,32,384]{2,1,0:T(8,128)(2,1)}, u32[]{:S(2)}, u32[]{:S(2)}) async-start(bf16[32,32,384]{2,1,0:T(8,128)(2,1)} %bitcast.104), calls=%async_computation.3 | async-start | bytes 1572864 | tf_op jit(solution)/shard_map/all_to_all | solution.py:511
  158.3 13.0 %all-to-all-done.3 = bf16[32,32,384]{2,1,0:T(8,128)(2,1)} async-done(((bf16[32,32,384]{2,1,0:T(8,128)(2,1)}), bf16[32,32,384]{2,1,0:T(8,128)(2,1)}, u32[]{:S(2)}, u32[]{:S(2)}) %all-to-all-start.3) | async-done | bytes 786464 | tf_op jit(solution)/shard_map/all_to_all | solution.py:511
  172.6 2.1 copy.113
  174.7 2.7 div.41
  177.4 2.9 fusion.16
  180.3 24.5 %all_to_all.132 = bf16[32,48,256]{2,1,0:T(8,128)(2,1)S(1)} all-to-all(bf16[32,48,256]{2,1,0:T(8,128)(2,1)S(1)} %fusion.16), channel_id=1, replica_groups=mesh['ctrl'=16,'shelf'=32] {'ctrl'}, dimensions={0} | all-to-all | bytes 1572864 | tf_op jit(solution)/shard_map/all_to_all | solution.py:498
  206.4 24.7 %all_to_all.133 = bf16[2,768,256]{2,0,1:T(2,128)(2,1)S(1)} all-to-all(bf16[2,768,256]{2,0,1:T(2,128)(2,1)S(1)} %copy.116), channel_id=1, replica_groups=mesh['ctrl'=16,'shelf'=32] {'ctrl'}, dimensions={1} | all-to-all | bytes 1572864 | tf_op jit(solution)/shard_map/all_to_all | solution.py:502
  233.4 2.3 all_to_all.116
  235.7 1.4 copy.119
  237.1 31.0 %all_to_all.134 = bf16[32,32,384]{2,0,1:T(8,128)(2,1)S(1)} all-to-all(bf16[32,32,384]{2,0,1:T(8,128)(2,1)S(1)} %copy.119), channel_id=1, replica_groups=mesh['ctrl'=16,'shelf'=32] {'shelf'}, dimensions={1} | all-to-all | bytes 1572864 | tf_op jit(solution)/shard_map/all_to_all | solution.py:507
  268.1 2.2 convolution_convert_fusion.4
  270.2 5.8 %all-to-all-start.7 = ((bf16[32,32,384]{2,1,0:T(8,128)(2,1)}), bf16[32,32,384]{2,1,0:T(8,128)(2,1)}, u32[]{:S(2)}, u32[]{:S(2)}) async-start(bf16[32,32,384]{2,1,0:T(8,128)(2,1)} %bitcast.105), calls=%async_computation.7 | async-start | bytes 1572864 | tf_op jit(solution)/shard_map/all_to_all | solution.py:511
  276.0 1.4 eq.29
  281.7 8.7 %member_product.1.first_ref = bf16[32,48,256]{2,1,0:T(8,128)(2,1)S(1)} custom-call(f32[32,768]{1,0:T(8,128)S(1)} %reshape.164.labels_ref, bf16[48,768]{1,0:T(8,128)(2,1)S(1)} %constant_dynamic-slice_fusion.factor_ref), custom_call_target="tpu_custom_call" | custom-call | tf_op jit(solution)/shard_map/member_product/pallas_call | solution.py:189
  290.5 8.2 %all-to-all-done.7 = bf16[32,32,384]{2,1,0:T(8,128)(2,1)} async-done(((bf16[32,32,384]{2,1,0:T(8,128)(2,1)}), bf16[32,32,384]{2,1,0:T(8,128)(2,1)}, u32[]{:S(2)}, u32[]{:S(2)}) %all-to-all-start.7) | async-done | bytes 786464 | tf_op jit(solution)/shard_map/all_to_all | solution.py:511
  300.0 2.1 copy.120
  302.1 2.8 div.46
  304.9 4.3 %multiply_reduce_fusion = (f32[32,48]{1,0:T(8,128)S(1)}, f32[32,48]{1,0:T(8,128)S(1)}, f32[32,48]{1,0:T(8,128)S(1)}, f32[32,48,256]{2,1,0:T(8,128)}) fusion(f32[]{:T(128)S(6)} %mul.92, f32[256]{0:T(256)S(1)} %copy-done.10, f32[32,48]{1,0:T(8,128)S(1)} %broadcast_multiply_fusion, f32[32,48,256]{2,1,0:T(8,128)} %div.46, f32[32,48,256]{2,1,0:T(8,128)} %div.41, ...), kind=kLoop, calls=%fused_computation.9 | loop fusion | flops 4713984 | bytes 6317060 | tf_op jit(solution)/shard_map/reduce_sum | solution.py:561
  311.4 16.9 %gather_weight.1 = f32[4,8,16,128]{3,2,1,0:T(8,128)} custom-call(f32[16,128]{1,0:T(8,128)} %pad.11.own_ref), custom_call_target="tpu_custom_call" | custom-call | tf_op jit(solution)/shard_map/gather_weight/pallas_call | solution.py:356
  329.9 15.4 %flow_product.1 = f32[256,256]{1,0:T(8,128)S(1)} custom-call(f32[48,1024]{1,0:T(8,128)S(1)} %copy.126.labels_ref, f32[48,1024]{1,0:T(8,128)S(1)} %copy.127.weight_ref, f32[32,1024]{1,0:T(8,128)S(1)} %convert_bitcast_fusion.factor_ref, bf16[32,48,256]{2,1,0:T(8,128)(2,1)S(1)} %member_product.1.first_ref), custom_call_target="tpu_custom_call" | custom-call | tf_op jit(solution)/shard_map/flow_product/pallas_call | solution.py:231
  346.1 31.0 %reduce_all.1 = (f32[256,256]{1,0:T(8,128)}, f32[8,128]{1,0:T(8,128)}) custom-call(f32[256,256]{1,0:T(8,128)} %select_add_fusion.part_ref, f32[8,128]{1,0:T(8,128)} %scatter.4.mass_ref), custom_call_target="tpu_custom_call" | custom-call | tf_op jit(solution)/shard_map/reduce_all/pallas_call | solution.py:148
  378.6 6.8 %balance.1 = f32[8,256]{1,0:T(8,128)} custom-call(f32[256,256]{1,0:T(8,128)} %get-tuple-element.24.numer_ref, f32[256,256]{1,0:T(8,128)} %broadcast_in_dim.5.mass_ref), custom_call_target="tpu_custom_call" | custom-call | tf_op jit(solution)/shard_map/balance/pallas_call | solution.py:267
  386.7 2.0 fusion.2
  388.9 2.1 copy.128
  (82 shorter events, 31.9 us)
Async XLA Ops:
  0.6 11.9 %copy-start.7 = (s32[48,32]{0,1:T(8,128)S(1)}, s32[48,32]{0,1:T(8,128)}, u32[]{:S(2)}) copy-start(s32[48,32]{0,1:T(8,128)} %param.11) | copy-start | bytes 18436
  0.6 12.1 %copy-start.6 = (f32[24,768]{1,0:T(8,128)S(1)}, f32[24,768]{1,0:T(8,128)}, u32[]{:S(2)}) copy-start(f32[24,768]{1,0:T(8,128)} %param.8) | copy-start | bytes 221188
  0.7 12.1 %copy-start.5 = (f32[32,1024]{1,0:T(8,128)S(1)}, f32[32,1024]{1,0:T(8,128)}, u32[]{:S(2)}) copy-start(f32[32,1024]{1,0:T(8,128)} %param.9) | copy-start | bytes 393220
  3.8 71.1 %all-to-all-start = ((bf16[32,48,256]{2,1,0:T(8,128)(2,1)}), bf16[32,48,256]{2,1,0:T(8,128)(2,1)}, u32[]{:S(2)}, u32[]{:S(2)}) async-start(bf16[32,48,256]{2,1,0:T(8,128)(2,1)} %bitcast.81), calls=%async_computation | async-start | bytes 1572864 | tf_op jit(solution)/shard_map/all_to_all | solution.py:498
  74.3 0.6 copy-start
  102.6 1.0 copy-start.3
  142.9 28.4 %all-to-all-start.3 = ((bf16[32,32,384]{2,1,0:T(8,128)(2,1)}), bf16[32,32,384]{2,1,0:T(8,128)(2,1)}, u32[]{:S(2)}, u32[]{:S(2)}) async-start(bf16[32,32,384]{2,1,0:T(8,128)(2,1)} %bitcast.104), calls=%async_computation.3 | async-start | bytes 1572864 | tf_op jit(solution)/shard_map/all_to_all | solution.py:511
  153.0 3.8 copy-start.9
  231.2 1.0 copy-start.4
  270.2 28.4 %all-to-all-start.7 = ((bf16[32,32,384]{2,1,0:T(8,128)(2,1)}), bf16[32,32,384]{2,1,0:T(8,128)(2,1)}, u32[]{:S(2)}, u32[]{:S(2)}) async-start(bf16[32,32,384]{2,1,0:T(8,128)(2,1)} %bitcast.105), calls=%async_computation.7 | async-start | bytes 1572864 | tf_op jit(solution)/shard_map/all_to_all | solution.py:511
  302.0 2.8 copy-start.1
  302.0 2.8 copy-start.10
  304.9 4.5 %copy-start.11 = (s32[1536]{0:T(1024)S(1)}, s32[1536]{0:T(1024)}, u32[]{:S(2)}) copy-start(s32[1536]{0:T(1024)} %eq.29) | copy-start | bytes 18436
  329.9 56.7 %copy-start.8 = (s32[48,32]{0,1:T(8,128)S(1)}, s32[48,32]{0,1:T(8,128)}, u32[]{:S(2)}) copy-start(s32[48,32]{0,1:T(8,128)} %param.11) | copy-start | bytes 18436
  329.9 58.7 %copy-start.2 = (f32[32,48,256]{2,1,0:T(8,128)S(1)}, f32[32,48,256]{2,1,0:T(8,128)}, u32[]{:S(2)}) copy-start(f32[32,48,256]{2,1,0:T(8,128)} %get-tuple-element.39) | copy-start | bytes 4718596

commit v3 on v2

--- a/solution.py
+++ b/solution.py
@@ -492,24 +492,264 @@
     return jnp.transpose(kept, (3, 1, 0, 2)).reshape(32, CTRL)
 
 
-def ctrl_product(tensor, factor, pattern):
-    result = jnp.einsum(
-        pattern,
-        lax.all_to_all(tensor, "ctrl", split_axis=0, concat_axis=1, tiled=True),
-        factor,
-        preferred_element_type=jnp.float32,
+def steps_kernel(
+    prob_ref, ctrl_ref, shelf_ref, disk_ref, rate_ref, shelf_rate_ref, scale_ref, state_ref,
+    home_y, home_z, at_y, made_y, at_z, made_z, back_y, back_z,
+    send_sem, recv_sem,
+):
+    ctrl = lax.axis_index("ctrl")
+    shelf = lax.axis_index("shelf")
+    chip, core = shelf // 2, shelf % 2
+    ctrls, shelves = 16, 32
+    chips = shelves // 2
+    rows_c, rows_s = state_ref.shape[0], state_ref.shape[1]
+    per_y, per_z = rows_s // ctrls, rows_c // chips
+    lanes = 128
+
+    barrier = pltpu.get_barrier_semaphore()
+
+    def signal_y(step, carry):
+        target = ((ctrl + step) % ctrls, shelf)
+        pl.semaphore_signal(barrier, inc=1, device_id=target, device_id_type=MESH)
+        return carry
+
+    def signal_z(step, carry):
+        target = (ctrl, (shelf + step) % shelves)
+        pl.semaphore_signal(barrier, inc=1, device_id=target, device_id_type=MESH)
+        return carry
+
+    lax.fori_loop(1, ctrls, signal_y, 0)
+    lax.fori_loop(1, shelves, signal_z, 0)
+    state_ref[...] = prob_ref[...]
+
+    order = lax.broadcasted_iota(jnp.int32, (256, 256), 0)
+    other = lax.broadcasted_iota(jnp.int32, (256, 256), 1)
+    swap = jnp.where(
+        jnp.logical_and(order // 16 == other % 16, order % 16 == other // 16), 1.0, 0.0
     ).astype(jnp.bfloat16)
-    return lax.all_to_all(result, "ctrl", split_axis=1, concat_axis=0, tiled=True)
-
-
-def shelf_product(tensor, factor, pattern):
-    flattened = tensor.reshape(tensor.shape[0], tensor.shape[1] * tensor.shape[2])
-    regrouped = lax.all_to_all(flattened, "shelf", split_axis=1, concat_axis=0, tiled=True)
-    result = jnp.einsum(pattern, regrouped, factor, preferred_element_type=jnp.float32).astype(
-        jnp.bfloat16
-    )
-    returned = lax.all_to_all(result, "shelf", split_axis=0, concat_axis=1, tiled=True)
-    return returned.reshape(tensor.shape)
+    pl.semaphore_wait(barrier, ctrls - 1 + shelves - 1)
+
+    def swapped(block):
+        flat = jnp.dot(swap, block.reshape(256, lanes), preferred_element_type=jnp.float32)
+        return flat.astype(jnp.bfloat16).reshape(16, 16, lanes)
+
+    def exchange_rows(source, target):
+        first, second = source.shape[0], source.shape[1]
+        for p in range(0, first, 16):
+            for q in range(0, second, 16):
+                target[q : q + 16, p : p + 16, :] = swapped(source[p : p + 16, q : q + 16, :])
+
+    def part_c(ref, owner):
+        return ref.at[:, pl.ds(pl.multiple_of(owner * rows_c, 16), rows_c), :]
+
+    def part_s(ref, owner):
+        return ref.at[:, pl.ds(pl.multiple_of(owner * rows_s, 16), rows_s), :]
+
+    def remote(source, target, stream, mine, theirs, device):
+        return pltpu.make_async_remote_copy(
+            src_ref=source, dst_ref=target,
+            send_sem=send_sem.at[stream, theirs], recv_sem=recv_sem.at[stream, mine],
+            device_id=device, device_id_type=MESH,
+        )
+
+    def each(count, first, act):
+        def body(step, carry):
+            act((first + step) % count)
+            return carry
+
+        lax.fori_loop(1, count, body, 0)
+
+    def y_forward(half):
+        def act(peer):
+            remote(
+                home_y.at[half, pl.ds(peer * per_y, per_y)], part_c(at_y.at[half], ctrl),
+                4 * half, ctrl, peer, (peer, shelf),
+            ).start()
+
+        each(ctrls, ctrl, act)
+        part_c(at_y.at[half], ctrl)[...] = home_y[half, pl.ds(ctrl * per_y, per_y)]
+
+    def y_forward_wait(half):
+        def act(peer):
+            remote(
+                home_y.at[half, pl.ds(peer * per_y, per_y)], part_c(at_y.at[half], peer),
+                4 * half, peer, peer, (peer, shelf),
+            ).wait()
+
+        each(ctrls, ctrl, act)
+
+    def y_product(half):
+        both = jnp.concatenate([at_y[half, n] for n in range(per_y)], axis=1)
+        for m in range(0, ctrls * rows_c, 256):
+            made = jnp.dot(ctrl_ref[m : m + 256], both, preferred_element_type=jnp.float32)
+            for n in range(per_y):
+                made_y[half, n, m : m + 256, :] = made[:, n * lanes : (n + 1) * lanes].astype(
+                    jnp.bfloat16
+                )
+
+    def y_back(half):
+        def act(peer):
+            remote(
+                part_c(made_y.at[half], peer), back_y.at[half, pl.ds(ctrl * per_y, per_y)],
+                4 * half + 1, ctrl, peer, (peer, shelf),
+            ).start()
+
+        each(ctrls, ctrl, act)
+        back_y[half, pl.ds(ctrl * per_y, per_y)] = part_c(made_y.at[half], ctrl)[...]
+
+    def y_back_wait(half):
+        def act(peer):
+            remote(
+                part_c(made_y.at[half], peer), back_y.at[half, pl.ds(peer * per_y, per_y)],
+                4 * half + 1, peer, peer, (peer, shelf),
+            ).wait()
+
+        each(ctrls, ctrl, act)
+
+    def z_forward_copy(half, to):
+        return remote(
+            home_z.at[half, pl.ds(to * per_z, per_z)], part_s(at_z, shelf),
+            4 * half + 2, shelf, to, (ctrl, 2 * to + half),
+        )
+
+    def z_forward(half):
+        each(chips, chip, lambda to: z_forward_copy(half, to).start())
+
+        @pl.when(core != half)
+        def _():
+            z_forward_copy(half, chip).start()
+
+        @pl.when(core == half)
+        def _():
+            part_s(at_z, shelf)[...] = home_z[half, pl.ds(chip * per_z, per_z)]
+
+    def z_forward_sent(half):
+        each(chips, chip, lambda to: z_forward_copy(half, to).wait_send())
+
+        @pl.when(core != half)
+        def _():
+            z_forward_copy(half, chip).wait_send()
+
+    def z_middle(half):
+        @pl.when(core == half)
+        def _():
+            def arrived(peer):
+                remote(
+                    home_z.at[half, pl.ds(0, per_z)], part_s(at_z, peer),
+                    4 * half + 2, peer, 0, (ctrl, peer),
+                ).wait_recv()
+
+            each(shelves, shelf, arrived)
+            wide = jnp.concatenate([at_z[n] for n in range(per_z)], axis=1)
+            for m in range(0, shelves * rows_s, 256):
+                made = jnp.dot(shelf_ref[m : m + 256], wide, preferred_element_type=jnp.float32)
+                for n in range(per_z):
+                    made_z[n, m : m + 256, :] = made[:, n * lanes : (n + 1) * lanes].astype(
+                        jnp.bfloat16
+                    )
+
+            def act(peer):
+                remote(
+                    part_s(made_z, peer), back_z.at[half, pl.ds(chip * per_z, per_z)],
+                    4 * half + 3, chip, peer, (ctrl, peer),
+                ).start()
+
+            each(shelves, shelf, act)
+            back_z[half, pl.ds(chip * per_z, per_z)] = part_s(made_z, shelf)[...]
+
+    def z_back_from(half, source):
+        return remote(
+            part_s(made_z, shelf), back_z.at[half, pl.ds(source * per_z, per_z)],
+            4 * half + 3, source, 0, (ctrl, 2 * source + half),
+        )
+
+    def z_back_wait(half):
+        each(chips, chip, lambda source: z_back_from(half, source).wait_recv())
+
+        @pl.when(core != half)
+        def _():
+            z_back_from(half, chip).wait_recv()
+
+    def z_back_sent(half):
+        @pl.when(core == half)
+        def _():
+            def act(peer):
+                remote(
+                    part_s(made_z, peer), back_z.at[half, pl.ds(chip * per_z, per_z)],
+                    4 * half + 3, chip, peer, (ctrl, peer),
+                ).wait_send()
+
+            each(shelves, shelf, act)
+
+    def one_step(repeat, carry):
+        for p in range(0, rows_c, 16):
+            rounded = state_ref[p : p + 16].astype(jnp.bfloat16).reshape(16 * rows_s, 256)
+            made = jnp.dot(rounded, disk_ref[...], preferred_element_type=jnp.float32)
+            made = made.astype(jnp.bfloat16).reshape(16, rows_s, 256)
+            home_z[1, p : p + 16] = made[:, :, lanes:]
+            for q in range(0, rows_s, 16):
+                home_y[0, q : q + 16, p : p + 16, :] = swapped(made[:, q : q + 16, :lanes])
+        z_forward(1)
+        y_forward(0)
+        y_forward_wait(0)
+        y_product(0)
+        y_back(0)
+        z_middle(1)
+        y_back_wait(0)
+        exchange_rows(back_y.at[0], home_z.at[0])
+        z_forward(0)
+        z_back_wait(1)
+        exchange_rows(back_z.at[1], home_y.at[1])
+        y_forward(1)
+        z_middle(0)
+        y_forward_wait(1)
+        y_product(1)
+        y_back(1)
+        z_back_wait(0)
+        y_back_wait(1)
+        z_forward_sent(1)
+        exchange_rows(back_y.at[1], home_z.at[1])
+
+        def update(row, inner):
+            kept = 1.0 - rate_ref[pl.ds(row, 1), :] * shelf_rate_ref[...]
+            third = jnp.concatenate([back_z[0, row], home_z[1, row]], axis=1)
+            state_ref[row] = third.astype(jnp.float32) * scale_ref[...] + state_ref[row] * kept
+            return inner
+
+        lax.fori_loop(0, rows_c, update, 0)
+        z_forward_sent(0)
+        z_back_sent(0)
+        z_back_sent(1)
+        return carry
+
+    lax.fori_loop(0, STEPS, one_step, 0)
+
+
+def power_steps(prob, ctrl_t, shelf_t, disk_bf, rate, shelf_rate, scale):
+    rows_c, rows_s, _ = prob.shape
+    bf = jnp.bfloat16
+    return pl.pallas_call(
+        steps_kernel,
+        out_shape=jax.ShapeDtypeStruct(prob.shape, jnp.float32),
+        in_specs=[pl.BlockSpec(memory_space=VMEM)] * 7,
+        out_specs=pl.BlockSpec(memory_space=VMEM),
+        scratch_shapes=[
+            pltpu.VMEM((2, rows_s, rows_c, 128), bf),
+            pltpu.VMEM((2, rows_c, rows_s, 128), bf),
+            pltpu.VMEM((2, 2, CTRL, 128), bf),
+            pltpu.VMEM((2, 2, CTRL, 128), bf),
+            pltpu.VMEM((3, SHELF, 128), bf),
+            pltpu.VMEM((3, SHELF, 128), bf),
+            pltpu.VMEM((2, rows_s, rows_c, 128), bf),
+            pltpu.VMEM((2, rows_c, rows_s, 128), bf),
+            pltpu.SemaphoreType.DMA((8, 32)),
+            pltpu.SemaphoreType.DMA((8, 32)),
+        ],
+        compiler_params=pltpu.CompilerParams(
+            collective_id=4, has_side_effects=True, vmem_limit_bytes=48 << 20
+        ),
+        name="power_steps",
+    )(prob, ctrl_t, shelf_t, disk_bf, rate, shelf_rate, scale)
 
 
 def local(prob, ctrl_rates, shelf_rates, disk_rates, labels):
@@ -533,39 +773,30 @@
     shelf_at = lax.axis_index("shelf") * shelf_rows
     ctrl_loc = lax.dynamic_slice_in_dim(ctrl_out, ctrl_at, ctrl_rows)
     shelf_loc = lax.dynamic_slice_in_dim(shelf_out, shelf_at, shelf_rows)
-    retain = (
-        1.0
-        - ctrl_loc[None, :, None]
-        * shelf_loc[:, None, None]
-        * disk_out[None, None, :]
-        / uniform_rate
-    )
-    iterate = jnp.transpose(prob, (1, 0, 2))
-    for repeat in range(STEPS):
-        rounded = iterate.astype(jnp.bfloat16)
-        section_one = ctrl_product(rounded, ctrl_bf, "bac,ad->bdc")
-        section_two = jnp.dot(
-            section_one.reshape(shelf_rows * ctrl_rows, DISK),
-            disk_bf,
-            preferred_element_type=jnp.float32,
-        )
-        section_two = section_two.astype(jnp.bfloat16).reshape(section_one.shape)
-        section_three = shelf_product(section_two, shelf_bf, "bq,bd->dq")
-        iterate = section_three.astype(jnp.float32) / uniform_rate + iterate * retain
+    rate = ctrl_loc[:, None] * disk_out[None, :] / uniform_rate
+    shelf_rate = jnp.broadcast_to(shelf_loc[:, None], (shelf_rows, DISK))
+    iterate = power_steps(
+        prob,
+        ctrl_bf.T,
+        shelf_bf.T,
+        disk_bf,
+        rate,
+        shelf_rate,
+        jnp.full((1, DISK), 1.0, jnp.float32) / uniform_rate,
+    )
 
     first = member_product(ctrl_labels, lax.dynamic_slice_in_dim(ctrl_bf, ctrl_at, ctrl_rows))
     shelf_columns = lax.dynamic_slice_in_dim(shelf_bf, shelf_at, shelf_rows, axis=1)
     shelf_columns = shelf_columns.T.astype(jnp.float32)
 
     pair_mass = jnp.sum(iterate, axis=2)
-    pair_kept = jnp.sum(iterate * retain, axis=2)
     weighted = jnp.sum(iterate * disk_out, axis=2)
-    shelf_weight = shelf_wide(gather_weight(as_tile(weighted.T)))
+    pair_kept = pair_mass - weighted * (ctrl_loc[:, None] * shelf_loc[None, :] / uniform_rate)
+    shelf_weight = shelf_wide(gather_weight(as_tile(weighted)))
     part = flow_product(shelf_labels, shelf_weight, shelf_columns, first) / uniform_rate
     pair_count = shelf_rows * ctrl_rows
-    own_labels = labels.T
     blocks = jnp.arange(NBLK, dtype=jnp.int32)
-    member_table = (own_labels.reshape(pair_count)[:, None] == blocks[None, :]).astype(
+    member_table = (labels.reshape(pair_count)[:, None] == blocks[None, :]).astype(
         jnp.float32
     )
     terms = jnp.dot(
@@ -581,10 +812,9 @@
     balance = balance_of(numer, jnp.broadcast_to(block_mass[:, None], (NBLK, NBLK)))
     ratio_share = balance / block_mass
     pair_share = jnp.dot(member_table, ratio_share, precision=HIGHEST).reshape(
-        shelf_rows, ctrl_rows
-    )
-    scaled = iterate * pair_share[:, :, None] * float(CTRL * SHELF * DISK)
-    refined = jnp.transpose(scaled, (1, 0, 2))
+        ctrl_rows, shelf_rows
+    )
+    refined = iterate * pair_share[:, :, None] * float(CTRL * SHELF * DISK)
     coarse = balance * NBLK
     return (refined, coarse)
 

time: 392 us -> 307 us (0.78)
  blocking collectives: 137 us -> 0 us
  Pallas kernels: 140 us -> 257 us
  waiting for transfers between devices: 21.2 us -> 0 us
  starting transfers between devices: 20.2 us -> 0 us
  local copies, waits for them, and re-layouts: 41.4 us -> 30 us
  matrix products: 11.1 us -> 3.04 us
    all_to_all x5 -> x0, blocking collectives: 137 us -> none  [the longest x2 63.3 us: shelf_product(): lax.all_to_all(flattened, 'shelf', split_axis=1, concat_axis=0, tiled=True)]
    pallas_call x0 -> x1, Pallas kernels: none -> 122 us  [power_steps(): pl.pallas_call(steps_kernel, out_shape=jax.ShapeDtypeStruct(prob.shape, j...]
    all_to_all x3 -> x0, waiting for transfers between devices: 21.2 us -> none  [the longest x2 21.2 us: shelf_product(): lax.all_to_all(result, 'shelf', split_axis=0, concat_axis=1, tiled=True)]
    all_to_all x3 -> x0, starting transfers between devices: 20.2 us -> none  [the longest x2 11.5 us: shelf_product(): lax.all_to_all(result, 'shelf', split_axis=0, concat_axis=1, tiled=True)]
    div x4 -> x0, local copies, waits for them, and re-layouts: 9.64 us -> none  [local(): section_three.astype(jnp.float32) / uniform_rate + iterate * retain]
    all_to_all x10 -> x0, local copies, waits for them, and re-layouts: 8.91 us -> none  [the longest x4 7.32 us: shelf_product(): lax.all_to_all(flattened, 'shelf', split_axis=1, concat_axis=0, tiled=True)]
    dot_general x6 -> x0, matrix products: 8.43 us -> none  [the longest x2 4.33 us: shelf_product(): jnp.einsum(pattern, regrouped, factor, preferred_element_type=jnp.float32)]
    pallas_call x1, Pallas kernels: 61.5 us -> 55.2 us  [gather_rows(): pl.pallas_call(rows_kernel, out_shape=(jax.ShapeDtypeStruct((8, 2, 2, *ct...]
  transfers between devices with their start and end apart: 3 -> 0, of which waited for: 2 -> 0; matrix products, arithmetic and copies ran while one was open for 3% -> 0% of each run, Pallas kernels for 18% -> 0%
where the time goes in v3:
time: 307 us; the launch traced here: 306 us
  Pallas kernels  257 us (84%)
  local copies, waits for them, and re-layouts  30 us (10%)
  other arithmetic  13 us (4%)
    pallas_call x1, Pallas kernels, power_steps(): pl.pallas_call(steps_kernel, out_shape=jax.ShapeDtypeStruct(prob.shape, j...  122 us
    pallas_call x1, Pallas kernels, gather_rows(): pl.pallas_call(rows_kernel, out_shape=(jax.ShapeDtypeStruct((8, 2, 2, *ct...  55.2 us
    pallas_call x1, Pallas kernels, reduce_all(): pl.pallas_call(reduce_kernel, out_shape=(jax.ShapeDtypeStruct((NBLK, NBLK...  31.1 us
    pallas_call x1, Pallas kernels, gather_weight(): pl.pallas_call(weight_kernel, out_shape=jax.ShapeDtypeStruct((4, 8, 16, 1...  18.2 us
    pallas_call x1, Pallas kernels, flow_product(): pl.pallas_call(flow_kernel, out_shape=jax.ShapeDtypeStruct((NBLK, NBLK),...  15.6 us
    pallas_call x1, Pallas kernels, member_product(): pl.pallas_call(member_kernel, out_shape=jax.ShapeDtypeStruct((labels.shap...  8.74 us
    unnamed x45, local copies, waits for them, and re-layouts  6.99 us
    pallas_call x1, Pallas kernels, balance_of(): pl.pallas_call(balance_kernel, out_shape=jax.ShapeDtypeStruct((8, NBLK),...  6.78 us

profile of v3, /device:TPU:1, one launch (start us, length us, event | category | flops | bytes accessed | tf_op | source)
XLA Modules:
  0.0 306.3 jit_solution(7518808178360023622)
XLA Ops:
  1.5 0.8 copy.41
  3.0 0.9 convert_element_type.33.ctrl_ref
  3.9 0.9 convert_element_type.34.shelf_ref
  4.8 1.6 convert_reduce_fusion.2
  7.1 55.2 %gather_rows.1 = (bf16[8,2,2,24,768]{4,3,2,1,0:T(8,128)(2,1)S(1)}, bf16[8,2,2,32,1024]{4,3,2,1,0:T(8,128)(2,1)S(1)}, f32[4,8,16,128]{3,2,1,0:T(8,128)S(1)}, f32[2,8,16,128]{3,2,1,0:T(8,128)S(1)}) custom-call(bf16[24,768]{1,0:T(8,128)(2,1)S(1)} %convert_element_type.33.ctrl_ref, bf16[32,1024]{1,0:T(8,128)(2,1)S(1)} %convert_element_type.34.shelf_ref, ...), custom_call_target="tpu_custom_call" | custom-call | tf_op jit(solution)/shard_map/gather_rows/pallas_call | solution.py:452
  69.9 0.9 reshape.149
  70.8 1.9 copy.45
  72.6 1.9 reshape.150.labels_ref
  74.6 2.0 reshape.144
  76.6 2.2 copy.42
  78.8 1.2 copy.46.labels_ref
  80.1 0.9 copy-done.6
  80.9 8.7 %member_product.1.first_ref = bf16[32,48,256]{2,1,0:T(8,128)(2,1)S(1)} custom-call(f32[32,768]{1,0:T(8,128)S(1)} %copy-done.6, bf16[48,768]{1,0:T(8,128)(2,1)S(1)} %constant_dynamic-slice_fusion.factor_ref), custom_call_target="tpu_custom_call" | custom-call | tf_op jit(solution)/shard_map/member_product/pallas_call | solution.py:189
  89.7 0.9 copy-done.1
  90.6 1.4 copy.40.ctrl_ref
  92.1 2.6 copy.37
  94.6 1.5 convert_bitcast_fusion.factor_ref
  96.2 1.4 copy-done.3
  97.6 0.9 copy-done.4
  99.2 121.9 %power_steps.1 = f32[48,32,256]{2,1,0:T(8,128)S(1)} custom-call(f32[48,32,256]{2,1,0:T(8,128)S(1)} %copy-done.3, bf16[768,768]{1,0:T(8,128)(2,1)S(1)} %copy-done, bf16[1024,1024]{1,0:T(8,128)(2,1)} %bitcast.33, bf16[256,256]{1,0:T(8,128)(2,1)S(1)} %copy-done.4, f32[48,256]{1,0:T(8,128)S(1)} %copy-done.8, f32[32,256]{1,0:T(8,128)S(1)} %copy-done.9, ...), custom_call_target="tpu_custom_call" | custom-call | tf_op jit(solution)/shard_map/power_steps/pallas_call | solution.py:731
  223.7 18.2 %gather_weight.1 = f32[4,8,16,128]{3,2,1,0:T(8,128)} custom-call(f32[16,128]{1,0:T(8,128)} %pad.11.own_ref), custom_call_target="tpu_custom_call" | custom-call | tf_op jit(solution)/shard_map/gather_weight/pallas_call | solution.py:356
  241.9 1.2 reshape.147
  243.2 1.1 copy.43
  244.2 1.2 copy.47.weight_ref
  245.5 15.6 %flow_product.1 = f32[256,256]{1,0:T(8,128)S(1)} custom-call(f32[48,1024]{1,0:T(8,128)S(1)} %copy.46.labels_ref, f32[48,1024]{1,0:T(8,128)S(1)} %copy.47.weight_ref, f32[32,1024]{1,0:T(8,128)S(1)} %copy-done.5, bf16[32,48,256]{2,1,0:T(8,128)(2,1)S(1)} %copy-done.2), custom_call_target="tpu_custom_call" | custom-call | tf_op jit(solution)/shard_map/flow_product/pallas_call | solution.py:231
  261.0 0.8 select_add_fusion.part_ref
  261.8 31.1 %reduce_all.1 = (f32[256,256]{1,0:T(8,128)}, f32[8,128]{1,0:T(8,128)}) custom-call(f32[256,256]{1,0:T(8,128)} %select_add_fusion.part_ref, f32[8,128]{1,0:T(8,128)} %scatter.4.mass_ref), custom_call_target="tpu_custom_call" | custom-call | tf_op jit(solution)/shard_map/reduce_all/pallas_call | solution.py:148
  293.6 0.8 broadcast_in_dim.11.mass_ref
  294.4 6.8 %balance.1 = f32[8,256]{1,0:T(8,128)} custom-call(f32[256,256]{1,0:T(8,128)} %get-tuple-element.24.numer_ref, f32[256,256]{1,0:T(8,128)} %broadcast_in_dim.11.mass_ref), custom_call_target="tpu_custom_call" | custom-call | tf_op jit(solution)/shard_map/balance/pallas_call | solution.py:267
  301.2 2.4 fusion.1
  303.6 1.3 slice_multiply_fusion
  304.9 1.4 multiply_multiply_fusion
  (69 shorter events, 11.8 us)
Async XLA Ops:
  2.3 4.8 %copy-start.13 = (s32[48,32]{1,0:T(8,128)}, s32[48,32]{1,0:T(8,128)S(1)}, u32[]{:S(2)}) copy-start(s32[48,32]{1,0:T(8,128)S(1)} %copy.41) | copy-start | bytes 18436
  6.4 62.8 %copy-start.15 = (f32[256]{0:T(256)}, f32[256]{0:T(256)S(1)}, u32[]{:S(2)}) copy-start(f32[256]{0:T(256)S(1)} %get-tuple-element.28) | copy-start | bytes 3076
  62.3 0.7 copy-start.7
  63.0 0.7 copy-start.10
  63.6 6.2 %copy-start.11 = (f32[2,8,16,128]{3,2,1,0:T(8,128)S(1)}, f32[2,8,16,128]{3,2,1,0:T(8,128)}, u32[]{:S(2)}) copy-start(f32[2,8,16,128]{3,2,1,0:T(8,128)} %copy-done.10) | copy-start | bytes 393220
  64.9 11.8 %copy-start.18 = (f32[32]{0:T(128)}, f32[32]{0:T(128)S(1)}, u32[]{:S(2)}) copy-start(f32[32]{0:T(128)S(1)} %dynamic_slice.13) | copy-start | bytes 388
  68.0 10.9 %copy-start.20 = (f32[48]{0:T(128)}, f32[48]{0:T(128)S(1)}, u32[]{:S(2)}) copy-start(f32[48]{0:T(128)S(1)} %dynamic_slice.12) | copy-start | bytes 580
  80.1 0.9 copy-start.6
  89.7 0.9 copy-start.1
  92.1 4.1 %copy-start = (bf16[768,768]{1,0:T(8,128)(2,1)S(1)}, bf16[768,768]{1,0:T(8,128)(2,1)}, u32[]{:S(2)}) copy-start(bf16[768,768]{1,0:T(8,128)(2,1)} %copy.40.ctrl_ref) | copy-start | bytes 3538948
  92.1 4.1 %copy-start.8 = (f32[48,256]{1,0:T(8,128)S(1)}, f32[48,256]{1,0:T(8,128)}, u32[]{:S(2)}) copy-start(f32[48,256]{1,0:T(8,128)} %multiply_divide_fusion.rate_ref) | copy-start | bytes 147460
  92.1 4.1 %copy-start.9 = (f32[32,256]{1,0:T(8,128)S(1)}, f32[32,256]{1,0:T(8,128)}, u32[]{:S(2)}) copy-start(f32[32,256]{1,0:T(8,128)} %broadcast_in_dim.8.shelf_rate_ref) | copy-start | bytes 98308
  96.2 1.4 copy-start.3
  97.6 0.9 copy-start.4
  98.5 0.7 copy-start.12
  99.2 121.9 %copy-start.16 = (f32[256]{0:T(256)S(1)}, f32[256]{0:T(256)}, u32[]{:S(2)}) copy-start(f32[256]{0:T(256)} %copy-done.15) | copy-start | bytes 3076
  221.0 0.7 copy-start.19
  221.0 0.7 copy-start.21
  221.0 0.8 copy-start.17
  241.9 3.5 %copy-start.2 = (bf16[32,48,256]{2,1,0:T(8,128)(2,1)S(1)}, bf16[32,48,256]{2,1,0:T(8,128)(2,1)}, u32[]{:S(2)}) copy-start(bf16[32,48,256]{2,1,0:T(8,128)(2,1)} %copy-done.1) | copy-start | bytes 2359300
  241.9 3.5 %copy-start.5 = (f32[32,1024]{1,0:T(8,128)S(1)}, f32[32,1024]{1,0:T(8,128)}, u32[]{:S(2)}) copy-start(f32[32,1024]{1,0:T(8,128)} %convert_bitcast_fusion.factor_ref) | copy-start | bytes 393220
  245.5 55.8 %copy-start.14 = (s32[48,32]{1,0:T(8,128)S(1)}, s32[48,32]{1,0:T(8,128)}, u32[]{:S(2)}) copy-start(s32[48,32]{1,0:T(8,128)} %copy-done.13) | copy-start | bytes 18436

commit v4 on v3

--- a/solution.py
+++ b/solution.py
@@ -170,32 +170,6 @@
     )(part, mass)
 
 
-def member_kernel(labels_ref, factor_ref, out_ref):
-    count = labels_ref.shape[1]
-    blocks = lax.broadcasted_iota(jnp.int32, (NBLK, count), 0).astype(jnp.float32)
-
-    def body(row, carry):
-        names = jnp.broadcast_to(labels_ref[pl.ds(row, 1), :], (NBLK, count))
-        member = jnp.where(names == blocks, 1.0, 0.0).astype(jnp.bfloat16)
-        out_ref[row] = lax.dot_general(
-            factor_ref[...], member, (((1,), (1,)), ((), ())), preferred_element_type=jnp.float32
-        ).astype(out_ref.dtype)
-        return carry
-
-    lax.fori_loop(0, labels_ref.shape[0], body, 0)
-
-
-def member_product(labels, factor):
-    return pl.pallas_call(
-        member_kernel,
-        out_shape=jax.ShapeDtypeStruct((labels.shape[0], factor.shape[0], NBLK), jnp.bfloat16),
-        in_specs=[pl.BlockSpec(memory_space=VMEM)] * 2,
-        out_specs=pl.BlockSpec(memory_space=VMEM),
-        compiler_params=pltpu.CompilerParams(vmem_limit_bytes=40 << 20),
-        name="member_product",
-    )(labels, factor)
-
-
 def flow_kernel(labels_ref, weight_ref, factor_ref, first_ref, out_ref, wide, held):
     count = labels_ref.shape[1]
     depth = factor_ref.shape[0]
@@ -364,120 +338,6 @@
     )(own)
 
 
-def rows_kernel(
-    ctrl_ref, shelf_ref, label_ref, ctrl_all, shelf_all, by_shelf, by_ctrl,
-    swap_send, swap_recv, ring_send, ring_recv, pair_send, pair_recv,
-    send_a, recv_a, send_b, recv_b,
-):
-    ctrl = lax.axis_index("ctrl")
-    shelf = lax.axis_index("shelf")
-    deep, side, core = shelf // 4, (shelf // 2) % 2, shelf % 2
-    stages_a, stages_b = shelf_stages(), ctrl_stages()
-    greet_each(stages_a + stages_b)
-
-    wides = (ctrl_all, shelf_all)
-    ctrl_all[deep, side, core] = ctrl_ref[...]
-    shelf_all[deep, side, core] = shelf_ref[...]
-
-    def remote(piece, send_sem, recv_sem, target):
-        return pltpu.make_async_remote_copy(
-            src_ref=piece, dst_ref=piece, send_sem=send_sem, recv_sem=recv_sem,
-            device_id=(ctrl, target), device_id_type=MESH,
-        )
-
-    across = shelf + 2 - 4 * side
-    swaps = [
-        remote(wide.at[deep, side, core], swap_send.at[n], swap_recv.at[n], across)
-        for n, wide in enumerate(wides)
-    ]
-    for swap in swaps:
-        swap.start()
-    label_a = spread_small(label_ref[...], by_shelf, stages_a, send_a, recv_a)
-    label_b = spread_small(label_ref[...], by_ctrl, stages_b, send_b, recv_b)
-    run_loop(label_a[0])
-    run_loop(label_b[0])
-    for swap in swaps:
-        swap.wait()
-
-    right = ((deep + 1) % 8) * 4 + shelf % 4
-    left = ((deep + 7) % 8) * 4 + shelf % 4
-    sibling = shelf + 1 - 2 * core
-
-    def pair(n, block):
-        return remote(wides[n].at[block, :, core], pair_send.at[n, block], pair_recv.at[n, block], sibling)
-
-    def hop(n, way, count):
-        block = (deep + 8 - count + 1) % 8 if way == 0 else (deep + count - 1) % 8
-        return remote(
-            wides[n].at[block, :, core],
-            ring_send.at[n, way, count - 1],
-            ring_recv.at[n, way, count - 1],
-            right if way == 0 else left,
-        )
-
-    def used(n, way, count):
-        return count < 4 or n == way
-
-    for n in range(2):
-        for way in range(2):
-            hop(n, way, 1).start()
-        pair(n, deep).start()
-    for count in range(1, 5):
-        for n in range(2):
-            for way in range(2):
-                if not used(n, way, count):
-                    continue
-                hop(n, way, count).wait_recv()
-                if count < 4 and used(n, way, count + 1):
-                    hop(n, way, count + 1).start()
-                pair(n, (deep + 8 - count) % 8 if way == 0 else (deep + count) % 8).start()
-    run_loop(label_a[1])
-    run_loop(label_b[1])
-    for count in range(1, 5):
-        for n in range(2):
-            for way in range(2):
-                if used(n, way, count):
-                    hop(n, way, count).wait_send()
-    for block in range(8):
-        for n in range(2):
-            pltpu.make_async_remote_copy(
-                src_ref=wides[n].at[block, :, core],
-                dst_ref=wides[n].at[block, :, 1 - core],
-                send_sem=pair_send.at[n, block], recv_sem=pair_recv.at[n, block],
-                device_id=(ctrl, sibling), device_id_type=MESH,
-            ).wait()
-
-
-def gather_rows(ctrl_rows, shelf_rows, label_tile):
-    return pl.pallas_call(
-        rows_kernel,
-        out_shape=(
-            jax.ShapeDtypeStruct((8, 2, 2, *ctrl_rows.shape), jnp.bfloat16),
-            jax.ShapeDtypeStruct((8, 2, 2, *shelf_rows.shape), jnp.bfloat16),
-            jax.ShapeDtypeStruct((4, 8, 16, 128), jnp.float32),
-            jax.ShapeDtypeStruct((2, 8, 16, 128), jnp.float32),
-        ),
-        in_specs=[pl.BlockSpec(memory_space=VMEM)] * 3,
-        out_specs=tuple([pl.BlockSpec(memory_space=VMEM)] * 4),
-        scratch_shapes=[
-            pltpu.SemaphoreType.DMA((2,)),
-            pltpu.SemaphoreType.DMA((2,)),
-            pltpu.SemaphoreType.DMA((2, 2, 4)),
-            pltpu.SemaphoreType.DMA((2, 2, 4)),
-            pltpu.SemaphoreType.DMA((2, 8)),
-            pltpu.SemaphoreType.DMA((2, 8)),
-            pltpu.SemaphoreType.DMA((2, 8)),
-            pltpu.SemaphoreType.DMA((2, 8)),
-            pltpu.SemaphoreType.DMA((2, 8)),
-            pltpu.SemaphoreType.DMA((2, 8)),
-        ],
-        compiler_params=pltpu.CompilerParams(
-            collective_id=3, has_side_effects=True, vmem_limit_bytes=32 << 20
-        ),
-        name="gather_rows",
-    )(ctrl_rows, shelf_rows, label_tile)
-
-
 def as_tile(values):
     return jnp.pad(values.reshape(12, 128), ((0, 4), (0, 0)))
 
@@ -487,15 +347,15 @@
     return jnp.transpose(kept, (2, 1, 0, 3)).reshape(48, SHELF)
 
 
-def ctrl_wide(tiles):
-    kept = tiles[:, :, 0:12].reshape(2, 8, 48, 32)
-    return jnp.transpose(kept, (3, 1, 0, 2)).reshape(32, CTRL)
-
-
 def steps_kernel(
-    prob_ref, ctrl_ref, shelf_ref, disk_ref, rate_ref, shelf_rate_ref, scale_ref, state_ref,
+    prob_ref, ctrl_rows_ref, shelf_rows_ref, disk_in_ref, label_ref,
+    state_ref, first_ref, shelf_labels_ref, shelf_cols_ref, weight_ref, mass_ref, out_c_ref, out_s_ref,
+    base_ref,
+    ctrl_all, shelf_all, by_shelf, by_ctrl, ctrl_wide, ctrl_own, ctrl_ref, shelf_ref, disk_ref,
+    label_rows, shelf_wide_rows, ctrl_labels, rate_ref, shelf_rate_ref, scale_ref, disk_row,
     home_y, home_z, at_y, made_y, at_z, made_z, back_y, back_z,
-    send_sem, recv_sem,
+    swap_send, swap_recv, ring_send, ring_recv, pair_send, pair_recv,
+    send_a, recv_a, send_b, recv_b, send_sem, recv_sem,
 ):
     ctrl = lax.axis_index("ctrl")
     shelf = lax.axis_index("shelf")
@@ -521,6 +381,13 @@
     lax.fori_loop(1, ctrls, signal_y, 0)
     lax.fori_loop(1, shelves, signal_z, 0)
     state_ref[...] = prob_ref[...]
+    disk_ref[...] = disk_in_ref[...].astype(jnp.bfloat16)
+    deep, side = shelf // 4, (shelf // 2) % 2
+    wides = (ctrl_all, shelf_all)
+    ctrl_all[deep, side, core] = ctrl_rows_ref[...].astype(jnp.bfloat16)
+    shelf_all[deep, side, core] = shelf_rows_ref[...].astype(jnp.bfloat16)
+    label_a = spread_small(label_ref[...], by_shelf, shelf_stages(), send_a, recv_a)
+    label_b = spread_small(label_ref[...], by_ctrl, ctrl_stages(), send_b, recv_b)
 
     order = lax.broadcasted_iota(jnp.int32, (256, 256), 0)
     other = lax.broadcasted_iota(jnp.int32, (256, 256), 1)
@@ -528,6 +395,147 @@
         jnp.logical_and(order // 16 == other % 16, order % 16 == other // 16), 1.0, 0.0
     ).astype(jnp.bfloat16)
     pl.semaphore_wait(barrier, ctrls - 1 + shelves - 1)
+
+    def along_shelf(piece, send, recv, target):
+        return pltpu.make_async_remote_copy(
+            src_ref=piece, dst_ref=piece, send_sem=send, recv_sem=recv,
+            device_id=(ctrl, target), device_id_type=MESH,
+        )
+
+    swaps = [
+        along_shelf(
+            wide.at[deep, side, core], swap_send.at[n], swap_recv.at[n], shelf + 2 - 4 * side
+        )
+        for n, wide in enumerate(wides)
+    ]
+    for copy in swaps:
+        copy.start()
+    for start, _, size in (label_a[0], label_b[0]):
+        lax.fori_loop(1, size, start, 0)
+
+    right = ((deep + 1) % 8) * 4 + shelf % 4
+    left = ((deep + 7) % 8) * 4 + shelf % 4
+    sibling = shelf + 1 - 2 * core
+
+    def pair(n, block, side_core):
+        piece = wides[n].at[block, :, side_core]
+        return along_shelf(piece, pair_send.at[n, block], pair_recv.at[n, block], sibling)
+
+    def hop(n, way, count):
+        block = (deep + 8 - count + 1) % 8 if way == 0 else (deep + count - 1) % 8
+        return along_shelf(
+            wides[n].at[block, :, core],
+            ring_send.at[n, way, count - 1],
+            ring_recv.at[n, way, count - 1],
+            right if way == 0 else left,
+        )
+
+    def used(n, way, count):
+        return count < 4 or n == way
+
+    def gather_rows():
+        for copy in swaps:
+            copy.wait()
+        for n in range(2):
+            for way in range(2):
+                hop(n, way, 1).start()
+            pair(n, deep, core).start()
+        for _, finish, size in (label_a[0], label_b[0]):
+            lax.fori_loop(1, size, finish, 0)
+        for start, _, size in (label_a[1], label_b[1]):
+            lax.fori_loop(1, size, start, 0)
+        for count in range(1, 5):
+            for n in range(2):
+                for way in range(2):
+                    if not used(n, way, count):
+                        continue
+                    hop(n, way, count).wait_recv()
+                    if count < 4 and used(n, way, count + 1):
+                        hop(n, way, count + 1).start()
+                    pair(n, (deep + 8 - count) % 8 if way == 0 else (deep + count) % 8, core).start()
+        for _, finish, size in (label_a[1], label_b[1]):
+            lax.fori_loop(1, size, finish, 0)
+        for count in range(1, 5):
+            for n in range(2):
+                for way in range(2):
+                    if used(n, way, count):
+                        hop(n, way, count).wait_send()
+
+        def settle(block, carry):
+            for n in range(2):
+                pair(n, block, 1 - core).wait_recv()
+                pair(n, block, core).wait_send()
+            return carry
+
+        lax.fori_loop(0, 8, settle, 0)
+
+    def prepare():
+        unit = jnp.where(order == other, 1.0, 0.0).astype(jnp.bfloat16)
+        dims = (((1,), (1,)), ((), ()))
+        for n in range(shelves):
+            wide = ctrl_all[n // 4, (n // 2) % 2, n % 2].astype(jnp.float32)
+            ctrl_wide[n * 24 : n * 24 + 24] = wide
+        for m in range(0, CTRL, 256):
+            block = ctrl_wide[:, m : m + 256].astype(jnp.bfloat16)
+            turned = lax.dot_general(unit, block, dims, preferred_element_type=jnp.float32)
+            ctrl_ref[m : m + 256] = turned.astype(jnp.bfloat16)
+        shelf_sum = jnp.zeros((SHELF, 1), jnp.float32)
+        for m in range(0, SHELF, 256):
+            block = shelf_all[:, :, :, :, m : m + 256].reshape(SHELF, 256)
+            turned = lax.dot_general(unit, block, dims, preferred_element_type=jnp.float32)
+            shelf_ref[m : m + 256] = turned.astype(jnp.bfloat16)
+            shelf_sum += jnp.sum(block.astype(jnp.float32), axis=1, keepdims=True)
+        shelf_cols_ref[...] = shelf_ref[
+            pl.ds(pl.multiple_of(shelf * rows_s, 16), rows_s)
+        ].astype(jnp.float32)
+
+        ctrl_max = jnp.max(
+            jnp.sum(ctrl_wide[...], axis=1, keepdims=True), axis=0, keepdims=True
+        )
+        shelf_max = jnp.max(shelf_sum, axis=0, keepdims=True)
+        ones = jnp.ones((8, 256), jnp.bfloat16)
+        disk_sum = lax.dot_general(ones, disk_ref[...], dims, preferred_element_type=jnp.float32)
+        disk_max = jnp.max(disk_sum[0:1], axis=1, keepdims=True)
+        base = 1.05 * (ctrl_max * shelf_max) * disk_max
+        own_rows = ctrl_wide[pl.ds(pl.multiple_of(ctrl * rows_c, 8), rows_c)]
+        ctrl_own[...] = own_rows.astype(jnp.bfloat16)
+        own_c = jnp.sum(own_rows, axis=1, keepdims=True)
+        own_s = jnp.sum(
+            shelf_rows_ref[...].astype(jnp.bfloat16).astype(jnp.float32), axis=1, keepdims=True
+        )
+        rate_ref[...] = own_c * disk_sum[0:1] / base
+        shelf_rate_ref[...] = jnp.broadcast_to(own_s, (rows_s, 256))
+        scale_ref[...] = jnp.broadcast_to(1.0 / base, (8, 256))
+        disk_row[...] = disk_sum
+        base_ref[...] = jnp.broadcast_to(base, (8, lanes))
+        out_c_ref[...] = jnp.broadcast_to(own_c, (rows_c, lanes))
+        out_s_ref[...] = jnp.broadcast_to(own_s, (rows_s, lanes))
+
+        spread_pairs(by_shelf, shelf_wide_rows)
+        for z in range(8):
+            shelf_labels_ref[:, z * lanes : (z + 1) * lanes] = shelf_wide_rows[z, 0:rows_c]
+        for i in range(ctrls):
+            tile = by_ctrl[i % 2, i // 2]
+            for q in range(4):
+                moved = tile if q == 0 else pltpu.roll(tile, lanes - 32 * q, 1)
+                label_rows[i, pl.ds(q, 16, stride=4), :] = moved
+        turned = jnp.transpose(label_rows[:, 0:rows_c, :].reshape(CTRL, lanes))
+        ctrl_labels[...] = turned[0:rows_s]
+
+    names = lax.broadcasted_iota(jnp.int32, (NBLK, CTRL), 0).astype(jnp.float32)
+
+    def fill(slot):
+        part = rows_s // 8
+
+        def body(row, carry):
+            have = jnp.broadcast_to(ctrl_labels[pl.ds(row, 1), :], (NBLK, CTRL))
+            member = jnp.where(have == names, 1.0, 0.0).astype(jnp.bfloat16)
+            first_ref[row] = lax.dot_general(
+                ctrl_own[...], member, (((1,), (1,)), ((), ())), preferred_element_type=jnp.float32
+            ).astype(first_ref.dtype)
+            return carry
+
+        lax.fori_loop(slot * part, slot * part + part, body, 0)
 
     def swapped(block):
         flat = jnp.dot(swap, block.reshape(256, lanes), preferred_element_type=jnp.float32)
@@ -691,20 +699,30 @@
                 home_y[0, q : q + 16, p : p + 16, :] = swapped(made[:, q : q + 16, :lanes])
         z_forward(1)
         y_forward(0)
+
+        @pl.when(repeat == 0)
+        def _():
+            gather_rows()
+            prepare()
+
+        fill(repeat * 4)
         y_forward_wait(0)
         y_product(0)
         y_back(0)
         z_middle(1)
+        fill(repeat * 4 + 1)
         y_back_wait(0)
         exchange_rows(back_y.at[0], home_z.at[0])
         z_forward(0)
         z_back_wait(1)
         exchange_rows(back_z.at[1], home_y.at[1])
         y_forward(1)
+        fill(repeat * 4 + 2)
         z_middle(0)
         y_forward_wait(1)
         y_product(1)
         y_back(1)
+        fill(repeat * 4 + 3)
         z_back_wait(0)
         y_back_wait(1)
         z_forward_sent(1)
@@ -713,7 +731,7 @@
         def update(row, inner):
             kept = 1.0 - rate_ref[pl.ds(row, 1), :] * shelf_rate_ref[...]
             third = jnp.concatenate([back_z[0, row], home_z[1, row]], axis=1)
-            state_ref[row] = third.astype(jnp.float32) * scale_ref[...] + state_ref[row] * kept
+            state_ref[row] = third.astype(jnp.float32) * scale_ref[0:1] + state_ref[row] * kept
             return inner
 
         lax.fori_loop(0, rows_c, update, 0)
@@ -724,16 +742,64 @@
 
     lax.fori_loop(0, STEPS, one_step, 0)
 
-
-def power_steps(prob, ctrl_t, shelf_t, disk_bf, rate, shelf_rate, scale):
+    lead = lax.broadcasted_iota(jnp.int32, (8, 256), 0) == 0
+    sums = jnp.where(lead, 1.0, disk_row[...])
+    weight_ref[...] = jnp.zeros_like(weight_ref)
+    mass_ref[...] = jnp.zeros_like(mass_ref)
+    for r in range(rows_c // 4):
+        both = lax.dot_general(
+            sums,
+            state_ref[4 * r : 4 * r + 4].reshape(4 * rows_s, 256),
+            (((1,), (1,)), ((), ())),
+            precision=HIGHEST,
+            preferred_element_type=jnp.float32,
+        )
+        mass_ref[r : r + 1] = both[0:1]
+        weight_ref[r : r + 1] = both[1:2]
+
+
+def spread_pairs(tiles, wide):
+    lane = lax.broadcasted_iota(jnp.int32, (16, 128), 1) // 32
+    for z in range(8):
+        for q in range(4):
+            made = jnp.zeros((16, 128), jnp.float32)
+            for p in range(4):
+                tile = tiles[p, z]
+                moved = tile if p == q else pltpu.roll(tile, (32 * (p - q)) % 128, 1)
+                made = jnp.where(lane == p, moved, made)
+            wide[z, pl.ds(q, 16, stride=4), :] = made
+
+
+def power_steps(prob, ctrl_rows, shelf_rows, disk, label_tile):
     rows_c, rows_s, _ = prob.shape
-    bf = jnp.bfloat16
+    bf, f32 = jnp.bfloat16, jnp.float32
+    outs = [
+        (prob.shape, f32), ((rows_s, rows_c, NBLK), bf), ((rows_c, SHELF), f32), ((rows_s, SHELF), f32),
+        ((16, 128), f32), ((16, 128), f32), ((rows_c, 128), f32), ((rows_s, 128), f32), ((8, 128), f32),
+    ]
+    dma = pltpu.SemaphoreType.DMA
     return pl.pallas_call(
         steps_kernel,
-        out_shape=jax.ShapeDtypeStruct(prob.shape, jnp.float32),
-        in_specs=[pl.BlockSpec(memory_space=VMEM)] * 7,
-        out_specs=pl.BlockSpec(memory_space=VMEM),
+        out_shape=tuple(jax.ShapeDtypeStruct(*out) for out in outs),
+        in_specs=[pl.BlockSpec(memory_space=VMEM)] * 5,
+        out_specs=tuple([pl.BlockSpec(memory_space=VMEM)] * len(outs)),
         scratch_shapes=[
+            pltpu.VMEM((8, 2, 2, 24, CTRL), bf),
+            pltpu.VMEM((8, 2, 2, 32, SHELF), bf),
+            pltpu.VMEM((4, 8, 16, 128), f32),
+            pltpu.VMEM((2, 8, 16, 128), f32),
+            pltpu.VMEM((CTRL, CTRL), f32),
+            pltpu.VMEM((rows_c, CTRL), bf),
+            pltpu.VMEM((CTRL, CTRL), bf),
+            pltpu.VMEM((SHELF, SHELF), bf),
+            pltpu.VMEM((DISK, DISK), bf),
+            pltpu.VMEM((16, 64, 128), f32),
+            pltpu.VMEM((8, 64, 128), f32),
+            pltpu.VMEM((rows_s, CTRL), f32),
+            pltpu.VMEM((rows_c, DISK), f32),
+            pltpu.VMEM((rows_s, DISK), f32),
+            pltpu.VMEM((8, DISK), f32),
+            pltpu.VMEM((8, DISK), f32),
             pltpu.VMEM((2, rows_s, rows_c, 128), bf),
             pltpu.VMEM((2, rows_c, rows_s, 128), bf),
             pltpu.VMEM((2, 2, CTRL, 128), bf),
@@ -742,57 +808,27 @@
             pltpu.VMEM((3, SHELF, 128), bf),
             pltpu.VMEM((2, rows_s, rows_c, 128), bf),
             pltpu.VMEM((2, rows_c, rows_s, 128), bf),
-            pltpu.SemaphoreType.DMA((8, 32)),
-            pltpu.SemaphoreType.DMA((8, 32)),
+            dma((2,)), dma((2,)), dma((2, 2, 4)), dma((2, 2, 4)), dma((2, 8)), dma((2, 8)),
+            dma((2, 8)), dma((2, 8)), dma((2, 8)), dma((2, 8)), dma((8, 32)), dma((8, 32)),
         ],
         compiler_params=pltpu.CompilerParams(
-            collective_id=4, has_side_effects=True, vmem_limit_bytes=48 << 20
+            collective_id=4, has_side_effects=True, vmem_limit_bytes=56 << 20
         ),
         name="power_steps",
-    )(prob, ctrl_t, shelf_t, disk_bf, rate, shelf_rate, scale)
+    )(prob, ctrl_rows, shelf_rows, disk, label_tile)
 
 
 def local(prob, ctrl_rates, shelf_rates, disk_rates, labels):
-    ctrl_all, shelf_all, by_shelf, by_ctrl = gather_rows(
-        ctrl_rates.astype(jnp.bfloat16),
-        shelf_rates.astype(jnp.bfloat16),
-        as_tile(labels.astype(jnp.float32)),
-    )
-    ctrl_bf = ctrl_all.reshape(CTRL, CTRL)
-    shelf_bf = shelf_all.reshape(SHELF, SHELF)
-    shelf_labels = shelf_wide(by_shelf)
-    ctrl_labels = ctrl_wide(by_ctrl)
-    disk_bf = disk_rates.astype(jnp.bfloat16)
-    ctrl_out = jnp.sum(ctrl_bf.astype(jnp.float32), axis=1)
-    shelf_out = jnp.sum(shelf_bf.astype(jnp.float32), axis=1)
-    disk_out = jnp.sum(disk_bf.astype(jnp.float32), axis=1)
-    uniform_rate = 1.05 * (jnp.max(ctrl_out) * jnp.max(shelf_out)) * jnp.max(disk_out)
-    ctrl_rows = prob.shape[0]
-    shelf_rows = prob.shape[1]
-    ctrl_at = lax.axis_index("ctrl") * ctrl_rows
-    shelf_at = lax.axis_index("shelf") * shelf_rows
-    ctrl_loc = lax.dynamic_slice_in_dim(ctrl_out, ctrl_at, ctrl_rows)
-    shelf_loc = lax.dynamic_slice_in_dim(shelf_out, shelf_at, shelf_rows)
-    rate = ctrl_loc[:, None] * disk_out[None, :] / uniform_rate
-    shelf_rate = jnp.broadcast_to(shelf_loc[:, None], (shelf_rows, DISK))
-    iterate = power_steps(
-        prob,
-        ctrl_bf.T,
-        shelf_bf.T,
-        disk_bf,
-        rate,
-        shelf_rate,
-        jnp.full((1, DISK), 1.0, jnp.float32) / uniform_rate,
-    )
-
-    first = member_product(ctrl_labels, lax.dynamic_slice_in_dim(ctrl_bf, ctrl_at, ctrl_rows))
-    shelf_columns = lax.dynamic_slice_in_dim(shelf_bf, shelf_at, shelf_rows, axis=1)
-    shelf_columns = shelf_columns.T.astype(jnp.float32)
-
-    pair_mass = jnp.sum(iterate, axis=2)
-    weighted = jnp.sum(iterate * disk_out, axis=2)
-    pair_kept = pair_mass - weighted * (ctrl_loc[:, None] * shelf_loc[None, :] / uniform_rate)
-    shelf_weight = shelf_wide(gather_weight(as_tile(weighted)))
+    ctrl_rows, shelf_rows = prob.shape[0], prob.shape[1]
+    outs = power_steps(
+        prob, ctrl_rates, shelf_rates, disk_rates, as_tile(labels.astype(jnp.float32))
+    )
+    iterate, first, shelf_labels, shelf_columns, weight_tile, mass_tile, out_c, out_s, base = outs
+    uniform_rate = base[0, 0]
+    pair_mass = mass_tile[0:12].reshape(ctrl_rows, shelf_rows)
+    weighted = weight_tile[0:12].reshape(ctrl_rows, shelf_rows)
+    pair_kept = pair_mass - weighted * (out_c[:, 0:1] * out_s[:, 0][None, :] / uniform_rate)
+    shelf_weight = shelf_wide(gather_weight(weight_tile))
     part = flow_product(shelf_labels, shelf_weight, shelf_columns, first) / uniform_rate
     pair_count = shelf_rows * ctrl_rows
     blocks = jnp.arange(NBLK, dtype=jnp.int32)

time: 307 us -> 251 us (0.82)
  Pallas kernels: 257 us -> 233 us
  local copies, waits for them, and re-layouts: 30 us -> 8.38 us
  other arithmetic: 13 us -> 5.67 us
    pallas_call x3 -> x1, Pallas kernels: 186 us -> 162 us  [power_steps(): pl.pallas_call(steps_kernel, out_shape=tuple((jax.ShapeDtypeStruct(*out)...]
    unnamed x45 -> x12, local copies, waits for them, and re-layouts: 6.99 us -> 0.82 us
    reshape x3 -> x0, local copies, waits for them, and re-layouts: 5.38 us -> none  [the longest x1 2.56 us: local(): shelf_bf = shelf_all.reshape(SHELF, SHELF)]
    convert_element_type x3 -> x0, other arithmetic: 3.31 us -> none  [the longest x1 1.51 us: local(): shelf_columns = shelf_columns.T.astype(jnp.float32)]
    transpose x2 -> x0, local copies, waits for them, and re-layouts: 3.31 us -> none  [the longest x1 1.87 us: ctrl_wide(): return jnp.transpose(kept, (3, 1, 0, 2)).reshape(32, CTRL)]
where the time goes in v4:
time: 251 us
  Pallas kernels  233 us (93%)
  local copies, waits for them, and re-layouts  8.38 us (3%)
  other arithmetic  5.67 us (2%)
  matrix products  3.05 us (1%)
    pallas_call x1, Pallas kernels, power_steps(): pl.pallas_call(steps_kernel, out_shape=tuple((jax.ShapeDtypeStruct(*out)...  162 us
    pallas_call x1, Pallas kernels, reduce_all(): pl.pallas_call(reduce_kernel, out_shape=(jax.ShapeDtypeStruct((NBLK, NBLK...  32.4 us
    pallas_call x1, Pallas kernels, gather_weight(): pl.pallas_call(weight_kernel, out_shape=jax.ShapeDtypeStruct((4, 8, 16, 1...  16 us
    pallas_call x1, Pallas kernels, flow_product(): pl.pallas_call(flow_kernel, out_shape=jax.ShapeDtypeStruct((NBLK, NBLK),...  15.4 us
    pallas_call x1, Pallas kernels, balance_of(): pl.pallas_call(balance_kernel, out_shape=jax.ShapeDtypeStruct((8, NBLK),...  6.78 us

profile of v4, /device:TPU:1, one launch (start us, length us, event | category | flops | bytes accessed | tf_op | source)
XLA Modules:
  0.0 250.6 jit_solution(208902169554693803)
XLA Ops:
  0.6 0.8 convert_element_type.4
  1.4 0.1 copy.10
  1.5 0.1 reshape.117
  1.6 0.6 pad.7.label_ref
  2.2 162.2 %power_steps.1 = (f32[48,32,256]{2,1,0:T(8,128)}, bf16[32,48,256]{2,1,0:T(8,128)(2,1)}, f32[48,1024]{1,0:T(8,128)}, f32[32,1024]{1,0:T(8,128)}, f32[16,128]{1,0:...) custom-call(f32[48,32,256]{2,1,0:T(8,128)} %prob_ref.1, ...), custom_call_target="tpu_custom_call" | custom-call | tf_op jit(solution)/shard_map/power_steps/pallas_call | solution.py:781
  164.4 1.2 slice.47
  165.6 0.8 slice_reduce_fusion
  166.4 0.8 slice_reduce_fusion.1
  167.2 0.7 multiply_divide_fusion
  168.0 0.1 div.30
  168.0 0.7 slice_bitcast_fusion
  168.8 0.1 copy.11
  168.9 0.1 eq.29
  168.9 0.7 fusion
  169.6 16.0 %gather_weight.1 = f32[4,8,16,128]{3,2,1,0:T(8,128)} custom-call(f32[16,128]{1,0:T(8,128)} %get-tuple-element.27.own_ref), custom_call_target="tpu_custom_call" | custom-call | tf_op jit(solution)/shard_map/gather_weight/pallas_call | solution.py:330
  185.7 1.3 reshape.118
  186.9 0.3 copy.12
  187.2 0.2 copy.13.weight_ref
  187.4 0.0 copy-done
  187.4 0.0 copy-done.1
  187.4 0.0 copy-done.2
  187.4 0.0 copy-start.3
  187.4 15.4 %flow_product.1 = f32[256,256]{1,0:T(8,128)S(1)} custom-call(f32[48,1024]{1,0:T(8,128)S(1)} %copy-done.1, f32[48,1024]{1,0:T(8,128)S(1)} %copy.13.weight_ref, f32[32,1024]{1,0:T(8,128)S(1)} %copy-done.2, bf16[32,48,256]{2,1,0:T(8,128)(2,1)S(1)} %copy-done), custom_call_target="tpu_custom_call" | custom-call | tf_op jit(solution)/shard_map/flow_product/pallas_call | solution.py:205
  202.8 1.5 select_add_fusion.part_ref
  204.3 0.6 scatter.4.mass_ref
  204.8 32.4 %reduce_all.1 = (f32[256,256]{1,0:T(8,128)}, f32[8,128]{1,0:T(8,128)}) custom-call(f32[256,256]{1,0:T(8,128)} %select_add_fusion.part_ref, f32[8,128]{1,0:T(8,128)} %scatter.4.mass_ref), custom_call_target="tpu_custom_call" | custom-call | tf_op jit(solution)/shard_map/reduce_all/pallas_call | solution.py:148
  237.3 0.7 slice_bitcast_fusion.2
  237.9 0.8 broadcast_in_dim.10.mass_ref
  238.8 6.8 %balance.1 = f32[8,256]{1,0:T(8,128)} custom-call(f32[256,256]{1,0:T(8,128)} %get-tuple-element.34.numer_ref, f32[256,256]{1,0:T(8,128)} %broadcast_in_dim.10.mass_ref), custom_call_target="tpu_custom_call" | custom-call | tf_op jit(solution)/shard_map/balance/pallas_call | solution.py:241
  245.5 2.4 fusion.1
  247.9 1.4 multiply_multiply_fusion
  249.4 1.3 slice_multiply_fusion
  (8 shorter events, 0.0 us)
Async XLA Ops:
  0.6 168.2 %copy-start.4 = (s32[48,32]{0,1:T(8,128)S(1)}, s32[48,32]{0,1:T(8,128)}, u32[]{:S(2)}) copy-start(s32[48,32]{0,1:T(8,128)} %param.11) | copy-start | bytes 18436
  185.6 1.7 copy-start
  185.6 1.7 copy-start.1
  185.7 1.7 copy-start.2
  187.4 60.5 %copy-start.3 = (f32[48,32,256]{2,1,0:T(8,128)S(1)}, f32[48,32,256]{2,1,0:T(8,128)}, u32[]{:S(2)}) copy-start(f32[48,32,256]{2,1,0:T(8,128)} %get-tuple-element.25) | copy-start | bytes 4718596

commit v5 on v4

--- a/solution.py
+++ b/solution.py
@@ -48,7 +48,7 @@
             return carry
 
         lax.fori_loop(1, GROUP, signal, 0)
-    pl.semaphore_wait(barrier, len(groups) * (GROUP - 1))
+    return barrier, len(groups) * (GROUP - 1)
 
 
 def exchange(group, streams, send_sem, recv_sem):
@@ -80,14 +80,74 @@
     lax.fori_loop(1, GROUP, finish, 0)
 
 
+NT = (((1,), (1,)), ((), ()))
+
+
+def flow_part(labels_ref, weight_ref, factor_ref, first_ref, out_ref, wide, held):
+    count = labels_ref.shape[1]
+    depth = factor_ref.shape[0]
+    blocks = lax.broadcasted_iota(jnp.int32, (NBLK, count), 0).astype(jnp.float32)
+
+    def body(row, carry):
+        names = jnp.broadcast_to(labels_ref[pl.ds(row, 1), :], (NBLK, count))
+        member = jnp.where(names == blocks, 1.0, 0.0).astype(jnp.bfloat16)
+        scaled = factor_ref[...] * weight_ref[pl.ds(row, 1), :]
+        upper = scaled.astype(jnp.bfloat16)
+        slot = row % 2
+        wide[slot, 0:depth, :] = upper
+        wide[slot, depth : 2 * depth, :] = (scaled - upper.astype(jnp.float32)).astype(jnp.bfloat16)
+        both = lax.dot_general(wide[slot], member, NT, preferred_element_type=jnp.float32)
+        held[:, pl.ds(row, 1), :] = (both[0:depth] + both[depth:]).reshape(depth, 1, NBLK)
+        return carry
+
+    lax.fori_loop(0, labels_ref.shape[0], body, 0, unroll=2)
+    rows = held.shape[0] * held.shape[1]
+    mine = held[...].reshape(rows, NBLK)
+    first = first_ref[...].reshape(rows, NBLK)
+    upper = mine.astype(jnp.bfloat16)
+    lower = (mine - upper.astype(jnp.float32)).astype(jnp.bfloat16)
+    dims = (((0,), (0,)), ((), ()))
+    out_ref[...] = lax.dot_general(
+        upper, first, dims, preferred_element_type=jnp.float32
+    ) + lax.dot_general(lower, first, dims, preferred_element_type=jnp.float32)
+
+
+def block_terms(label_ref, pair_mass_ref, pair_kept_ref):
+    line = lax.broadcasted_iota(jnp.int32, (8, 128), 0)
+    names = lax.broadcasted_iota(jnp.int32, (NBLK, 128), 0).astype(jnp.float32)
+    terms = jnp.zeros((8, NBLK), jnp.float32)
+    for r in range(12):
+        have = jnp.broadcast_to(label_ref[r : r + 1], (NBLK, 128))
+        member = jnp.where(have == names, 1.0, 0.0)
+        pair = jnp.where(line == 0, pair_mass_ref[r : r + 1], 0.0)
+        pair = jnp.where(line == 1, pair_kept_ref[r : r + 1], pair)
+        terms += lax.dot_general(
+            pair, member, NT, precision=HIGHEST, preferred_element_type=jnp.float32
+        )
+    return terms
+
+
 def reduce_kernel(
-    part_ref, mass_ref, sum_ref, total_ref,
+    labels_ref, weight_ref, factor_ref, first_ref, label_ref, pair_mass_ref, pair_kept_ref, base_ref,
+    sum_ref, total_ref,
+    part_ref, mass_ref, wide, held,
     rows, tiles, highs, deeps, blocks, mass_plane, mass_deep, mass_high,
     send_sem, recv_sem,
 ):
     plane, deep, high = place()
-    greet((plane, deep, high))
+    barrier, greetings = greet((plane, deep, high))
     plane_me, deep_me, high_me = plane[0], deep[0], high[0]
+
+    flow_part(labels_ref, weight_ref, factor_ref, first_ref, part_ref, wide, held)
+    terms = block_terms(label_ref, pair_mass_ref, pair_kept_ref)
+    mass_ref[...] = jnp.zeros_like(mass_ref)
+    mass_ref[0:1] = terms[0:1, 0:128]
+    mass_ref[1:2] = terms[0:1, 128:256]
+    row = lax.broadcasted_iota(jnp.int32, (NBLK, NBLK), 0)
+    column = lax.broadcasted_iota(jnp.int32, (NBLK, NBLK), 1)
+    kept = jnp.where(row == column, jnp.broadcast_to(terms[1:2], (NBLK, NBLK)), 0.0)
+    part_ref[...] = part_ref[...] / base_ref[0:1, 0:1] + kept
+    pl.semaphore_wait(barrier, greetings)
 
     exchange(
         plane,
@@ -143,17 +203,22 @@
     exchange(plane, ((lambda m: own, own),), send_sem.at[4], recv_sem.at[4])
 
 
-def reduce_all(part, mass):
+def reduce_all(labels, weight, factor, first, label_tile, mass_tile, kept_tile, base):
     tile = (8, 128)
+    depth, count = factor.shape
     return pl.pallas_call(
         reduce_kernel,
         out_shape=(
             jax.ShapeDtypeStruct((NBLK, NBLK), jnp.float32),
             jax.ShapeDtypeStruct(tile, jnp.float32),
         ),
-        in_specs=[pl.BlockSpec(memory_space=VMEM)] * 2,
+        in_specs=[pl.BlockSpec(memory_space=VMEM)] * 8,
         out_specs=(pl.BlockSpec(memory_space=VMEM), pl.BlockSpec(memory_space=VMEM)),
         scratch_shapes=[
+            pltpu.VMEM((NBLK, NBLK), jnp.float32),
+            pltpu.VMEM(tile, jnp.float32),
+            pltpu.VMEM((2, 2 * depth, count), jnp.bfloat16),
+            pltpu.VMEM((depth, labels.shape[0], NBLK), jnp.float32),
             pltpu.VMEM((GROUP, 32, NBLK), jnp.float32),
             pltpu.VMEM((GROUP, *tile), jnp.float32),
             pltpu.VMEM((GROUP, *tile), jnp.float32),
@@ -165,60 +230,22 @@
             pltpu.SemaphoreType.DMA((5, 2, GROUP)),
             pltpu.SemaphoreType.DMA((5, 2, GROUP)),
         ],
-        compiler_params=pltpu.CompilerParams(collective_id=1, has_side_effects=True),
+        compiler_params=pltpu.CompilerParams(
+            collective_id=1, has_side_effects=True, vmem_limit_bytes=40 << 20
+        ),
         name="reduce_all",
-    )(part, mass)
-
-
-def flow_kernel(labels_ref, weight_ref, factor_ref, first_ref, out_ref, wide, held):
-    count = labels_ref.shape[1]
-    depth = factor_ref.shape[0]
-    blocks = lax.broadcasted_iota(jnp.int32, (NBLK, count), 0).astype(jnp.float32)
-
-    def body(row, carry):
-        names = jnp.broadcast_to(labels_ref[pl.ds(row, 1), :], (NBLK, count))
-        member = jnp.where(names == blocks, 1.0, 0.0).astype(jnp.bfloat16)
-        scaled = factor_ref[...] * weight_ref[pl.ds(row, 1), :]
-        upper = scaled.astype(jnp.bfloat16)
-        wide[0:depth, :] = upper
-        wide[depth : 2 * depth, :] = (scaled - upper.astype(jnp.float32)).astype(jnp.bfloat16)
-        both = lax.dot_general(
-            wide[...], member, (((1,), (1,)), ((), ())), preferred_element_type=jnp.float32
-        )
-        held[:, pl.ds(row, 1), :] = (both[0:depth] + both[depth:]).reshape(depth, 1, NBLK)
-        return carry
-
-    lax.fori_loop(0, labels_ref.shape[0], body, 0)
-    rows = held.shape[0] * held.shape[1]
-    mine = held[...].reshape(rows, NBLK)
-    first = first_ref[...].reshape(rows, NBLK)
-    upper = mine.astype(jnp.bfloat16)
-    lower = (mine - upper.astype(jnp.float32)).astype(jnp.bfloat16)
-    dims = (((0,), (0,)), ((), ()))
-    out_ref[...] = lax.dot_general(
-        upper, first, dims, preferred_element_type=jnp.float32
-    ) + lax.dot_general(lower, first, dims, preferred_element_type=jnp.float32)
-
-
-def flow_product(labels, weight, factor, first):
-    depth, count = factor.shape
-    return pl.pallas_call(
-        flow_kernel,
-        out_shape=jax.ShapeDtypeStruct((NBLK, NBLK), jnp.float32),
-        in_specs=[pl.BlockSpec(memory_space=VMEM)] * 4,
-        out_specs=pl.BlockSpec(memory_space=VMEM),
-        scratch_shapes=[
-            pltpu.VMEM((2 * depth, count), jnp.bfloat16),
-            pltpu.VMEM((depth, labels.shape[0], NBLK), jnp.float32),
-        ],
-        compiler_params=pltpu.CompilerParams(vmem_limit_bytes=40 << 20),
-        name="flow_product",
-    )(labels, weight, factor, first)
-
-
-def balance_kernel(numer_ref, mass_ref, out_ref, power):
+    )(labels, weight, factor, first, label_tile, mass_tile, kept_tile, base)
+
+
+def balance_kernel(numer_ref, total_ref, label_ref, state_ref, refined_ref, coarse_ref, power, spread):
     size = NBLK
-    power[...] = numer_ref[...] / mass_ref[...] - 1.0 / size
+    line = lax.broadcasted_iota(jnp.int32, (size, size), 0)
+    column = lax.broadcasted_iota(jnp.int32, (size, size), 1)
+    mass = jnp.concatenate([total_ref[0:1], total_ref[1:2]], axis=1)
+    mass_column = jnp.sum(
+        jnp.where(line == column, jnp.broadcast_to(mass, (size, size)), 0.0), axis=1, keepdims=True
+    )
+    power[...] = numer_ref[...] / mass_column - 1.0 / size
     start = jnp.full((8, size), 1.0 / size, jnp.float32)
 
     def going(state):
@@ -234,18 +261,38 @@
         return turn + 1, jnp.max(jnp.abs(after)), row
 
     state = (jnp.int32(0), jnp.max(jnp.abs(power[...])), start)
-    out_ref[...] = lax.while_loop(going, turn_once, state)[2]
-
-
-def balance_of(numer, mass):
+    balance = lax.while_loop(going, turn_once, state)[2]
+    coarse_ref[...] = balance * float(size)
+
+    share = balance[0:1] / mass
+    spread[...] = jnp.zeros_like(spread)
+    for q in range(4):
+        tile = label_ref[...]
+        spread[pl.ds(q, 16, stride=4), :] = tile if q == 0 else pltpu.roll(tile, 128 - 32 * q, 1)
+    names = jnp.transpose(spread[...])[0:32]
+    lane = lax.broadcasted_iota(jnp.int32, (32, size), 1).astype(jnp.float32)
+    for a in range(state_ref.shape[0]):
+        picked = jnp.where(names[:, a : a + 1] == lane, share, 0.0)
+        factor = jnp.sum(picked, axis=1, keepdims=True)
+        refined_ref[a] = state_ref[a] * factor * float(CTRL * SHELF * DISK)
+
+
+def balance_of(numer, total, label_tile, state):
     return pl.pallas_call(
         balance_kernel,
-        out_shape=jax.ShapeDtypeStruct((8, NBLK), jnp.float32),
-        in_specs=[pl.BlockSpec(memory_space=VMEM)] * 2,
-        out_specs=pl.BlockSpec(memory_space=VMEM),
-        scratch_shapes=[pltpu.VMEM((NBLK, NBLK), jnp.float32)],
+        out_shape=(
+            jax.ShapeDtypeStruct(state.shape, jnp.float32),
+            jax.ShapeDtypeStruct((8, NBLK), jnp.float32),
+        ),
+        in_specs=[pl.BlockSpec(memory_space=VMEM)] * 4,
+        out_specs=(pl.BlockSpec(memory_space=VMEM), pl.BlockSpec(memory_space=VMEM)),
+        scratch_shapes=[
+            pltpu.VMEM((NBLK, NBLK), jnp.float32),
+            pltpu.VMEM((128, 128), jnp.float32),
+        ],
+        compiler_params=pltpu.CompilerParams(vmem_limit_bytes=32 << 20),
         name="balance",
-    )(numer, mass)[0]
+    )(numer, total, label_tile, state)
 
 
 def spread_small(own, wide, stages, send_sem, recv_sem):
@@ -278,28 +325,6 @@
     return first, second
 
 
-def run_loop(part):
-    start, finish, size = part
-    lax.fori_loop(1, size, start, 0)
-    lax.fori_loop(1, size, finish, 0)
-
-
-def greet_each(peers):
-    barrier = pltpu.get_barrier_semaphore()
-    count = 0
-    for me, size, peer in peers:
-
-        def signal(step, carry, me=me, size=size, peer=peer):
-            pl.semaphore_signal(
-                barrier, inc=1, device_id=peer((me + step) % size), device_id_type=MESH
-            )
-            return carry
-
-        lax.fori_loop(1, size, signal, 0)
-        count += size - 1
-    pl.semaphore_wait(barrier, count)
-
-
 def shelf_stages():
     ctrl = lax.axis_index("ctrl")
     shelf = lax.axis_index("shelf")
@@ -318,44 +343,19 @@
     )
 
 
-def weight_kernel(own_ref, wide_ref, send_sem, recv_sem):
-    stages = shelf_stages()
-    greet_each(stages)
-    first, second = spread_small(own_ref[...], wide_ref, stages, send_sem, recv_sem)
-    run_loop(first)
-    run_loop(second)
-
-
-def gather_weight(own):
-    return pl.pallas_call(
-        weight_kernel,
-        out_shape=jax.ShapeDtypeStruct((4, 8, 16, 128), jnp.float32),
-        in_specs=[pl.BlockSpec(memory_space=VMEM)],
-        out_specs=pl.BlockSpec(memory_space=VMEM),
-        scratch_shapes=[pltpu.SemaphoreType.DMA((2, 8)), pltpu.SemaphoreType.DMA((2, 8))],
-        compiler_params=pltpu.CompilerParams(collective_id=2, has_side_effects=True),
-        name="gather_weight",
-    )(own)
-
-
 def as_tile(values):
     return jnp.pad(values.reshape(12, 128), ((0, 4), (0, 0)))
 
 
-def shelf_wide(tiles):
-    kept = tiles[:, :, 0:12].reshape(4, 8, 48, 32)
-    return jnp.transpose(kept, (2, 1, 0, 3)).reshape(48, SHELF)
-
-
 def steps_kernel(
     prob_ref, ctrl_rows_ref, shelf_rows_ref, disk_in_ref, label_ref,
-    state_ref, first_ref, shelf_labels_ref, shelf_cols_ref, weight_ref, mass_ref, out_c_ref, out_s_ref,
-    base_ref,
+    state_ref, first_ref, shelf_labels_ref, shelf_cols_ref, weight_wide_ref, mass_ref, kept_ref, base_ref,
+    weight_ref, by_weight,
     ctrl_all, shelf_all, by_shelf, by_ctrl, ctrl_wide, ctrl_own, ctrl_ref, shelf_ref, disk_ref,
     label_rows, shelf_wide_rows, ctrl_labels, rate_ref, shelf_rate_ref, scale_ref, disk_row,
     home_y, home_z, at_y, made_y, at_z, made_z, back_y, back_z,
     swap_send, swap_recv, ring_send, ring_recv, pair_send, pair_recv,
-    send_a, recv_a, send_b, recv_b, send_sem, recv_sem,
+    send_a, recv_a, send_b, recv_b, send_w, recv_w, send_y, recv_y, send_sem, recv_sem,
 ):
     ctrl = lax.axis_index("ctrl")
     shelf = lax.axis_index("shelf")
@@ -508,8 +508,6 @@
         scale_ref[...] = jnp.broadcast_to(1.0 / base, (8, 256))
         disk_row[...] = disk_sum
         base_ref[...] = jnp.broadcast_to(base, (8, lanes))
-        out_c_ref[...] = jnp.broadcast_to(own_c, (rows_c, lanes))
-        out_s_ref[...] = jnp.broadcast_to(own_s, (rows_s, lanes))
 
         spread_pairs(by_shelf, shelf_wide_rows)
         for z in range(8):
@@ -547,9 +545,6 @@
             for q in range(0, second, 16):
                 target[q : q + 16, p : p + 16, :] = swapped(source[p : p + 16, q : q + 16, :])
 
-    def part_c(ref, owner):
-        return ref.at[:, pl.ds(pl.multiple_of(owner * rows_c, 16), rows_c), :]
-
     def part_s(ref, owner):
         return ref.at[:, pl.ds(pl.multiple_of(owner * rows_s, 16), rows_s), :]
 
@@ -560,6 +555,13 @@
             device_id=device, device_id_type=MESH,
         )
 
+    def remote_y(source, target, half, way, n, mine, peer):
+        return pltpu.make_async_remote_copy(
+            src_ref=source, dst_ref=target,
+            send_sem=send_y.at[half, way, n, peer], recv_sem=recv_y.at[half, way, n, mine],
+            device_id=(peer, shelf), device_id_type=MESH,
+        )
+
     def each(count, first, act):
         def body(step, carry):
             act((first + step) % count)
@@ -567,57 +569,61 @@
 
         lax.fori_loop(1, count, body, 0)
 
+    def rows_of(ref, owner):
+        return ref.at[pl.ds(pl.multiple_of(owner * rows_c, 16), rows_c), :]
+
     def y_forward(half):
-        def act(peer):
-            remote(
-                home_y.at[half, pl.ds(peer * per_y, per_y)], part_c(at_y.at[half], ctrl),
-                4 * half, ctrl, peer, (peer, shelf),
-            ).start()
-
-        each(ctrls, ctrl, act)
-        part_c(at_y.at[half], ctrl)[...] = home_y[half, pl.ds(ctrl * per_y, per_y)]
-
-    def y_forward_wait(half):
-        def act(peer):
-            remote(
-                home_y.at[half, pl.ds(peer * per_y, per_y)], part_c(at_y.at[half], peer),
-                4 * half, peer, peer, (peer, shelf),
-            ).wait()
-
-        each(ctrls, ctrl, act)
-
-    def y_product(half):
-        both = jnp.concatenate([at_y[half, n] for n in range(per_y)], axis=1)
-        for m in range(0, ctrls * rows_c, 256):
-            made = jnp.dot(ctrl_ref[m : m + 256], both, preferred_element_type=jnp.float32)
-            for n in range(per_y):
-                made_y[half, n, m : m + 256, :] = made[:, n * lanes : (n + 1) * lanes].astype(
-                    jnp.bfloat16
+        for n in range(per_y):
+
+            def act(peer, n=n):
+                remote_y(
+                    home_y.at[half, peer * per_y + n], rows_of(at_y.at[half, n], ctrl),
+                    half, 0, n, ctrl, peer,
+                ).start()
+
+            each(ctrls, ctrl, act)
+            rows_of(at_y.at[half, n], ctrl)[...] = home_y[half, ctrl * per_y + n]
+
+    def y_middle(half):
+        for n in range(per_y):
+
+            def arrived(peer, n=n):
+                remote_y(
+                    home_y.at[half, peer * per_y + n], rows_of(at_y.at[half, n], peer),
+                    half, 0, n, peer, peer,
+                ).wait()
+
+            each(ctrls, ctrl, arrived)
+            for m in range(0, ctrls * rows_c, 256):
+                made = jnp.dot(
+                    ctrl_ref[m : m + 256], at_y[half, n], preferred_element_type=jnp.float32
                 )
-
-    def y_back(half):
-        def act(peer):
-            remote(
-                part_c(made_y.at[half], peer), back_y.at[half, pl.ds(ctrl * per_y, per_y)],
-                4 * half + 1, ctrl, peer, (peer, shelf),
-            ).start()
-
-        each(ctrls, ctrl, act)
-        back_y[half, pl.ds(ctrl * per_y, per_y)] = part_c(made_y.at[half], ctrl)[...]
+                made_y[half, n, m : m + 256, :] = made.astype(jnp.bfloat16)
+
+            def act(peer, n=n):
+                remote_y(
+                    rows_of(made_y.at[half, n], peer), back_y.at[half, ctrl * per_y + n],
+                    half, 1, n, ctrl, peer,
+                ).start()
+
+            each(ctrls, ctrl, act)
+            back_y[half, ctrl * per_y + n] = rows_of(made_y.at[half, n], ctrl)[...]
 
     def y_back_wait(half):
-        def act(peer):
-            remote(
-                part_c(made_y.at[half], peer), back_y.at[half, pl.ds(peer * per_y, per_y)],
-                4 * half + 1, peer, peer, (peer, shelf),
-            ).wait()
-
-        each(ctrls, ctrl, act)
+        for n in range(per_y):
+
+            def act(peer, n=n):
+                remote_y(
+                    rows_of(made_y.at[half, n], peer), back_y.at[half, peer * per_y + n],
+                    half, 1, n, peer, peer,
+                ).wait()
+
+            each(ctrls, ctrl, act)
 
     def z_forward_copy(half, to):
         return remote(
             home_z.at[half, pl.ds(to * per_z, per_z)], part_s(at_z, shelf),
-            4 * half + 2, shelf, to, (ctrl, 2 * to + half),
+            2 * half, shelf, to, (ctrl, 2 * to + half),
         )
 
     def z_forward(half):
@@ -644,7 +650,7 @@
             def arrived(peer):
                 remote(
                     home_z.at[half, pl.ds(0, per_z)], part_s(at_z, peer),
-                    4 * half + 2, peer, 0, (ctrl, peer),
+                    2 * half, peer, 0, (ctrl, peer),
                 ).wait_recv()
 
             each(shelves, shelf, arrived)
@@ -659,7 +665,7 @@
             def act(peer):
                 remote(
                     part_s(made_z, peer), back_z.at[half, pl.ds(chip * per_z, per_z)],
-                    4 * half + 3, chip, peer, (ctrl, peer),
+                    2 * half + 1, chip, peer, (ctrl, peer),
                 ).start()
 
             each(shelves, shelf, act)
@@ -668,7 +674,7 @@
     def z_back_from(half, source):
         return remote(
             part_s(made_z, shelf), back_z.at[half, pl.ds(source * per_z, per_z)],
-            4 * half + 3, source, 0, (ctrl, 2 * source + half),
+            2 * half + 1, source, 0, (ctrl, 2 * source + half),
         )
 
     def z_back_wait(half):
@@ -684,7 +690,7 @@
             def act(peer):
                 remote(
                     part_s(made_z, peer), back_z.at[half, pl.ds(chip * per_z, per_z)],
-                    4 * half + 3, chip, peer, (ctrl, peer),
+                    2 * half + 1, chip, peer, (ctrl, peer),
                 ).wait_send()
 
             each(shelves, shelf, act)
@@ -706,9 +712,7 @@
             prepare()
 
         fill(repeat * 4)
-        y_forward_wait(0)
-        y_product(0)
-        y_back(0)
+        y_middle(0)
         z_middle(1)
         fill(repeat * 4 + 1)
         y_back_wait(0)
@@ -719,9 +723,7 @@
         y_forward(1)
         fill(repeat * 4 + 2)
         z_middle(0)
-        y_forward_wait(1)
-        y_product(1)
-        y_back(1)
+        y_middle(1)
         fill(repeat * 4 + 3)
         z_back_wait(0)
         y_back_wait(1)
@@ -756,6 +758,25 @@
         )
         mass_ref[r : r + 1] = both[0:1]
         weight_ref[r : r + 1] = both[1:2]
+    stages = spread_small(weight_ref[...], by_weight, shelf_stages(), send_w, recv_w)
+    lax.fori_loop(1, stages[0][2], stages[0][0], 0)
+    kept_ref[...] = jnp.zeros_like(kept_ref)
+    ones = jnp.ones((8, 256), jnp.float32)
+    for r in range(rows_c // 4):
+        part = [
+            state_ref[n] * (1.0 - rate_ref[n : n + 1] * shelf_rate_ref[...])
+            for n in range(4 * r, 4 * r + 4)
+        ]
+        kept_ref[r : r + 1] = lax.dot_general(
+            ones, jnp.concatenate(part, axis=0), NT,
+            precision=HIGHEST, preferred_element_type=jnp.float32,
+        )[0:1]
+    lax.fori_loop(1, stages[0][2], stages[0][1], 0)
+    lax.fori_loop(1, stages[1][2], stages[1][0], 0)
+    lax.fori_loop(1, stages[1][2], stages[1][1], 0)
+    spread_pairs(by_weight, shelf_wide_rows)
+    for z in range(8):
+        weight_wide_ref[:, z * lanes : (z + 1) * lanes] = shelf_wide_rows[z, 0:rows_c]
 
 
 def spread_pairs(tiles, wide):
@@ -775,7 +796,7 @@
     bf, f32 = jnp.bfloat16, jnp.float32
     outs = [
         (prob.shape, f32), ((rows_s, rows_c, NBLK), bf), ((rows_c, SHELF), f32), ((rows_s, SHELF), f32),
-        ((16, 128), f32), ((16, 128), f32), ((rows_c, 128), f32), ((rows_s, 128), f32), ((8, 128), f32),
+        ((rows_c, SHELF), f32), ((16, 128), f32), ((16, 128), f32), ((8, 128), f32),
     ]
     dma = pltpu.SemaphoreType.DMA
     return pl.pallas_call(
@@ -784,6 +805,8 @@
         in_specs=[pl.BlockSpec(memory_space=VMEM)] * 5,
         out_specs=tuple([pl.BlockSpec(memory_space=VMEM)] * len(outs)),
         scratch_shapes=[
+            pltpu.VMEM((16, 128), f32),
+            pltpu.VMEM((4, 8, 16, 128), f32),
             pltpu.VMEM((8, 2, 2, 24, CTRL), bf),
             pltpu.VMEM((8, 2, 2, 32, SHELF), bf),
             pltpu.VMEM((4, 8, 16, 128), f32),
@@ -809,7 +832,8 @@
             pltpu.VMEM((2, rows_s, rows_c, 128), bf),
             pltpu.VMEM((2, rows_c, rows_s, 128), bf),
             dma((2,)), dma((2,)), dma((2, 2, 4)), dma((2, 2, 4)), dma((2, 8)), dma((2, 8)),
-            dma((2, 8)), dma((2, 8)), dma((2, 8)), dma((2, 8)), dma((8, 32)), dma((8, 32)),
+            dma((2, 8)), dma((2, 8)), dma((2, 8)), dma((2, 8)), dma((2, 8)), dma((2, 8)),
+            dma((2, 2, 2, 16)), dma((2, 2, 2, 16)), dma((4, 32)), dma((4, 32)),
         ],
         compiler_params=pltpu.CompilerParams(
             collective_id=4, has_side_effects=True, vmem_limit_bytes=56 << 20
@@ -819,40 +843,14 @@
 
 
 def local(prob, ctrl_rates, shelf_rates, disk_rates, labels):
-    ctrl_rows, shelf_rows = prob.shape[0], prob.shape[1]
-    outs = power_steps(
-        prob, ctrl_rates, shelf_rates, disk_rates, as_tile(labels.astype(jnp.float32))
+    label_tile = as_tile(labels.astype(jnp.float32))
+    outs = power_steps(prob, ctrl_rates, shelf_rates, disk_rates, label_tile)
+    iterate, first, shelf_labels, shelf_columns, shelf_weight, mass_tile, kept_tile, base = outs
+    numer, total = reduce_all(
+        shelf_labels, shelf_weight, shelf_columns, first, label_tile, mass_tile, kept_tile, base
     )
-    iterate, first, shelf_labels, shelf_columns, weight_tile, mass_tile, out_c, out_s, base = outs
-    uniform_rate = base[0, 0]
-    pair_mass = mass_tile[0:12].reshape(ctrl_rows, shelf_rows)
-    weighted = weight_tile[0:12].reshape(ctrl_rows, shelf_rows)
-    pair_kept = pair_mass - weighted * (out_c[:, 0:1] * out_s[:, 0][None, :] / uniform_rate)
-    shelf_weight = shelf_wide(gather_weight(weight_tile))
-    part = flow_product(shelf_labels, shelf_weight, shelf_columns, first) / uniform_rate
-    pair_count = shelf_rows * ctrl_rows
-    blocks = jnp.arange(NBLK, dtype=jnp.int32)
-    member_table = (labels.reshape(pair_count)[:, None] == blocks[None, :]).astype(
-        jnp.float32
-    )
-    terms = jnp.dot(
-        jnp.stack([pair_mass.reshape(pair_count), pair_kept.reshape(pair_count)]),
-        member_table,
-        precision=HIGHEST,
-    )
-    identity = jnp.eye(NBLK, dtype=jnp.float32)
-    part = part + identity * terms[1][:, None]
-    mass_tile = jnp.zeros((8, 128), jnp.float32).at[0:2].set(terms[0].reshape(2, 128))
-    numer, mass_sum = reduce_all(part, mass_tile)
-    block_mass = mass_sum[0:2].reshape(NBLK)
-    balance = balance_of(numer, jnp.broadcast_to(block_mass[:, None], (NBLK, NBLK)))
-    ratio_share = balance / block_mass
-    pair_share = jnp.dot(member_table, ratio_share, precision=HIGHEST).reshape(
-        ctrl_rows, shelf_rows
-    )
-    refined = iterate * pair_share[:, :, None] * float(CTRL * SHELF * DISK)
-    coarse = balance * NBLK
-    return (refined, coarse)
+    refined, coarse = balance_of(numer, total, label_tile, iterate)
+    return (refined, coarse[0])
 
 
 def solution(mesh):

time: 251 us -> 234 us (0.932)
  Pallas kernels: 233 us -> 224 us
  other arithmetic: 5.67 us -> 0.72 us
  matrix products: 3.05 us -> 0 us
    pallas_call x3 -> x1, Pallas kernels: 38.2 us -> 10.1 us  [balance_of(): pl.pallas_call(balance_kernel, out_shape=(jax.ShapeDtypeStruct(state.shap...]
    pallas_call x1, Pallas kernels: 32.4 us -> 42.6 us  [reduce_all(): pl.pallas_call(reduce_kernel, out_shape=(jax.ShapeDtypeStruct((NBLK, NBLK...]
    pallas_call x1, Pallas kernels: 162 us -> 171 us  [power_steps(): pl.pallas_call(steps_kernel, out_shape=tuple((jax.ShapeDtypeStruct(*out)...]
    unnamed x12 -> x18, local copies, waits for them, and re-layouts: 0.82 us -> 7.36 us
    dot_general x2 -> x0, matrix products: 3.05 us -> none  [the longest x1 2.39 us: local(): jnp.dot(member_table, ratio_share, precision=HIGHEST)]
    mul x2 -> x0, other arithmetic: 2.69 us -> none  [the longest x1 1.43 us: local(): refined = iterate * pair_share[:, :, None] * float(CTRL * SHELF * DISK)]
where the time goes in v5:
time: 234 us
  Pallas kernels  224 us (96%)
  local copies, waits for them, and re-layouts  8.68 us (4%)
    pallas_call x1, Pallas kernels, power_steps(): pl.pallas_call(steps_kernel, out_shape=tuple((jax.ShapeDtypeStruct(*out)...  171 us
    pallas_call x1, Pallas kernels, reduce_all(): pl.pallas_call(reduce_kernel, out_shape=(jax.ShapeDtypeStruct((NBLK, NBLK...  42.6 us
    pallas_call x1, Pallas kernels, balance_of(): pl.pallas_call(balance_kernel, out_shape=(jax.ShapeDtypeStruct(state.shap...  10.1 us
    unnamed x18, local copies, waits for them, and re-layouts  7.36 us

profile of v5, /device:TPU:1, one launch (start us, length us, event | category | flops | bytes accessed | tf_op | source)
XLA Modules:
  0.0 233.6 jit_solution(4561613288639292379)
XLA Ops:
  0.6 0.7 convert_element_type.5
  1.4 0.1 copy.8
  1.4 0.1 reshape.7
  1.5 0.6 pad.4.label_ref
  2.1 0.0 copy-start.4
  2.1 170.8 %power_steps.1 = (f32[48,32,256]{2,1,0:T(8,128)}, bf16[32,48,256]{2,1,0:T(8,128)(2,1)}, f32[48,1024]{1,0:T(8,128)}, f32[32,1024]{1,0:T(8,128)}, f32[48,1024]{1,0...) custom-call(f32[48,32,256]{2,1,0:T(8,128)} %prob_ref.1, f32[24,768]{1,0:T(8,128)} %ctrl_rows_ref.1, ...), custom_call_target="tpu_custom_call" | custom-call | tf_op jit(solution)/shard_map/power_steps/pallas_call | solution.py:802
  172.9 0.0 copy-done.4
  172.9 0.0 copy-start.1
  172.9 1.1 copy-done.1
  174.0 0.0 copy-start.2
  174.1 0.9 copy-done.2
  175.0 0.0 copy-start.3
  175.0 0.9 copy-done.3
  175.9 0.0 copy-start.5
  175.9 0.9 copy-done.5
  176.8 0.0 copy-start.6
  176.8 0.7 copy-done.6
  177.5 0.0 copy-start.7
  177.5 0.7 copy-done.7
  178.2 0.0 copy-start.8
  178.2 0.7 copy-done.8
  178.9 42.6 %reduce_all.1 = (f32[256,256]{1,0:T(8,128)S(1)}, f32[8,128]{1,0:T(8,128)S(1)}) custom-call(f32[48,1024]{1,0:T(8,128)S(1)} %copy-done.2, f32[48,1024]{1,0:T(8,128)S(1)} %copy-done.3, f32[32,1024]{1,0:T(8,128)S(1)} %copy-done.5, bf16[32,48,256]{2,1,0:T(8,128)(2,1)S(1)} %copy-done.1, f32[16,128]{1,0:T(8,128)S(1)} %copy-done.4, f32[16,128]{1,0:T(8,128)S(1)} %copy-done.6, ...), custom_call_target="tpu_custom_call" | custom-call | tf_op jit(solution)/shard_map/reduce_all/pallas_call | solution.py:209
  221.5 0.0 copy-start
  221.5 1.4 copy-done
  222.9 10.1 %balance.1 = (f32[48,32,256]{2,1,0:T(8,128)}, f32[8,256]{1,0:T(8,128)S(1)}) custom-call(f32[256,256]{1,0:T(8,128)S(1)} %get-tuple-element.21.numer_ref, f32[8,128]{1,0:T(8,128)S(1)} %get-tuple-element.22.total_ref, f32[16,128]{1,0:T(8,128)S(1)} %copy-done.4, f32[48,32,256]{2,1,0:T(8,128)S(1)} %copy-done), custom_call_target="tpu_custom_call" | custom-call | tf_op jit(solution)/shard_map/balance/pallas_call | solution.py:281
  233.0 0.6 slice.3
Async XLA Ops:
  2.1 170.8 %copy-start.4 = (f32[16,128]{1,0:T(8,128)S(1)}, f32[16,128]{1,0:T(8,128)}, u32[]{:S(2)}) copy-start(f32[16,128]{1,0:T(8,128)} %pad.4.label_ref) | copy-start | bytes 24580
  172.9 1.1 copy-start.1
  174.0 0.9 copy-start.2
  175.0 0.9 copy-start.3
  175.9 0.9 copy-start.5
  176.8 0.7 copy-start.6
  177.5 0.7 copy-start.7
  178.2 0.7 copy-start.8
  221.5 1.4 copy-start

commit v6 on v5

--- a/solution.py
+++ b/solution.py
@@ -35,20 +35,6 @@
         return (member * 2 + ctrl % 2, shelf)
 
     return (plane_me, plane), (deep_me, deep), (high_me, high)
-
-
-def greet(groups):
-    barrier = pltpu.get_barrier_semaphore()
-    for me, peer in groups:
-
-        def signal(step, carry, me=me, peer=peer):
-            pl.semaphore_signal(
-                barrier, inc=1, device_id=peer((me + step) % GROUP), device_id_type=MESH
-            )
-            return carry
-
-        lax.fori_loop(1, GROUP, signal, 0)
-    return barrier, len(groups) * (GROUP - 1)
 
 
 def exchange(group, streams, send_sem, recv_sem):
@@ -127,15 +113,15 @@
     return terms
 
 
-def reduce_kernel(
+def reduce_part(
+    groups,
     labels_ref, weight_ref, factor_ref, first_ref, label_ref, pair_mass_ref, pair_kept_ref, base_ref,
     sum_ref, total_ref,
     part_ref, mass_ref, wide, held,
     rows, tiles, highs, deeps, blocks, mass_plane, mass_deep, mass_high,
     send_sem, recv_sem,
 ):
-    plane, deep, high = place()
-    barrier, greetings = greet((plane, deep, high))
+    plane, deep, high = groups
     plane_me, deep_me, high_me = plane[0], deep[0], high[0]
 
     flow_part(labels_ref, weight_ref, factor_ref, first_ref, part_ref, wide, held)
@@ -147,7 +133,6 @@
     column = lax.broadcasted_iota(jnp.int32, (NBLK, NBLK), 1)
     kept = jnp.where(row == column, jnp.broadcast_to(terms[1:2], (NBLK, NBLK)), 0.0)
     part_ref[...] = part_ref[...] / base_ref[0:1, 0:1] + kept
-    pl.semaphore_wait(barrier, greetings)
 
     exchange(
         plane,
@@ -203,41 +188,9 @@
     exchange(plane, ((lambda m: own, own),), send_sem.at[4], recv_sem.at[4])
 
 
-def reduce_all(labels, weight, factor, first, label_tile, mass_tile, kept_tile, base):
-    tile = (8, 128)
-    depth, count = factor.shape
-    return pl.pallas_call(
-        reduce_kernel,
-        out_shape=(
-            jax.ShapeDtypeStruct((NBLK, NBLK), jnp.float32),
-            jax.ShapeDtypeStruct(tile, jnp.float32),
-        ),
-        in_specs=[pl.BlockSpec(memory_space=VMEM)] * 8,
-        out_specs=(pl.BlockSpec(memory_space=VMEM), pl.BlockSpec(memory_space=VMEM)),
-        scratch_shapes=[
-            pltpu.VMEM((NBLK, NBLK), jnp.float32),
-            pltpu.VMEM(tile, jnp.float32),
-            pltpu.VMEM((2, 2 * depth, count), jnp.bfloat16),
-            pltpu.VMEM((depth, labels.shape[0], NBLK), jnp.float32),
-            pltpu.VMEM((GROUP, 32, NBLK), jnp.float32),
-            pltpu.VMEM((GROUP, *tile), jnp.float32),
-            pltpu.VMEM((GROUP, *tile), jnp.float32),
-            pltpu.VMEM((GROUP, *tile), jnp.float32),
-            pltpu.VMEM((GROUP, *tile), jnp.float32),
-            pltpu.VMEM((GROUP, *tile), jnp.float32),
-            pltpu.VMEM((GROUP, *tile), jnp.float32),
-            pltpu.VMEM((GROUP, *tile), jnp.float32),
-            pltpu.SemaphoreType.DMA((5, 2, GROUP)),
-            pltpu.SemaphoreType.DMA((5, 2, GROUP)),
-        ],
-        compiler_params=pltpu.CompilerParams(
-            collective_id=1, has_side_effects=True, vmem_limit_bytes=40 << 20
-        ),
-        name="reduce_all",
-    )(labels, weight, factor, first, label_tile, mass_tile, kept_tile, base)
-
-
-def balance_kernel(numer_ref, total_ref, label_ref, state_ref, refined_ref, coarse_ref, power, spread):
+def balance_kernel(numer_ref, total_ref, label_ref, state_ref, refined_ref, coarse_ref, power, spread, held, sem):
+    load = pltpu.make_async_copy(state_ref, held, sem)
+    load.start()
     size = NBLK
     line = lax.broadcasted_iota(jnp.int32, (size, size), 0)
     column = lax.broadcasted_iota(jnp.int32, (size, size), 1)
@@ -271,10 +224,11 @@
         spread[pl.ds(q, 16, stride=4), :] = tile if q == 0 else pltpu.roll(tile, 128 - 32 * q, 1)
     names = jnp.transpose(spread[...])[0:32]
     lane = lax.broadcasted_iota(jnp.int32, (32, size), 1).astype(jnp.float32)
-    for a in range(state_ref.shape[0]):
+    load.wait()
+    for a in range(held.shape[0]):
         picked = jnp.where(names[:, a : a + 1] == lane, share, 0.0)
         factor = jnp.sum(picked, axis=1, keepdims=True)
-        refined_ref[a] = state_ref[a] * factor * float(CTRL * SHELF * DISK)
+        refined_ref[a] = held[a] * factor * float(CTRL * SHELF * DISK)
 
 
 def balance_of(numer, total, label_tile, state):
@@ -284,11 +238,13 @@
             jax.ShapeDtypeStruct(state.shape, jnp.float32),
             jax.ShapeDtypeStruct((8, NBLK), jnp.float32),
         ),
-        in_specs=[pl.BlockSpec(memory_space=VMEM)] * 4,
+        in_specs=[pl.BlockSpec(memory_space=VMEM)] * 3 + [pl.BlockSpec(memory_space=pl.ANY)],
         out_specs=(pl.BlockSpec(memory_space=VMEM), pl.BlockSpec(memory_space=VMEM)),
         scratch_shapes=[
             pltpu.VMEM((NBLK, NBLK), jnp.float32),
             pltpu.VMEM((128, 128), jnp.float32),
+            pltpu.VMEM(state.shape, jnp.float32),
+            pltpu.SemaphoreType.DMA,
         ],
         compiler_params=pltpu.CompilerParams(vmem_limit_bytes=32 << 20),
         name="balance",
@@ -349,13 +305,17 @@
 
 def steps_kernel(
     prob_ref, ctrl_rows_ref, shelf_rows_ref, disk_in_ref, label_ref,
-    state_ref, first_ref, shelf_labels_ref, shelf_cols_ref, weight_wide_ref, mass_ref, kept_ref, base_ref,
+    state_ref, sum_ref, total_ref,
+    first_ref, shelf_labels_ref, shelf_cols_ref, weight_wide_ref, mass_ref, kept_ref, base_ref,
+    part_ref, block_mass_ref, wide, held,
+    rows, tiles, highs, deeps, blocks, mass_plane, mass_deep, mass_high,
     weight_ref, by_weight,
     ctrl_all, shelf_all, by_shelf, by_ctrl, ctrl_wide, ctrl_own, ctrl_ref, shelf_ref, disk_ref,
     label_rows, shelf_wide_rows, ctrl_labels, rate_ref, shelf_rate_ref, scale_ref, disk_row,
     home_y, home_z, at_y, made_y, at_z, made_z, back_y, back_z,
     swap_send, swap_recv, ring_send, ring_recv, pair_send, pair_recv,
     send_a, recv_a, send_b, recv_b, send_w, recv_w, send_y, recv_y, send_sem, recv_sem,
+    send_r, recv_r,
 ):
     ctrl = lax.axis_index("ctrl")
     shelf = lax.axis_index("shelf")
@@ -380,6 +340,15 @@
 
     lax.fori_loop(1, ctrls, signal_y, 0)
     lax.fori_loop(1, shelves, signal_z, 0)
+    groups = place()
+    plane_me, plane_peer = groups[0]
+
+    def signal_plane(step, carry):
+        target = plane_peer((plane_me + step) % GROUP)
+        pl.semaphore_signal(barrier, inc=1, device_id=target, device_id_type=MESH)
+        return carry
+
+    lax.fori_loop(1, GROUP, signal_plane, 0)
     state_ref[...] = prob_ref[...]
     disk_ref[...] = disk_in_ref[...].astype(jnp.bfloat16)
     deep, side = shelf // 4, (shelf // 2) % 2
@@ -394,7 +363,7 @@
     swap = jnp.where(
         jnp.logical_and(order // 16 == other % 16, order % 16 == other // 16), 1.0, 0.0
     ).astype(jnp.bfloat16)
-    pl.semaphore_wait(barrier, ctrls - 1 + shelves - 1)
+    pl.semaphore_wait(barrier, ctrls - 1 + shelves - 1 + GROUP - 1)
 
     def along_shelf(piece, send, recv, target):
         return pltpu.make_async_remote_copy(
@@ -620,80 +589,92 @@
 
             each(ctrls, ctrl, act)
 
-    def z_forward_copy(half, to):
+    chunks = ((0, 2), (2, 1))
+
+    def z_forward_copy(half, part, to):
+        at, size = chunks[part]
         return remote(
-            home_z.at[half, pl.ds(to * per_z, per_z)], part_s(at_z, shelf),
-            2 * half, shelf, to, (ctrl, 2 * to + half),
+            home_z.at[half, pl.ds(to * per_z + at, size)], part_s(at_z.at[pl.ds(at, size)], shelf),
+            (2 * half) * 2 + part, shelf, to, (ctrl, 2 * to + half),
         )
 
     def z_forward(half):
-        each(chips, chip, lambda to: z_forward_copy(half, to).start())
-
-        @pl.when(core != half)
-        def _():
-            z_forward_copy(half, chip).start()
-
-        @pl.when(core == half)
-        def _():
-            part_s(at_z, shelf)[...] = home_z[half, pl.ds(chip * per_z, per_z)]
+        for part in range(2):
+            at, size = chunks[part]
+            each(chips, chip, lambda to: z_forward_copy(half, part, to).start())
+
+            @pl.when(core != half)
+            def _():
+                z_forward_copy(half, part, chip).start()
+
+            @pl.when(core == half)
+            def _():
+                part_s(at_z.at[pl.ds(at, size)], shelf)[...] = home_z[
+                    half, pl.ds(chip * per_z + at, size)
+                ]
 
     def z_forward_sent(half):
-        each(chips, chip, lambda to: z_forward_copy(half, to).wait_send())
-
-        @pl.when(core != half)
-        def _():
-            z_forward_copy(half, chip).wait_send()
+        for part in range(2):
+            each(chips, chip, lambda to: z_forward_copy(half, part, to).wait_send())
+
+            @pl.when(core != half)
+            def _():
+                z_forward_copy(half, part, chip).wait_send()
+
+    def z_back_copy(half, part, peer):
+        at, size = chunks[part]
+        return remote(
+            part_s(made_z.at[pl.ds(at, size)], peer),
+            back_z.at[half, pl.ds(chip * per_z + at, size)],
+            (2 * half + 1) * 2 + part, chip, peer, (ctrl, peer),
+        )
 
     def z_middle(half):
         @pl.when(core == half)
         def _():
-            def arrived(peer):
-                remote(
-                    home_z.at[half, pl.ds(0, per_z)], part_s(at_z, peer),
-                    2 * half, peer, 0, (ctrl, peer),
-                ).wait_recv()
-
-            each(shelves, shelf, arrived)
-            wide = jnp.concatenate([at_z[n] for n in range(per_z)], axis=1)
-            for m in range(0, shelves * rows_s, 256):
-                made = jnp.dot(shelf_ref[m : m + 256], wide, preferred_element_type=jnp.float32)
-                for n in range(per_z):
-                    made_z[n, m : m + 256, :] = made[:, n * lanes : (n + 1) * lanes].astype(
-                        jnp.bfloat16
-                    )
-
-            def act(peer):
-                remote(
-                    part_s(made_z, peer), back_z.at[half, pl.ds(chip * per_z, per_z)],
-                    2 * half + 1, chip, peer, (ctrl, peer),
-                ).start()
-
-            each(shelves, shelf, act)
-            back_z[half, pl.ds(chip * per_z, per_z)] = part_s(made_z, shelf)[...]
-
-    def z_back_from(half, source):
+            for part in range(2):
+                at, size = chunks[part]
+
+                def arrived(peer):
+                    remote(
+                        home_z.at[half, pl.ds(0, size)], part_s(at_z.at[pl.ds(at, size)], peer),
+                        (2 * half) * 2 + part, peer, 0, (ctrl, peer),
+                    ).wait_recv()
+
+                each(shelves, shelf, arrived)
+                both = jnp.concatenate([at_z[at + n] for n in range(size)], axis=1)
+                for m in range(0, shelves * rows_s, 256):
+                    made = jnp.dot(shelf_ref[m : m + 256], both, preferred_element_type=jnp.float32)
+                    for n in range(size):
+                        made_z[at + n, m : m + 256, :] = made[
+                            :, n * lanes : (n + 1) * lanes
+                        ].astype(jnp.bfloat16)
+                each(shelves, shelf, lambda peer: z_back_copy(half, part, peer).start())
+                back_z[half, pl.ds(chip * per_z + at, size)] = part_s(
+                    made_z.at[pl.ds(at, size)], shelf
+                )[...]
+
+    def z_back_from(half, part, source):
+        at, size = chunks[part]
         return remote(
-            part_s(made_z, shelf), back_z.at[half, pl.ds(source * per_z, per_z)],
-            2 * half + 1, source, 0, (ctrl, 2 * source + half),
+            part_s(made_z.at[pl.ds(at, size)], shelf),
+            back_z.at[half, pl.ds(source * per_z + at, size)],
+            (2 * half + 1) * 2 + part, source, 0, (ctrl, 2 * source + half),
         )
 
     def z_back_wait(half):
-        each(chips, chip, lambda source: z_back_from(half, source).wait_recv())
-
-        @pl.when(core != half)
-        def _():
-            z_back_from(half, chip).wait_recv()
+        for part in range(2):
+            each(chips, chip, lambda source: z_back_from(half, part, source).wait_recv())
+
+            @pl.when(core != half)
+            def _():
+                z_back_from(half, part, chip).wait_recv()
 
     def z_back_sent(half):
         @pl.when(core == half)
         def _():
-            def act(peer):
-                remote(
-                    part_s(made_z, peer), back_z.at[half, pl.ds(chip * per_z, per_z)],
-                    2 * half + 1, chip, peer, (ctrl, peer),
-                ).wait_send()
-
-            each(shelves, shelf, act)
+            for part in range(2):
+                each(shelves, shelf, lambda peer: z_back_copy(half, part, peer).wait_send())
 
     def one_step(repeat, carry):
         for p in range(0, rows_c, 16):
@@ -712,8 +693,8 @@
             prepare()
 
         fill(repeat * 4)
+        z_middle(1)
         y_middle(0)
-        z_middle(1)
         fill(repeat * 4 + 1)
         y_back_wait(0)
         exchange_rows(back_y.at[0], home_z.at[0])
@@ -777,6 +758,12 @@
     spread_pairs(by_weight, shelf_wide_rows)
     for z in range(8):
         weight_wide_ref[:, z * lanes : (z + 1) * lanes] = shelf_wide_rows[z, 0:rows_c]
+    reduce_part(
+        groups,
+        shelf_labels_ref, weight_wide_ref, shelf_cols_ref, first_ref, label_ref, mass_ref, kept_ref,
+        base_ref, sum_ref, total_ref, part_ref, block_mass_ref, wide, held,
+        rows, tiles, highs, deeps, blocks, mass_plane, mass_deep, mass_high, send_r, recv_r,
+    )
 
 
 def spread_pairs(tiles, wide):
@@ -794,10 +781,7 @@
 def power_steps(prob, ctrl_rows, shelf_rows, disk, label_tile):
     rows_c, rows_s, _ = prob.shape
     bf, f32 = jnp.bfloat16, jnp.float32
-    outs = [
-        (prob.shape, f32), ((rows_s, rows_c, NBLK), bf), ((rows_c, SHELF), f32), ((rows_s, SHELF), f32),
-        ((rows_c, SHELF), f32), ((16, 128), f32), ((16, 128), f32), ((8, 128), f32),
-    ]
+    outs = [(prob.shape, f32), ((NBLK, NBLK), f32), ((8, 128), f32)]
     dma = pltpu.SemaphoreType.DMA
     return pl.pallas_call(
         steps_kernel,
@@ -805,6 +789,19 @@
         in_specs=[pl.BlockSpec(memory_space=VMEM)] * 5,
         out_specs=tuple([pl.BlockSpec(memory_space=VMEM)] * len(outs)),
         scratch_shapes=[
+            pltpu.VMEM((rows_s, rows_c, NBLK), bf),
+            pltpu.VMEM((rows_c, SHELF), f32),
+            pltpu.VMEM((rows_s, SHELF), f32),
+            pltpu.VMEM((rows_c, SHELF), f32),
+            pltpu.VMEM((16, 128), f32),
+            pltpu.VMEM((16, 128), f32),
+            pltpu.VMEM((8, 128), f32),
+            pltpu.VMEM((NBLK, NBLK), f32),
+            pltpu.VMEM((8, 128), f32),
+            pltpu.VMEM((2, 2 * rows_s, SHELF), bf),
+            pltpu.VMEM((rows_s, rows_c, NBLK), f32),
+            pltpu.VMEM((GROUP, 32, NBLK), f32),
+            *[pltpu.VMEM((GROUP, 8, 128), f32)] * 7,
             pltpu.VMEM((16, 128), f32),
             pltpu.VMEM((4, 8, 16, 128), f32),
             pltpu.VMEM((8, 2, 2, 24, CTRL), bf),
@@ -833,7 +830,8 @@
             pltpu.VMEM((2, rows_c, rows_s, 128), bf),
             dma((2,)), dma((2,)), dma((2, 2, 4)), dma((2, 2, 4)), dma((2, 8)), dma((2, 8)),
             dma((2, 8)), dma((2, 8)), dma((2, 8)), dma((2, 8)), dma((2, 8)), dma((2, 8)),
-            dma((2, 2, 2, 16)), dma((2, 2, 2, 16)), dma((4, 32)), dma((4, 32)),
+            dma((2, 2, 2, 16)), dma((2, 2, 2, 16)), dma((8, 32)), dma((8, 32)),
+            dma((5, 2, GROUP)), dma((5, 2, GROUP)),
         ],
         compiler_params=pltpu.CompilerParams(
             collective_id=4, has_side_effects=True, vmem_limit_bytes=56 << 20
@@ -844,11 +842,7 @@
 
 def local(prob, ctrl_rates, shelf_rates, disk_rates, labels):
     label_tile = as_tile(labels.astype(jnp.float32))
-    outs = power_steps(prob, ctrl_rates, shelf_rates, disk_rates, label_tile)
-    iterate, first, shelf_labels, shelf_columns, shelf_weight, mass_tile, kept_tile, base = outs
-    numer, total = reduce_all(
-        shelf_labels, shelf_weight, shelf_columns, first, label_tile, mass_tile, kept_tile, base
-    )
+    iterate, numer, total = power_steps(prob, ctrl_rates, shelf_rates, disk_rates, label_tile)
     refined, coarse = balance_of(numer, total, label_tile, iterate)
     return (refined, coarse[0])
 

time: 234 us -> 227 us (0.970)
  local copies, waits for them, and re-layouts: 8.68 us -> 4.36 us
  Pallas kernels: 224 us -> 221 us
    pallas_call x1 -> x0, Pallas kernels: 42.6 us -> none  [reduce_all(): pl.pallas_call(reduce_kernel, out_shape=(jax.ShapeDtypeStruct((NBLK, NBLK...]
    pallas_call x1, Pallas kernels: 171 us -> 210 us  [power_steps(): pl.pallas_call(steps_kernel, out_shape=tuple((jax.ShapeDtypeStruct(*out)...]
    unnamed x18 -> x8, local copies, waits for them, and re-layouts: 7.36 us -> 3.03 us
where the time goes in v6:
time: 227 us
  Pallas kernels  221 us (97%)
  local copies, waits for them, and re-layouts  4.36 us (2%)
    pallas_call x1, Pallas kernels, power_steps(): pl.pallas_call(steps_kernel, out_shape=tuple((jax.ShapeDtypeStruct(*out)...  210 us
    pallas_call x1, Pallas kernels, balance_of(): pl.pallas_call(balance_kernel, out_shape=(jax.ShapeDtypeStruct(state.shap...  10.5 us

profile of v6, /device:TPU:1, one launch (start us, length us, event | category | flops | bytes accessed | tf_op | source)
XLA Modules:
  0.0 226.7 jit_solution(16720758108323509209)
XLA Ops:
  0.6 0.7 convert_element_type.5
  1.4 0.1 copy.8
  1.4 0.1 reshape.7
  1.5 0.6 pad.4.label_ref
  2.1 0.0 copy-start.2
  2.1 210.5 %power_steps.1 = (f32[48,32,256]{2,1,0:T(8,128)}, f32[256,256]{1,0:T(8,128)}, f32[8,128]{1,0:T(8,128)}) custom-call(f32[48,32,256]{2,1,0:T(8,128)} %prob_ref.1, f32[24,768]{1,0:T(8,128)} %ctrl_rows_ref.1, f32[32,1024]{1,0:T(8,128)} %shelf_rows_ref.1, f32[256,256]{1,0:T(8,128)} %disk_in_ref.1, f32[16,128]{1,0:T(8,128)} %pad.4.label_ref), custom_call_target="tpu_custom_call" | custom-call | tf_op jit(solution)/shard_map/power_steps/pallas_call | solution.py:786
  212.6 0.0 copy-done.2
  212.6 0.0 copy-start
  212.6 1.4 copy-done
  214.0 0.0 copy-start.1
  214.0 0.9 copy-done.1
  215.0 0.0 copy-start.3
  215.0 0.7 copy-done.3
  215.6 10.5 %balance.1 = (f32[48,32,256]{2,1,0:T(8,128)}, f32[8,256]{1,0:T(8,128)S(1)}) custom-call(f32[256,256]{1,0:T(8,128)S(1)} %copy-done.1, f32[8,128]{1,0:T(8,128)S(1)} %copy-done.3, f32[16,128]{1,0:T(8,128)S(1)} %copy-done.2, f32[48,32,256]{2,1,0:T(8,128)S(1)} %copy-done), custom_call_target="tpu_custom_call" | custom-call | tf_op jit(solution)/shard_map/balance/pallas_call | solution.py:235
  226.1 0.6 slice.3
Async XLA Ops:
  2.1 210.5 %copy-start.2 = (f32[16,128]{1,0:T(8,128)S(1)}, f32[16,128]{1,0:T(8,128)}, u32[]{:S(2)}) copy-start(f32[16,128]{1,0:T(8,128)} %pad.4.label_ref) | copy-start | bytes 24580
  212.6 1.4 copy-start
  214.0 0.9 copy-start.1
  215.0 0.7 copy-start.3

commit v7 on v6

--- a/solution.py
+++ b/solution.py
@@ -504,15 +504,20 @@
 
         lax.fori_loop(slot * part, slot * part + part, body, 0)
 
-    def swapped(block):
-        flat = jnp.dot(swap, block.reshape(256, lanes), preferred_element_type=jnp.float32)
-        return flat.astype(jnp.bfloat16).reshape(16, 16, lanes)
-
     def exchange_rows(source, target):
         first, second = source.shape[0], source.shape[1]
-        for p in range(0, first, 16):
-            for q in range(0, second, 16):
-                target[q : q + 16, p : p + 16, :] = swapped(source[p : p + 16, q : q + 16, :])
+        blocks = [(p, q) for p in range(0, first, 16) for q in range(0, second, 16)]
+        for n in range(0, len(blocks), 2):
+            pieces = [
+                source[p : p + 16, q : q + 16, :].reshape(256, lanes) for p, q in blocks[n : n + 2]
+            ]
+            flat = jnp.dot(
+                swap, jnp.concatenate(pieces, axis=1), preferred_element_type=jnp.float32
+            ).astype(jnp.bfloat16)
+            for m, (p, q) in enumerate(blocks[n : n + 2]):
+                target[q : q + 16, p : p + 16, :] = flat[:, m * lanes : (m + 1) * lanes].reshape(
+                    16, 16, lanes
+                )
 
     def part_s(ref, owner):
         return ref.at[:, pl.ds(pl.multiple_of(owner * rows_s, 16), rows_s), :]
@@ -682,9 +687,9 @@
             made = jnp.dot(rounded, disk_ref[...], preferred_element_type=jnp.float32)
             made = made.astype(jnp.bfloat16).reshape(16, rows_s, 256)
             home_z[1, p : p + 16] = made[:, :, lanes:]
-            for q in range(0, rows_s, 16):
-                home_y[0, q : q + 16, p : p + 16, :] = swapped(made[:, q : q + 16, :lanes])
+            home_z[0, p : p + 16] = made[:, :, :lanes]
         z_forward(1)
+        exchange_rows(home_z.at[0], home_y.at[0])
         y_forward(0)
 
         @pl.when(repeat == 0)
@@ -702,14 +707,14 @@
         z_back_wait(1)
         exchange_rows(back_z.at[1], home_y.at[1])
         y_forward(1)
-        fill(repeat * 4 + 2)
         z_middle(0)
         y_middle(1)
+        fill(repeat * 4 + 2)
         fill(repeat * 4 + 3)
-        z_back_wait(0)
         y_back_wait(1)
         z_forward_sent(1)
         exchange_rows(back_y.at[1], home_z.at[1])
+        z_back_wait(0)
 
         def update(row, inner):
             kept = 1.0 - rate_ref[pl.ds(row, 1), :] * shelf_rate_ref[...]
@@ -717,7 +722,7 @@
             state_ref[row] = third.astype(jnp.float32) * scale_ref[0:1] + state_ref[row] * kept
             return inner
 
-        lax.fori_loop(0, rows_c, update, 0)
+        lax.fori_loop(0, rows_c, update, 0, unroll=4)
         z_forward_sent(0)
         z_back_sent(0)
         z_back_sent(1)

time: 227 us -> 225 us (level)
  no operation moved by 1% of the time
where the time goes in v7:
time: 225 us; the launch traced here: 224 us
  Pallas kernels  219 us (97%)
  local copies, waits for them, and re-layouts  4.36 us (2%)
    pallas_call x1, Pallas kernels, power_steps(): pl.pallas_call(steps_kernel, out_shape=tuple((jax.ShapeDtypeStruct(*out)...  208 us
    pallas_call x1, Pallas kernels, balance_of(): pl.pallas_call(balance_kernel, out_shape=(jax.ShapeDtypeStruct(state.shap...  10.5 us

profile of v7, /device:TPU:1, one launch (start us, length us, event | category | flops | bytes accessed | tf_op | source)
XLA Modules:
  0.0 224.5 jit_solution(2501166956108570706)
XLA Ops:
  0.6 0.7 convert_element_type.5
  1.4 0.1 copy.8
  1.4 0.1 reshape.7
  1.5 0.6 pad.4.label_ref
  2.1 0.0 copy-start.2
  2.1 208.3 %power_steps.1 = (f32[48,32,256]{2,1,0:T(8,128)}, f32[256,256]{1,0:T(8,128)}, f32[8,128]{1,0:T(8,128)}) custom-call(f32[48,32,256]{2,1,0:T(8,128)} %prob_ref.1, f32[24,768]{1,0:T(8,128)} %ctrl_rows_ref.1, f32[32,1024]{1,0:T(8,128)} %shelf_rows_ref.1, f32[256,256]{1,0:T(8,128)} %disk_in_ref.1, f32[16,128]{1,0:T(8,128)} %pad.4.label_ref), custom_call_target="tpu_custom_call" | custom-call | tf_op jit(solution)/shard_map/power_steps/pallas_call | solution.py:791
  210.4 0.0 copy-done.2
  210.4 0.0 copy-start
  210.4 1.4 copy-done
  211.8 0.0 copy-start.1
  211.8 0.9 copy-done.1
  212.8 0.0 copy-start.3
  212.8 0.7 copy-done.3
  213.4 10.5 %balance.1 = (f32[48,32,256]{2,1,0:T(8,128)}, f32[8,256]{1,0:T(8,128)S(1)}) custom-call(f32[256,256]{1,0:T(8,128)S(1)} %copy-done.1, f32[8,128]{1,0:T(8,128)S(1)} %copy-done.3, f32[16,128]{1,0:T(8,128)S(1)} %copy-done.2, f32[48,32,256]{2,1,0:T(8,128)S(1)} %copy-done), custom_call_target="tpu_custom_call" | custom-call | tf_op jit(solution)/shard_map/balance/pallas_call | solution.py:235
  223.9 0.6 slice.3
Async XLA Ops:
  2.1 208.3 %copy-start.2 = (f32[16,128]{1,0:T(8,128)S(1)}, f32[16,128]{1,0:T(8,128)}, u32[]{:S(2)}) copy-start(f32[16,128]{1,0:T(8,128)} %pad.4.label_ref) | copy-start | bytes 24580
  210.4 1.4 copy-start
  211.8 0.9 copy-start.1
  212.8 0.7 copy-start.3

commit v8 on v7

--- a/solution.py
+++ b/solution.py
@@ -15,6 +15,7 @@
 GROUP = 8
 MESH = pl.DeviceIdType.MESH
 VMEM = pltpu.MemorySpace.VMEM
+HBM = pltpu.MemorySpace.HBM
 HIGHEST = lax.Precision.HIGHEST
 
 
@@ -79,14 +80,14 @@
         member = jnp.where(names == blocks, 1.0, 0.0).astype(jnp.bfloat16)
         scaled = factor_ref[...] * weight_ref[pl.ds(row, 1), :]
         upper = scaled.astype(jnp.bfloat16)
-        slot = row % 2
+        slot = row % 4
         wide[slot, 0:depth, :] = upper
         wide[slot, depth : 2 * depth, :] = (scaled - upper.astype(jnp.float32)).astype(jnp.bfloat16)
         both = lax.dot_general(wide[slot], member, NT, preferred_element_type=jnp.float32)
         held[:, pl.ds(row, 1), :] = (both[0:depth] + both[depth:]).reshape(depth, 1, NBLK)
         return carry
 
-    lax.fori_loop(0, labels_ref.shape[0], body, 0, unroll=2)
+    lax.fori_loop(0, labels_ref.shape[0], body, 0, unroll=4)
     rows = held.shape[0] * held.shape[1]
     mine = held[...].reshape(rows, NBLK)
     first = first_ref[...].reshape(rows, NBLK)
@@ -115,7 +116,7 @@
 
 def reduce_part(
     groups,
-    labels_ref, weight_ref, factor_ref, first_ref, label_ref, pair_mass_ref, pair_kept_ref, base_ref,
+    labels_ref, weight_ref, factor_ref, first_ref, terms, base_ref,
     sum_ref, total_ref,
     part_ref, mass_ref, wide, held,
     rows, tiles, highs, deeps, blocks, mass_plane, mass_deep, mass_high,
@@ -125,7 +126,6 @@
     plane_me, deep_me, high_me = plane[0], deep[0], high[0]
 
     flow_part(labels_ref, weight_ref, factor_ref, first_ref, part_ref, wide, held)
-    terms = block_terms(label_ref, pair_mass_ref, pair_kept_ref)
     mass_ref[...] = jnp.zeros_like(mass_ref)
     mass_ref[0:1] = terms[0:1, 0:128]
     mass_ref[1:2] = terms[0:1, 128:256]
@@ -188,9 +188,20 @@
     exchange(plane, ((lambda m: own, own),), send_sem.at[4], recv_sem.at[4])
 
 
-def balance_kernel(numer_ref, total_ref, label_ref, state_ref, refined_ref, coarse_ref, power, spread, held, sem):
-    load = pltpu.make_async_copy(state_ref, held, sem)
-    load.start()
+def balance_kernel(
+    numer_hbm, total_hbm, label_ref, state_ref, refined_hbm, coarse_ref,
+    numer_ref, total_ref, power, spread, held, ready, sem, done,
+):
+    loads = [
+        pltpu.make_async_copy(source, target, sem.at[n])
+        for n, (source, target) in enumerate(
+            ((total_hbm, total_ref), (numer_hbm, numer_ref), (state_ref, held))
+        )
+    ]
+    for load in loads:
+        load.start()
+    loads[0].wait()
+    loads[1].wait()
     size = NBLK
     line = lax.broadcasted_iota(jnp.int32, (size, size), 0)
     column = lax.broadcasted_iota(jnp.int32, (size, size), 1)
@@ -224,11 +235,20 @@
         spread[pl.ds(q, 16, stride=4), :] = tile if q == 0 else pltpu.roll(tile, 128 - 32 * q, 1)
     names = jnp.transpose(spread[...])[0:32]
     lane = lax.broadcasted_iota(jnp.int32, (32, size), 1).astype(jnp.float32)
-    load.wait()
+    loads[2].wait()
+    stores = []
     for a in range(held.shape[0]):
         picked = jnp.where(names[:, a : a + 1] == lane, share, 0.0)
         factor = jnp.sum(picked, axis=1, keepdims=True)
-        refined_ref[a] = held[a] * factor * float(CTRL * SHELF * DISK)
+        ready[a] = held[a] * factor * float(CTRL * SHELF * DISK)
+        if a % 12 == 11:
+            rows = pl.ds(a - 11, 12)
+            stores.append(
+                pltpu.make_async_copy(ready.at[rows], refined_hbm.at[rows], done.at[a // 12])
+            )
+            stores[-1].start()
+    for store in stores:
+        store.wait()
 
 
 def balance_of(numer, total, label_tile, state):
@@ -238,13 +258,22 @@
             jax.ShapeDtypeStruct(state.shape, jnp.float32),
             jax.ShapeDtypeStruct((8, NBLK), jnp.float32),
         ),
-        in_specs=[pl.BlockSpec(memory_space=VMEM)] * 3 + [pl.BlockSpec(memory_space=pl.ANY)],
-        out_specs=(pl.BlockSpec(memory_space=VMEM), pl.BlockSpec(memory_space=VMEM)),
+        in_specs=[
+            pl.BlockSpec(memory_space=HBM),
+            pl.BlockSpec(memory_space=HBM),
+            pl.BlockSpec(memory_space=VMEM),
+            pl.BlockSpec(memory_space=HBM),
+        ],
+        out_specs=(pl.BlockSpec(memory_space=HBM), pl.BlockSpec(memory_space=VMEM)),
         scratch_shapes=[
+            pltpu.VMEM((NBLK, NBLK), jnp.float32),
+            pltpu.VMEM((8, 128), jnp.float32),
             pltpu.VMEM((NBLK, NBLK), jnp.float32),
             pltpu.VMEM((128, 128), jnp.float32),
             pltpu.VMEM(state.shape, jnp.float32),
-            pltpu.SemaphoreType.DMA,
+            pltpu.VMEM(state.shape, jnp.float32),
+            pltpu.SemaphoreType.DMA((3,)),
+            pltpu.SemaphoreType.DMA((4,)),
         ],
         compiler_params=pltpu.CompilerParams(vmem_limit_bytes=32 << 20),
         name="balance",
@@ -538,7 +567,8 @@
 
     def each(count, first, act):
         def body(step, carry):
-            act((first + step) % count)
+            away = count // 2 + (step // 2) * (1 - 2 * (step % 2))
+            act((first + away) % count)
             return carry
 
         lax.fori_loop(1, count, body, 0)
@@ -759,13 +789,14 @@
         )[0:1]
     lax.fori_loop(1, stages[0][2], stages[0][1], 0)
     lax.fori_loop(1, stages[1][2], stages[1][0], 0)
+    terms = block_terms(label_ref, mass_ref, kept_ref)
     lax.fori_loop(1, stages[1][2], stages[1][1], 0)
     spread_pairs(by_weight, shelf_wide_rows)
     for z in range(8):
         weight_wide_ref[:, z * lanes : (z + 1) * lanes] = shelf_wide_rows[z, 0:rows_c]
     reduce_part(
         groups,
-        shelf_labels_ref, weight_wide_ref, shelf_cols_ref, first_ref, label_ref, mass_ref, kept_ref,
+        shelf_labels_ref, weight_wide_ref, shelf_cols_ref, first_ref, terms,
         base_ref, sum_ref, total_ref, part_ref, block_mass_ref, wide, held,
         rows, tiles, highs, deeps, blocks, mass_plane, mass_deep, mass_high, send_r, recv_r,
     )
@@ -803,7 +834,7 @@
             pltpu.VMEM((8, 128), f32),
             pltpu.VMEM((NBLK, NBLK), f32),
             pltpu.VMEM((8, 128), f32),
-            pltpu.VMEM((2, 2 * rows_s, SHELF), bf),
+            pltpu.VMEM((4, 2 * rows_s, SHELF), bf),
             pltpu.VMEM((rows_s, rows_c, NBLK), f32),
             pltpu.VMEM((GROUP, 32, NBLK), f32),
             *[pltpu.VMEM((GROUP, 8, 128), f32)] * 7,

time: 225 us -> 215 us (0.956)
  Pallas kernels: 219 us -> 209 us
    pallas_call x1, Pallas kernels: 208 us -> 199 us  [power_steps(): pl.pallas_call(steps_kernel, out_shape=tuple((jax.ShapeDtypeStruct(*out)...]
where the time goes in v8:
time: 215 us
  Pallas kernels  209 us (97%)
  local copies, waits for them, and re-layouts  4.36 us (2%)
    pallas_call x1, Pallas kernels, power_steps(): pl.pallas_call(steps_kernel, out_shape=tuple((jax.ShapeDtypeStruct(*out)...  199 us
    pallas_call x1, Pallas kernels, balance_of(): pl.pallas_call(balance_kernel, out_shape=(jax.ShapeDtypeStruct(state.shap...  10.1 us

profile of v8, /device:TPU:1, one launch (start us, length us, event | category | flops | bytes accessed | tf_op | source)
XLA Modules:
  0.0 214.5 jit_solution(10879841776067375111)
XLA Ops:
  0.6 0.7 convert_element_type.5
  1.4 0.1 copy.8
  1.4 0.1 reshape.7
  1.5 0.6 pad.4.label_ref
  2.1 0.0 copy-start.2
  2.1 198.6 %power_steps.1 = (f32[48,32,256]{2,1,0:T(8,128)}, f32[256,256]{1,0:T(8,128)}, f32[8,128]{1,0:T(8,128)}) custom-call(f32[48,32,256]{2,1,0:T(8,128)} %prob_ref.1, f32[24,768]{1,0:T(8,128)} %ctrl_rows_ref.1, f32[32,1024]{1,0:T(8,128)} %shelf_rows_ref.1, f32[256,256]{1,0:T(8,128)} %disk_in_ref.1, f32[16,128]{1,0:T(8,128)} %pad.4.label_ref), custom_call_target="tpu_custom_call" | custom-call | tf_op jit(solution)/shard_map/power_steps/pallas_call | solution.py:822
  200.8 0.0 copy-done.2
  200.8 0.0 copy-start
  200.8 1.4 copy-done
  202.2 0.0 copy-start.1
  202.2 0.9 copy-done.1
  203.1 0.0 copy-start.3
  203.1 0.7 copy-done.3
  203.8 10.1 %balance.1 = (f32[48,32,256]{2,1,0:T(8,128)}, f32[8,256]{1,0:T(8,128)S(1)}) custom-call(f32[256,256]{1,0:T(8,128)S(1)} %copy-done.1, f32[8,128]{1,0:T(8,128)S(1)} %copy-done.3, f32[16,128]{1,0:T(8,128)S(1)} %copy-done.2, f32[48,32,256]{2,1,0:T(8,128)S(1)} %copy-done), custom_call_target="tpu_custom_call" | custom-call | tf_op jit(solution)/shard_map/balance/pallas_call | solution.py:255
  214.0 0.6 slice.3
Async XLA Ops:
  2.1 198.6 %copy-start.2 = (f32[16,128]{1,0:T(8,128)S(1)}, f32[16,128]{1,0:T(8,128)}, u32[]{:S(2)}) copy-start(f32[16,128]{1,0:T(8,128)} %pad.4.label_ref) | copy-start | bytes 24580
  200.8 1.4 copy-start
  202.2 0.9 copy-start.1
  203.1 0.7 copy-start.3

commit v9 on v8

--- a/solution.py
+++ b/solution.py
@@ -38,6 +38,10 @@
     return (plane_me, plane), (deep_me, deep), (high_me, high)
 
 
+def far_first(step, count):
+    return count // 2 + (step // 2) * (1 - 2 * (step % 2))
+
+
 def exchange(group, streams, send_sem, recv_sem):
     me, peer = group
 
@@ -55,7 +59,7 @@
 
     def start(step, carry):
         for index in range(len(streams)):
-            copy(step, index).start()
+            copy(far_first(step, GROUP), index).start()
         return carry
 
     def finish(step, carry):
@@ -295,7 +299,7 @@
             )
 
         def start(step, carry):
-            copy(step).start()
+            copy(far_first(step, size)).start()
             return carry
 
         def finish(step, carry):
@@ -567,8 +571,7 @@
 
     def each(count, first, act):
         def body(step, carry):
-            away = count // 2 + (step // 2) * (1 - 2 * (step % 2))
-            act((first + away) % count)
+            act((first + far_first(step, count)) % count)
             return carry
 
         lax.fori_loop(1, count, body, 0)

time: 215 us -> 215 us (level)
  no operation moved by 1% of the time
where the time goes in v9:
time: 215 us
  Pallas kernels  209 us (97%)
  local copies, waits for them, and re-layouts  4.36 us (2%)
    pallas_call x1, Pallas kernels, power_steps(): pl.pallas_call(steps_kernel, out_shape=tuple((jax.ShapeDtypeStruct(*out)...  199 us
    pallas_call x1, Pallas kernels, balance_of(): pl.pallas_call(balance_kernel, out_shape=(jax.ShapeDtypeStruct(state.shap...  10.1 us

profile of v9, /device:TPU:1, one launch (start us, length us, event | category | flops | bytes accessed | tf_op | source)
XLA Modules:
  0.0 214.9 jit_solution(15825215411541161012)
XLA Ops:
  0.6 0.7 convert_element_type.5
  1.4 0.1 copy.8
  1.4 0.1 reshape.7
  1.5 0.6 pad.4.label_ref
  2.1 0.0 copy-start.2
  2.1 199.0 %power_steps.1 = (f32[48,32,256]{2,1,0:T(8,128)}, f32[256,256]{1,0:T(8,128)}, f32[8,128]{1,0:T(8,128)}) custom-call(f32[48,32,256]{2,1,0:T(8,128)} %prob_ref.1, f32[24,768]{1,0:T(8,128)} %ctrl_rows_ref.1, f32[32,1024]{1,0:T(8,128)} %shelf_rows_ref.1, f32[256,256]{1,0:T(8,128)} %disk_in_ref.1, f32[16,128]{1,0:T(8,128)} %pad.4.label_ref), custom_call_target="tpu_custom_call" | custom-call | tf_op jit(solution)/shard_map/power_steps/pallas_call | solution.py:825
  201.1 0.0 copy-done.2
  201.1 0.0 copy-start
  201.1 1.4 copy-done
  202.5 0.0 copy-start.1
  202.5 0.9 copy-done.1
  203.5 0.0 copy-start.3
  203.5 0.7 copy-done.3
  204.2 10.1 %balance.1 = (f32[48,32,256]{2,1,0:T(8,128)}, f32[8,256]{1,0:T(8,128)S(1)}) custom-call(f32[256,256]{1,0:T(8,128)S(1)} %copy-done.1, f32[8,128]{1,0:T(8,128)S(1)} %copy-done.3, f32[16,128]{1,0:T(8,128)S(1)} %copy-done.2, f32[48,32,256]{2,1,0:T(8,128)S(1)} %copy-done), custom_call_target="tpu_custom_call" | custom-call | tf_op jit(solution)/shard_map/balance/pallas_call | solution.py:259
  214.3 0.6 slice.3
Async XLA Ops:
  2.1 199.0 %copy-start.2 = (f32[16,128]{1,0:T(8,128)S(1)}, f32[16,128]{1,0:T(8,128)}, u32[]{:S(2)}) copy-start(f32[16,128]{1,0:T(8,128)} %pad.4.label_ref) | copy-start | bytes 24580
  201.1 1.4 copy-start
  202.5 0.9 copy-start.1
  203.5 0.7 copy-start.3
